TPU v7x, 256 devices: a whole 4x4x8 slice. The times are simulated.
256 devices in a mesh: blk: 32 (over x_lo, z, core), own: 8 (over y, x_hi).
Axes of the slice: x: 4 (x_hi: 2, x_lo: 2; x = x_hi * 2 + x_lo), y: 4, z: 8, core: 2. Of those that a mesh axis runs over, the one named last changes fastest.
Arguments:
- embeddings: bfloat16 [32768, 768], P(('blk', 'own')), may hold values from -320 to 320
- centroids: bfloat16 [16384, 768], P('blk'), may hold values from -4 to 4
- log_weight: float32 [16384], P('blk'), may hold values from -0.5 to 1.6
Outputs:
- new_centroids: float32 [16384, 768], P(('blk', 'own'))
- counts: float32 [16384], P(('blk', 'own'))
- log_norm: float32 [32768], P(('blk', 'own'))
All inputs are finite; a program needn't handle non-finite values.
Results may differ from a plain program's by a relative error of at most 0.0015.
Values may be sent and summed in bfloat16 or wider, within the bound.
No kernel may reach another device: no remote copies, remote signals or barrier semaphores. Data moves between devices by JAX's collectives and lax.ppermute only.
A program may use at most 64 MiB of HBM per device.

v0:
```python
import math

import jax
import jax.numpy as jnp
from jax import lax
from jax.sharding import PartitionSpec as P

prior_mass = 1.0


def copy_for_each(array, axis):
    copies = jnp.broadcast_to(array, (lax.axis_size(axis), *array.shape))
    return lax.all_to_all(copies, axis, split_axis=0, concat_axis=0, tiled=True)


def collected_together(array, axis):
    leaves = jax.tree.leaves(array)
    turns = sorted(range(len(leaves)), key=lambda k: -leaves[k].size)
    width = (1, *leaves[turns[0]].shape)[-1]
    lines = [
        jnp.pad(leaves[k].reshape(-1), (0, -leaves[k].size % width)).reshape(-1, width)
        for k in turns
    ]
    both, at, found = (copy_for_each(jnp.concatenate(lines), axis), 0, {})
    for k, line in zip(turns, lines):
        share = both[:, at : at + len(line)].reshape(len(both), -1)
        found[k] = share[:, : leaves[k].size].reshape(-1, *leaves[k].shape)
        at += len(line)
    numbers = iter(range(len(leaves)))
    return jax.tree.map(lambda _: found[next(numbers)], array)


def combined_pairwise(pieces, combine):
    while len(jax.tree.leaves(pieces)[0]) > 1:
        pieces = jax.vmap(combine)(
            *(jax.tree.map(lambda part: part[side::2], pieces) for side in (0, 1))
        )
    return jax.tree.map(lambda part: part[0], pieces)


def merged(array, axis, combine):
    pieces = collected_together(array, axis)
    return combined_pairwise(pieces, combine)


def cut_along(array, dim, count):
    lengths = array.shape
    tiles = array.reshape(*lengths[:dim], count, lengths[dim] // count, *lengths[dim + 1 :])
    return jnp.moveaxis(tiles, dim, 0)


def sent_and_summed(array, axis, dim):
    count = lax.axis_size(axis)
    tiles = lax.all_to_all(cut_along(array, dim, count), axis, 0, 0, tiled=True)
    return jnp.sum(tiles, axis=0)


def score_rows(row_block, centroids, half_sq, log_weight, scale_root):
    dots = lax.dot_general(
        row_block, centroids, (((1,), (1,)), ((), ())), preferred_element_type=jnp.float32
    )
    return (dots - half_sq[None, :]) / scale_root + log_weight[None, :]


def local(embeddings, centroids, log_weight):
    row_count, feat_dim = embeddings.shape
    local_count = centroids.shape[0]
    centre_vals = centroids.astype(jnp.float32)
    half_sq = 0.5 * jnp.sum(centre_vals * centre_vals, axis=1)
    scale_root = math.sqrt(feat_dim)
    logits = score_rows(
        lax.all_gather(embeddings, "blk", axis=0, tiled=True),
        centroids,
        half_sq,
        log_weight,
        scale_root,
    )
    peak_val = jnp.max(logits, axis=1)
    peak_part = peak_val
    mass_part = jnp.sum(jnp.exp(logits - peak_val[:, None]), axis=1)
    peak_val = peak_part
    mass_sum = mass_part

    def combine(first_pair, later_pair):
        joined = jnp.maximum(first_pair[0], later_pair[0])
        return (
            joined,
            first_pair[1] * jnp.exp(first_pair[0] - joined)
            + later_pair[1] * jnp.exp(later_pair[0] - joined),
        )

    peak_val, mass_sum = merged((peak_val, mass_sum), "blk", combine)
    log_total = peak_val + jnp.log(mass_sum)
    empty_sums = jnp.zeros((local_count, feat_dim), jnp.float32)
    empty_counts = jnp.zeros((local_count,), jnp.float32)
    row_block = lax.all_gather(embeddings, "blk", axis=0, tiled=True)
    logits = score_rows(row_block, centroids, half_sq, log_weight, scale_root)
    resp_vals = jnp.exp(logits - log_total[:, None])
    contrib = lax.dot_general(
        resp_vals.astype(jnp.bfloat16),
        row_block,
        (((0,), (0,)), ((), ())),
        preferred_element_type=jnp.float32,
    )
    contrib, count_part = (contrib, jnp.sum(resp_vals, axis=0))
    weighted = contrib
    counts = (empty_sums, empty_counts)[1] + count_part
    weighted, counts = (sent_and_summed(weighted, "own", 0), sent_and_summed(counts, "own", 0))
    owned_count = local_count // lax.axis_size("own")
    own_index = lax.axis_index("own")
    own_centres = lax.dynamic_slice_in_dim(centre_vals, own_index * owned_count, owned_count, 0)
    updated = (weighted + prior_mass * own_centres) / (counts[:, None] + prior_mass)
    log_norm = lax.dynamic_slice_in_dim(log_total, lax.axis_index("blk") * row_count, row_count, 0)
    return (updated, counts, log_norm)


def solution(mesh):
    placed = (P(("blk", "own"), None), P("blk", None), P("blk"))
    return jax.shard_map(
        local,
        mesh=mesh,
        in_specs=placed,
        out_specs=(P(("blk", "own"), None), P(("blk", "own")), P(("blk", "own"))),
        check_vma=False,
    )
```

profile of v0, /device:TPU:8, one launch (start us, length us, event | category | flops | bytes accessed | tf_op | source)
XLA Modules:
  0.0 188.3 jit_solution(2781830788650535467)
XLA Ops:
  7.2 0.7 all-gather.2.cloned.1.call-update
  7.9 1.4 multiply_reduce_fusion
  9.3 73.7 %all-gather.2.cloned.1.call-done = bf16[4096,768]{1,0:T(8,128)(2,1)} async-done(((bf16[128,768]{1,0:T(8,128)(2,1)}), bf16[4096,768]{1,0:T(8,128)(2,1)}) %all-gather.2.cloned.1.call-update) | async-done | bytes 6291472 | tf_op jit(solution)/shard_map/all_gather | solution.py:96
  83.0 5.9 %fusion.8 = (f32[4096]{0:T(1024)S(1)}, f32[4096,512]{0,1:T(8,128)S(1)}) fusion(f32[512]{0:T(512)} %param.5, f32[512]{0:T(512)S(1)} %broadcast_multiply_fusion, bf16[4096,768]{1,0:T(8,128)(2,1)} %all-gather.2.cloned.1.call-done, bf16[512,768]{1,0:T(8,128)(2,1)} %param.4), kind=kOutput, calls=%fused_computation.26 | convolution fusion | flops 3229609984 | bytes 15486976 | tf_op jit(solution)/shard_map/dot_general | solution.py:59
  88.9 3.2 %copy-done = f32[4096,512]{0,1:T(8,128)} copy-done((f32[4096,512]{0,1:T(8,128)}, f32[4096,512]{0,1:T(8,128)S(1)}, u32[]{:S(2)}) %copy-start) | copy-done | bytes 8388632
  92.1 1.3 exponential_reduce_fusion
  93.5 0.5 broadcast_in_dim.2
  93.9 34.5 %all_to_all.19 = f32[32,2,4096]{2,1,0:T(2,128)S(1)} all-to-all(f32[32,2,4096]{2,1,0:T(2,128)S(1)} %broadcast_in_dim.2), channel_id=1, replica_groups=mesh['blk'=32,'own'=8] {'blk'}, dimensions={0} | all-to-all | bytes 2097152 | tf_op jit(solution)/shard_map/all_to_all | solution.py:13
  128.4 0.8 fusion.7
  129.2 0.6 copy_bitcast_fusion
  129.9 0.1 slice.71
  130.0 0.1 slice.72
  130.2 0.1 slice.82
  130.3 0.1 slice.83
  131.6 0.1 slice.77
  132.2 4.6 %fusion = f32[512]{0:T(512)S(1)} fusion(f32[4096,512]{0,1:T(8,128)} %copy-done, f32[4096]{0:T(1024)S(1)} %bitcast.15), kind=kLoop, calls=%fused_computation.3 | loop fusion | flops 4193792 | bytes 8407040 | tf_op jit(solution)/shard_map/reduce_sum | solution.py:105
  136.8 0.7 all_to_all.14
  137.5 7.0 %all-to-all-start.2 = ((f32[8,1,64]{2,1,0:T(1,128)}), f32[8,1,64]{2,1,0:T(1,128)S(1)}, u32[]{:S(2)}, u32[]{:S(2)}) async-start(f32[8,1,64]{2,1,0:T(1,128)} %all_to_all.14), calls=%async_computation.2 | async-start | bytes 8192 | tf_op jit(solution)/shard_map/all_to_all | solution.py:54
  144.4 9.9 %fusion.2 = f32[512,768]{1,0:T(8,128)} fusion(bf16[4096,768]{1,0:T(8,128)(2,1)} %all-gather.2.cloned.1.call-done, f32[4096,512]{0,1:T(8,128)} %copy-done, f32[4096]{0:T(1024)S(1)} %bitcast.16), kind=kOutput, calls=%fused_computation.5 | convolution fusion | flops 3225419776 | bytes 16269312 | tf_op jit(solution)/shard_map/dot_general | solution.py:99
  154.3 7.2 %all-to-all-start.1 = ((f32[8,64,768]{2,1,0:T(8,128)}), f32[8,64,768]{2,1,0:T(8,128)S(1)}, u32[]{:S(2)}, u32[]{:S(2)}) async-start(f32[8,64,768]{2,1,0:T(8,128)} %bitcast.14), calls=%async_computation.1 | async-start | bytes 3145728 | tf_op jit(solution)/shard_map/all_to_all | solution.py:54
  161.5 1.3 convert_element_type.6
  162.8 0.5 dynamic-slice_bitcast_fusion
  163.3 16.3 %all-to-all-done.1 = f32[8,64,768]{2,1,0:T(8,128)S(1)} async-done(((f32[8,64,768]{2,1,0:T(8,128)}), f32[8,64,768]{2,1,0:T(8,128)S(1)}, u32[]{:S(2)}, u32[]{:S(2)}) %all-to-all-start.1) | async-done | bytes 1572896 | tf_op jit(solution)/shard_map/all_to_all | solution.py:54
  179.7 1.7 add_divide_fusion
  (28 shorter events, 1.7 us)
Async XLA Ops:
  7.2 75.8 %all-gather.2.cloned.1.call-start = ((), (), s32[]{:S(2)}) async-start(), calls=%async_computation.3 | async-start | bytes 6488064 | tf_op jit(solution)/shard_map/all_gather | solution.py:96
  88.9 3.2 %copy-start = (f32[4096,512]{0,1:T(8,128)}, f32[4096,512]{0,1:T(8,128)S(1)}, u32[]{:S(2)}) copy-start(f32[4096,512]{0,1:T(8,128)S(1)} %get-tuple-element.14) | copy-start | bytes 25165828
  137.5 16.9 %all-to-all-start.2 = ((f32[8,1,64]{2,1,0:T(1,128)}), f32[8,1,64]{2,1,0:T(1,128)S(1)}, u32[]{:S(2)}, u32[]{:S(2)}) async-start(f32[8,1,64]{2,1,0:T(1,128)} %all_to_all.14), calls=%async_computation.2 | async-start | bytes 8192 | tf_op jit(solution)/shard_map/all_to_all | solution.py:54
  144.4 17.1 %copy-start.1 = (bf16[512,768]{1,0:T(8,128)(2,1)S(1)}, bf16[512,768]{1,0:T(8,128)(2,1)}, u32[]{:S(2)}) copy-start(bf16[512,768]{1,0:T(8,128)(2,1)} %param.4) | copy-start | bytes 2359300
  154.3 25.3 %all-to-all-start.1 = ((f32[8,64,768]{2,1,0:T(8,128)}), f32[8,64,768]{2,1,0:T(8,128)S(1)}, u32[]{:S(2)}, u32[]{:S(2)}) async-start(f32[8,64,768]{2,1,0:T(8,128)} %bitcast.14), calls=%async_computation.1 | async-start | bytes 3145728 | tf_op jit(solution)/shard_map/all_to_all | solution.py:54
  163.3 18.1 %copy-start.2 = (f32[64]{0:T(128)}, f32[64]{0:T(128)S(1)}, u32[]{:S(2)}) copy-start(f32[64]{0:T(128)S(1)} %reduce_sum.49) | copy-start | bytes 772
Sparse Core Ops, SparseCore 0:
  9.9 73.0 all-gather.1
where the time goes:
time: 192 us; the launch traced here: 188 us
  waiting for transfers between devices  90.7 us (47%)
  blocking collectives  34.5 us (18%)
  matrix products  15.8 us (8%)
  between operations  14.3 us (7%)
  starting transfers between devices  14.2 us (7%)
  other arithmetic  10.7 us (6%)
  local copies, waits for them, and re-layouts  8.15 us (4%)
    all_gather x1, waiting for transfers between devices, local(): row_block = lax.all_gather(embeddings, 'blk', axis=0, tiled=True)  73.7 us
    all_to_all x1, blocking collectives, copy_for_each(): return lax.all_to_all(copies, axis, split_axis=0, concat_axis=0, tiled=True)  34.5 us
    all_to_all x2, waiting for transfers between devices, sent_and_summed(): tiles = lax.all_to_all(cut_along(array, dim, count), axis, 0, 0, tiled=True)  16.3 us
    all_to_all x2, starting transfers between devices, sent_and_summed(): tiles = lax.all_to_all(cut_along(array, dim, count), axis, 0, 0, tiled=True)  14.2 us
    dot_general x1, matrix products, local(): lax.dot_general(resp_vals.astype(jnp.bfloat16), row_block, (((0,), (0,)),...  9.89 us
    dot_general x1, matrix products, score_rows(): lax.dot_general(row_block, centroids, (((1,), (1,)), ((), ())), preferred...  5.88 us
    reduce_sum x1, other arithmetic, local(): contrib, count_part = (contrib, jnp.sum(resp_vals, axis=0))  4.57 us
  transfers between devices with their start and end apart: 3, of which 2 were waited for; matrix products, arithmetic and copies ran while one was open for 7% of the time, Pallas kernels for 0%

commit v1 on v0

v1 whole, which is shorter than its diff:
```python
import functools
import math

import jax
import jax.numpy as jnp
from jax import lax
from jax.experimental import pallas as pl
from jax.experimental.pallas import tpu as pltpu
from jax.sharding import Mesh
from jax.sharding import PartitionSpec as P

prior_mass = 1.0

AXES = ("x_lo", "z", "core", "y", "x_hi")
XS = ("x_lo", "x_hi")
OWNERS = ("x_lo", "y", "x_hi")
NZ, NX = 8, 4
LANES = 128
VMEM = pl.BlockSpec(memory_space=pltpu.VMEM)
KERNEL_VMEM = 48 * 1024 * 1024


def along_z(step):
    return [(i, (i + step) % NZ) for i in range(NZ)]


def along_x(step):
    place = [(x % 2) * 2 + x // 2 for x in range(NX)]
    return [(place[x], place[(x + step) % NX]) for x in range(NX)]


def other_core(array):
    return lax.ppermute(array, "core", [(0, 1), (1, 0)])


def row_of(step):
    z, core = lax.axis_index("z"), lax.axis_index("core")
    first = lax.rem(z + step, NZ) * 2
    return first + core, first + 1 - core


def score_kernel(scale_root, n_parts, *refs):
    parts = refs[:n_parts]
    cent_ref, half_ref, weight_ref, rows_ref, logits_ref, lse_ref = refs[n_parts:]
    at = 0
    for part in parts:
        rows_ref[at : at + part.shape[0], :] = part[...]
        at += part.shape[0]
    rows = rows_ref[...]
    n_cent, tile = cent_ref.shape[0], 256
    peak = None
    for k in range(0, n_cent, tile):
        dots = lax.dot_general(
            cent_ref[k : k + tile, :], rows, (((1,), (1,)), ((), ())),
            preferred_element_type=jnp.float32,
        )
        logits = (dots - half_ref[k : k + tile, :]) * (1.0 / scale_root) + weight_ref[k : k + tile, :]
        logits_ref[k : k + tile, :] = logits
        top = jnp.max(logits, axis=0, keepdims=True)
        peak = top if peak is None else jnp.maximum(peak, top)
    mass = jnp.zeros_like(peak)
    for k in range(0, n_cent, tile):
        mass += jnp.sum(jnp.exp(logits_ref[k : k + tile, :] - peak), axis=0, keepdims=True)
    lse = peak + jnp.log(mass)
    for i in range(at // LANES):
        lse_ref[i : i + 1, :] = lse[:, i * LANES : (i + 1) * LANES]


def score(parts, cents, half_sq, log_weight, scale_root):
    count, depth = sum(p.shape[0] for p in parts), cents.shape[1]
    n_cent = cents.shape[0]
    return pl.pallas_call(
        functools.partial(score_kernel, scale_root, len(parts)),
        out_shape=(
            jax.ShapeDtypeStruct((count, depth), jnp.bfloat16),
            jax.ShapeDtypeStruct((n_cent, count), jnp.float32),
            jax.ShapeDtypeStruct((count // LANES, LANES), jnp.float32),
        ),
        in_specs=[VMEM] * (len(parts) + 3),
        out_specs=(VMEM,) * 3,
        compiler_params=pltpu.CompilerParams(vmem_limit_bytes=KERNEL_VMEM),
        cost_estimate=pl.CostEstimate(
            flops=2 * n_cent * count * depth,
            bytes_accessed=2 * (n_cent + 2 * count) * depth + 4 * n_cent * count,
            transcendentals=n_cent * count,
        ),
        name="score",
    )(*parts, cents, half_sq, log_weight)


STEPS = [(0,), (NZ - 1, 1), (NZ - 2, 2), (NZ - 3, 3), (4,)]


def table_kernel(*refs):
    table_ref = refs[-1]
    for dists, lse in zip(STEPS, refs[:-1]):
        for i, dist in enumerate(dists):
            mine, other = row_of(dist)
            table_ref[pl.ds(mine, 1), :] = lse[i : i + 1, :]
            table_ref[pl.ds(other, 1), :] = lse[len(dists) + i : len(dists) + i + 1, :]


def table_of(lses):
    return pl.pallas_call(
        table_kernel,
        out_shape=jax.ShapeDtypeStruct((2 * NZ, LANES), jnp.float32),
        in_specs=[VMEM] * len(lses),
        out_specs=VMEM,
        name="row_table",
    )(*lses)


def joined(*tables):
    top = functools.reduce(jnp.maximum, tables)
    return top + jnp.log(sum(jnp.exp(t - top) for t in tables))


def spread_kernel(*refs):
    n = len(STEPS)
    logits, rows = refs[:n], refs[n : 2 * n]
    norm_ref, sums_ref, counts_ref, own_ref = refs[2 * n :]
    total, count = None, None
    for dists, logits_ref, rows_ref in zip(STEPS, logits, rows):
        resp = []
        order = [row_of(dist) for dist in dists]
        order = [o[0] for o in order] + [o[1] for o in order]
        for i, at in enumerate(order):
            norm = norm_ref[pl.ds(at, 1), :]
            r = jnp.exp(logits_ref[:, i * LANES : (i + 1) * LANES] - norm)
            count = r if count is None else count + r
            resp.append(r.astype(jnp.bfloat16))
        part = jnp.dot(
            jnp.concatenate(resp, axis=1), rows_ref[...], preferred_element_type=jnp.float32
        )
        total = part if total is None else total + part
    sums_ref[...] = total
    counts_ref[...] = jnp.sum(count, axis=1, keepdims=True)
    own_ref[...] = norm_ref[pl.ds(row_of(0)[0], 1), :]


def spread(logits, rows, norm, tile=256):
    n_cent, depth = logits[0].shape[0], rows[0].shape[1]
    n_rows = sum(r.shape[0] for r in rows)
    whole = lambda a: pl.BlockSpec(a.shape, lambda k: (0, 0))
    return pl.pallas_call(
        spread_kernel,
        grid=(n_cent // tile,),
        out_shape=(
            jax.ShapeDtypeStruct((n_cent, depth), jnp.float32),
            jax.ShapeDtypeStruct((n_cent, 1), jnp.float32),
            jax.ShapeDtypeStruct((1, LANES), jnp.float32),
        ),
        in_specs=[pl.BlockSpec((tile, l.shape[1]), lambda k: (k, 0)) for l in logits]
        + [whole(r) for r in rows]
        + [whole(norm)],
        out_specs=(
            pl.BlockSpec((tile, depth), lambda k: (k, 0)),
            pl.BlockSpec((tile, 1), lambda k: (k, 0)),
            pl.BlockSpec((1, LANES), lambda k: (0, 0)),
        ),
        compiler_params=pltpu.CompilerParams(vmem_limit_bytes=KERNEL_VMEM),
        cost_estimate=pl.CostEstimate(
            flops=2 * n_cent * n_rows * depth,
            bytes_accessed=4 * n_cent * n_rows + 2 * n_rows * depth + 4 * n_cent * depth,
            transcendentals=n_cent * n_rows,
        ),
        name="spread",
    )(*logits, *rows, norm)


def gathered_steps(own):
    half = own.shape[0] // 2
    up = down = own
    yield [own, other_core(own)]
    for _ in range(3):
        up = lax.ppermute(up, "z", along_z(1))
        down = lax.ppermute(down, "z", along_z(-1))
        yield [up, down, other_core(jnp.concatenate([up, down]))]
    far = jnp.concatenate(
        [
            lax.ppermute(up[:half], "z", along_z(1)),
            lax.ppermute(down[half:], "z", along_z(-1)),
        ]
    )
    yield [far, other_core(far)]


def local(embeddings, centroids, log_weight):
    local_count, feat_dim = centroids.shape
    scale_root = math.sqrt(feat_dim)
    x_lo = lax.axis_index("x_lo")
    half = local_count // 2
    beside = jnp.concatenate(
        [
            lax.ppermute(centroids[:half], XS, along_x(1)),
            lax.ppermute(centroids[half:], XS, along_x(-1)),
        ]
    )
    weight_beside = lax.ppermute(log_weight, "x_lo", [(0, 1), (1, 0)])

    def in_order(mine, other):
        return jnp.where(x_lo == 0, jnp.concatenate([mine, other]), jnp.concatenate([other, mine]))

    cents = in_order(centroids, beside)
    weight = in_order(log_weight, weight_beside)[:, None]
    wide = cents.astype(jnp.float32)
    half_sq = 0.5 * jnp.sum(wide * wide, axis=1, keepdims=True)

    rows, logits, lses = zip(
        *(score(parts, cents, half_sq, weight, scale_root) for parts in gathered_steps(embeddings))
    )
    table = table_of(lses)
    table = joined(table, other_core(table))
    table = joined(table, lax.ppermute(table, "z", along_z(1)))
    table = joined(table, *(lax.ppermute(table, "z", along_z(s)) for s in (2, -2, 4)))

    sums, counts, log_norm = spread(logits, rows, table)
    low = jnp.maximum(jnp.max(jnp.abs(sums), axis=1, keepdims=True) * 2.0**-14, 2.0**-14)
    low = low.astype(jnp.float16)
    count_high = counts.astype(jnp.float16)
    count_rest = ((counts - count_high.astype(jnp.float32)) * 2.0**11).astype(jnp.float16)
    packed = jnp.concatenate(
        [
            (sums / low.astype(jnp.float32)).astype(jnp.float16),
            jnp.broadcast_to(low, (2 * local_count, 1)),
            count_high,
            count_rest,
            jnp.zeros((2 * local_count, LANES - 3), jnp.float16),
        ],
        axis=1,
    )
    owned = local_count // 8
    came = lax.all_to_all(packed.reshape(16, owned, -1), OWNERS, 0, 0, tiled=True)
    came = came.astype(jnp.float32)
    weighted = jnp.sum(came[:, :, :feat_dim] * came[:, :, feat_dim : feat_dim + 1], axis=0)
    counts = jnp.sum(came[:, :, feat_dim + 1] + came[:, :, feat_dim + 2] * 2.0**-11, axis=0)
    own_index = lax.axis_index(("y", "x_hi"))
    own_centres = lax.dynamic_slice_in_dim(centroids, own_index * owned, owned, 0).astype(jnp.float32)
    updated = (weighted + prior_mass * own_centres) / (counts[:, None] + prior_mass)
    return (updated, counts, log_norm.reshape(-1))


def solution(mesh):
    split = Mesh(mesh.devices.reshape(2, NZ, 2, 4, 2), AXES)
    block = ("x_lo", "z", "core")
    return jax.shard_map(
        local,
        mesh=split,
        in_specs=(P(AXES, None), P(block, None), P(block)),
        out_specs=(P(AXES, None), P(AXES), P(AXES)),
        check_vma=False,
    )
```

time: 192 us -> 141 us (0.73); the launches traced: 188 us -> 140 us
  waiting for transfers between devices: 90.7 us -> 39 us
  blocking collectives: 34.5 us -> 0 us
  Pallas kernels: 0 us -> 23.9 us
  starting transfers between devices: 14.2 us -> 36.7 us
  local copies, waits for them, and re-layouts: 8.15 us -> 26.5 us
  matrix products: 15.8 us -> 0 us
  between operations: 14.3 us -> 0.98 us
  other arithmetic: 10.7 us -> 12.7 us
    all_gather x1 -> x0, waiting for transfers between devices: 73.7 us -> none  [local(): row_block = lax.all_gather(embeddings, 'blk', axis=0, tiled=True)]
    all_to_all x1 -> x0, blocking collectives: 34.5 us -> none  [copy_for_each(): return lax.all_to_all(copies, axis, split_axis=0, concat_axis=0, tiled=True)]
    ppermute x0 -> x21, starting transfers between devices: none -> 31.1 us  [the longest x3 10.5 us: gathered_steps(): down = lax.ppermute(down, 'z', along_z(-1))]
    pallas_call x0 -> x7, Pallas kernels: none -> 23.9 us  [the longest x5 15.4 us: score(): pl.pallas_call(functools.partial(score_kernel, scale_root, len(parts)), o...]
    ppermute x0 -> x21, waiting for transfers between devices: none -> 17.4 us  [the longest x3 6.29 us: gathered_steps(): up = lax.ppermute(up, 'z', along_z(1))]
    dot_general x2 -> x0, matrix products: 15.8 us -> none  [the longest x1 9.89 us: local(): lax.dot_general(resp_vals.astype(jnp.bfloat16), row_block, (((0,), (0,)),...]
    unnamed x6 -> x57, local copies, waits for them, and re-layouts: 3.22 us -> 12.9 us
    all_to_all x2 -> x1, starting transfers between devices: 14.2 us -> 5.62 us  [local(): lax.all_to_all(packed.reshape(16, owned, -1), OWNERS, 0, 0, tiled=True)]
  transfers between devices with their start and end apart: 3 -> 22, of which waited for: 2 -> 8; matrix products, arithmetic and copies ran while one was open for 7% -> 7% of each run, Pallas kernels for 0% -> 8%
where the time goes in v1:
time: 141 us; the launch traced here: 140 us
  waiting for transfers between devices  39 us (28%)
  starting transfers between devices  36.7 us (26%)
  local copies, waits for them, and re-layouts  26.5 us (19%)
  Pallas kernels  23.9 us (17%)
  other arithmetic  12.7 us (9%)
    all_to_all x1, waiting for transfers between devices, local(): lax.all_to_all(packed.reshape(16, owned, -1), OWNERS, 0, 0, tiled=True)  21.7 us
    pallas_call x5, Pallas kernels, score(): pl.pallas_call(functools.partial(score_kernel, scale_root, len(parts)), o...  15.4 us
    unnamed x57, local copies, waits for them, and re-layouts  12.9 us
    ppermute x3, starting transfers between devices, gathered_steps(): down = lax.ppermute(down, 'z', along_z(-1))  10.5 us
    ppermute x3, starting transfers between devices, local(): lax.ppermute(table, 'z', along_z(s))  8.7 us
    pallas_call x1, Pallas kernels, spread(): pl.pallas_call(spread_kernel, grid=(n_cent // tile,), out_shape=(jax.Shap...  7.22 us
    all_to_all x1, local copies, waits for them, and re-layouts, local(): lax.all_to_all(packed.reshape(16, owned, -1), OWNERS, 0, 0, tiled=True)  6.33 us
    ppermute x3, waiting for transfers between devices, gathered_steps(): up = lax.ppermute(up, 'z', along_z(1))  6.29 us
  transfers between devices with their start and end apart: 22, of which 8 were waited for; matrix products, arithmetic and copies ran while one was open for 7% of the time, Pallas kernels for 8%

profile of v1, /device:TPU:8, one launch (start us, length us, event | category | flops | bytes accessed | tf_op | source)
XLA Modules:
  0.0 139.8 jit_solution(17741034438887167322)
XLA Ops:
  0.6 2.0 %collective-permute-start.4 = (bf16[128,768]{1,0:T(8,128)(2,1)}, bf16[128,768]{1,0:T(8,128)(2,1)S(1)}, u32[]{:S(2)}, u32[]{:S(2)}) collective-permute-start(bf16[128,768]{1,0:T(8,128)(2,1)} %refs_0_.1), channel_id=1, source_target_pairs={{0,16},{16,32},{32,48},{48,64},{64,80},{80,96},{96,112},{112,0},{1... | collective-permute-start | bytes 589832 | tf_op jit(solution)/shard_map/ppermute | solution.py:176
  2.6 4.0 %collective-permute-start.5 = (bf16[128,768]{1,0:T(8,128)(2,1)}, bf16[128,768]{1,0:T(8,128)(2,1)S(1)}, u32[]{:S(2)}, u32[]{:S(2)}) collective-permute-start(bf16[128,768]{1,0:T(8,128)(2,1)} %refs_0_.1), channel_id=1, source_target_pairs={{0,112},{16,0},{32,16},{48,32},{64,48},{80,64},{96,80},{112,96},{1... | collective-permute-start | bytes 589832 | tf_op jit(solution)/shard_map/ppermute | solution.py:177
  10.5 2.8 %collective-permute-start.2 = (bf16[256,768]{1,0:T(8,128)(2,1)S(1)}, bf16[256,768]{1,0:T(8,128)(2,1)}, u32[]{:S(2)}, u32[]{:S(2)}) collective-permute-start(bf16[256,768]{1,0:T(8,128)(2,1)S(1)} %get-tuple-element.51), channel_id=1, source_target_pairs={{0,129},{128,0},{1,128},{129,1},{2,131},{130,2},{3,130},{131,3},{4... | collective-permute-start | bytes 1179656 | tf_op jit(solution)/shard_map/ppermute | solution.py:196
  14.6 3.2 %collective-permute-start.8 = (bf16[128,768]{1,0:T(8,128)(2,1)S(1)}, bf16[128,768]{1,0:T(8,128)(2,1)S(1)}, u32[]{:S(2)}, u32[]{:S(2)}) collective-permute-start(bf16[128,768]{1,0:T(8,128)(2,1)S(1)} %collective-permute-done.5.refs_1_), channel_id=1, source_target_pairs={{0,112},{16,0},{32,16},{48,32},{64,48},{80,64},{96,80},{112,96},{1... | collective-permute-start | bytes 589832 | tf_op jit(solution)/shard_map/ppermute | solution.py:177
  18.6 3.3 %collective-permute-done.7.refs_0_ = bf16[128,768]{1,0:T(8,128)(2,1)S(1)} collective-permute-done((bf16[128,768]{1,0:T(8,128)(2,1)S(1)}, bf16[128,768]{1,0:T(8,128)(2,1)S(1)}, u32[]{:S(2)}, u32[]{:S(2)}) %collective-permute-start.7) | collective-permute-done | bytes 196640 | tf_op jit(solution)/shard_map/ppermute | solution.py:176
  23.3 3.2 %collective-permute-start.11 = (bf16[128,768]{1,0:T(8,128)(2,1)S(1)}, bf16[128,768]{1,0:T(8,128)(2,1)S(1)}, u32[]{:S(2)}, u32[]{:S(2)}) collective-permute-start(bf16[128,768]{1,0:T(8,128)(2,1)S(1)} %collective-permute-done.8.refs_1_), channel_id=1, source_target_pairs={{0,112},{16,0},{32,16},{48,32},{64,48},{80,64},{96,80},{112,96},{1... | collective-permute-start | bytes 589832 | tf_op jit(solution)/shard_map/ppermute | solution.py:177
  26.5 1.8 %multiply_reduce_fusion = (f32[1024]{0:T(1024)S(1)}, bf16[1024,768]{1,0:T(8,128)(2,1)S(1)}) fusion(bf16[512,768]{1,0:T(8,128)(2,1)S(1)} %copy-done.25, bf16[256,768]{1,0:T(8,128)(2,1)} %collective-permute-done.2, bf16[256,768]{1,0:T(8,128)(2,1)S(1)} %collective-permute-done.1, pred[]{:T(512)S(6)} %eq.4), kind=kLoop, calls=%fused_computation.4 | loop fusion | flops 12581888 | bytes 3149825 | tf_op jit(solution)/shard_map/reduce_sum | solution.py:207
  28.3 3.0 %collective-permute-done.10.refs_0_ = bf16[128,768]{1,0:T(8,128)(2,1)S(1)} collective-permute-done((bf16[128,768]{1,0:T(8,128)(2,1)S(1)}, bf16[128,768]{1,0:T(8,128)(2,1)S(1)}, u32[]{:S(2)}, u32[]{:S(2)}) %collective-permute-start.10) | collective-permute-done | bytes 196640 | tf_op jit(solution)/shard_map/ppermute | solution.py:176
  31.5 3.3 %collective-permute-start.14 = (bf16[64,768]{1,0:T(8,128)(2,1)S(1)}, bf16[64,768]{1,0:T(8,128)(2,1)S(1)}, u32[]{:S(2)}, u32[]{:S(2)}) collective-permute-start(bf16[64,768]{1,0:T(8,128)(2,1)S(1)} %slice.33), channel_id=1, source_target_pairs={{0,112},{16,0},{32,16},{48,32},{64,48},{80,64},{96,80},{112,96},{1... | collective-permute-start | bytes 294920 | tf_op jit(solution)/shard_map/ppermute | solution.py:182
  42.8 3.8 %score.6 = (bf16[512,768]{1,0:T(8,128)(2,1)S(1)}, f32[1024,512]{1,0:T(8,128)}, f32[4,128]{1,0:T(4,128)S(1)}) custom-call(bf16[128,768]{1,0:T(8,128)(2,1)S(1)} %collective-permute-done.4.refs_0_, bf16[128,768]{1,0:T(8,128)(2,1)S(1)} %collective-permute-done.5.refs_1_, bf16[256,768]{1,0:T(8,128)(2,1)} %collective-permute-done.6.refs_2_, ...), custom_call_target="tpu_custom_call" | custom-call | flops 805306368 | bytes 5242880 | tf_op jit(solution)/shard_map/score/pallas_call | solution.py:72
  46.6 3.8 %score.7 = (bf16[512,768]{1,0:T(8,128)(2,1)S(1)}, f32[1024,512]{1,0:T(8,128)}, f32[4,128]{1,0:T(4,128)S(1)}) custom-call(bf16[128,768]{1,0:T(8,128)(2,1)S(1)} %copy-done.1, bf16[128,768]{1,0:T(8,128)(2,1)S(1)} %copy-done.3, bf16[256,768]{1,0:T(8,128)(2,1)} %collective-permute-done.9.refs_2_, bf16[1024,768]{1,0:T(8,128)(2,1)S(1)} %get-tuple-element.47.refs_2_.refs_3_, ...), custom_call_target="tpu_custom_call" | custom-call | flops 805306368 | bytes 5242880 | tf_op jit(solution)/shard_map/score/pallas_call | solution.py:72
  50.5 2.1 %score.9 = (bf16[256,768]{1,0:T(8,128)(2,1)S(1)}, f32[1024,256]{1,0:T(8,128)S(1)}, f32[2,128]{1,0:T(2,128)S(1)}) custom-call(bf16[128,768]{1,0:T(8,128)(2,1)} %constant_dynamic-update-slice_fusion.refs_0_, bf16[128,768]{1,0:T(8,128)(2,1)} %collective-permute-done.15.refs_1_, bf16[1024,768]{1,0:T(8,128)(2,1)S(1)} %get-tuple-element.47.refs_2_.refs_3_, ...), custom_call_target="tpu_custom_call" | custom-call | flops 402653184 | bytes 3407872 | tf_op jit(solution)/shard_map/score/pallas_call | solution.py:72
  53.4 3.9 %score.8 = (bf16[512,768]{1,0:T(8,128)(2,1)S(1)}, f32[1024,512]{1,0:T(8,128)}, f32[4,128]{1,0:T(4,128)S(1)}) custom-call(bf16[128,768]{1,0:T(8,128)(2,1)S(1)} %collective-permute-done.10.refs_0_, bf16[128,768]{1,0:T(8,128)(2,1)S(1)} %collective-permute-done.11.refs_1_, bf16[256,768]{1,0:T(8,128)(2,1)} %collective-permute-done.12.refs_2_, ...), custom_call_target="tpu_custom_call" | custom-call | flops 805306368 | bytes 5242880 | tf_op jit(solution)/shard_map/score/pallas_call | solution.py:72
  62.6 4.4 %collective-permute-done.17 = f32[16,128]{1,0:T(8,128)S(1)} collective-permute-done((f32[16,128]{1,0:T(8,128)S(1)}, f32[16,128]{1,0:T(8,128)S(1)}, u32[]{:S(2)}, u32[]{:S(2)}) %collective-permute-start.17) | collective-permute-done | bytes 8224 | tf_op jit(solution)/shard_map/ppermute | solution.py:214
  68.3 2.9 %collective-permute-start.19 = (f32[16,128]{1,0:T(8,128)S(1)}, f32[16,128]{1,0:T(8,128)S(1)}, u32[]{:S(2)}, u32[]{:S(2)}) collective-permute-start(f32[16,128]{1,0:T(8,128)S(1)} %log_add_fusion.1), channel_id=1, source_target_pairs={{0,96},{16,112},{32,0},{48,16},{64,32},{80,48},{96,64},{112,80},{1... | collective-permute-start | bytes 24584 | tf_op jit(solution)/shard_map/ppermute | solution.py:215
  71.2 4.5 %collective-permute-start.20 = (f32[16,128]{1,0:T(8,128)S(1)}, f32[16,128]{1,0:T(8,128)S(1)}, u32[]{:S(2)}, u32[]{:S(2)}) collective-permute-start(f32[16,128]{1,0:T(8,128)S(1)} %log_add_fusion.1), channel_id=1, source_target_pairs={{0,64},{16,80},{32,96},{48,112},{64,0},{80,16},{96,32},{112,48},{1... | collective-permute-start | bytes 24584 | tf_op jit(solution)/shard_map/ppermute | solution.py:215
  75.7 3.1 %collective-permute-done.20 = f32[16,128]{1,0:T(8,128)S(1)} collective-permute-done((f32[16,128]{1,0:T(8,128)S(1)}, f32[16,128]{1,0:T(8,128)S(1)}, u32[]{:S(2)}, u32[]{:S(2)}) %collective-permute-start.20) | collective-permute-done | bytes 8224 | tf_op jit(solution)/shard_map/ppermute | solution.py:215
  85.7 7.2 %spread.1 = (f32[1024,768]{1,0:T(8,128)}, f32[1024,1]{1,0:T(8,128)S(1)}, f32[1,128]{1,0:T(1,128)}) custom-call(f32[1024,256]{1,0:T(8,128)S(1)} %copy-done.11, f32[1024,512]{1,0:T(8,128)} %get-tuple-element.22.refs_1_, f32[1024,512]{1,0:T(8,128)} %get-tuple-element.23.refs_2_, f32[1024,512]{1,0:T(8,128)} %get-tuple-element.24.refs_3_, ...), custom_call_target="tpu_custom_call" | custom-call | flops 3221225472 | bytes 14680064 | tf_op jit(solution)/shard_map/spread/pallas_call | solution.py:145
  92.9 2.3 %abs_reduce_fusion = f32[1024]{0:T(1024)S(1)} fusion(f32[1024,768]{1,0:T(8,128)} %get-tuple-element.36), kind=kLoop, calls=%fused_computation.3 | loop fusion | flops 1571840 | bytes 3149824 | tf_op jit(solution)/shard_map/reduce_max | solution.py:218
  96.7 3.4 %concatenate.68 = f16[16,64,896]{2,1,0:T(8,128)(2,1)} concatenate(f16[16,64,768]{2,1,0:T(8,128)(2,1)S(1)} %bitcast.9, f16[16,64,1]{2,1,0:T(8,128)(2,1)S(1)} %convert_element_type.58, f16[16,64,1]{2,1,0:T(8,128)(2,1)S(1)} %bitcast.11, f16[16,64,1]{2,1,0:T(8,128)(2,1)S(1)} %bitcast.10, f16[16,64,125]{2,1,0:T(8,128)(2,1)S(1)} %broadcast_in_dim.2), dimensions={2} | concatenate | bytes 3670016 | tf_op jit(solution)/shard_map/concatenate | solution.py:222
  100.2 5.6 %all-to-all-start = ((f16[16,64,896]{2,1,0:T(8,128)(2,1)}), f16[16,64,896]{2,1,0:T(8,128)(2,1)S(1)}, u32[]{:S(2)}, u32[]{:S(2)}) async-start(f16[16,64,896]{2,1,0:T(8,128)(2,1)} %concatenate.68), calls=%async_computation | async-start | bytes 3670016 | tf_op jit(solution)/shard_map/all_to_all | solution.py:233
  106.8 21.7 %all-to-all-done = f16[16,64,896]{2,1,0:T(8,128)(2,1)S(1)} async-done(((f16[16,64,896]{2,1,0:T(8,128)(2,1)}), f16[16,64,896]{2,1,0:T(8,128)(2,1)S(1)}, u32[]{:S(2)}, u32[]{:S(2)}) %all-to-all-start) | async-done | bytes 1835040 | tf_op jit(solution)/shard_map/all_to_all | solution.py:233
  128.5 6.3 %copy.28 = f16[16,64,896]{1,0,2:T(8,128)(2,1)} copy(f16[16,64,896]{2,1,0:T(8,128)(2,1)S(1)} %all-to-all-done) | data formatting | bytes 3670016 | tf_op jit(solution)/shard_map/all_to_all | solution.py:233
  134.8 2.6 %convert_element_type.56 = f32[16,64,896]{1,0,2:T(8,128)S(1)} convert(f16[16,64,896]{1,0,2:T(8,128)(2,1)} %copy.28) | non-fusion elementwise | flops 917504 | bytes 5505024 | tf_op jit(solution)/shard_map/convert_element_type | solution.py:234
  (115 shorter events, 34.6 us)
Async XLA Ops:
  0.6 13.8 %collective-permute-start.4 = (bf16[128,768]{1,0:T(8,128)(2,1)}, bf16[128,768]{1,0:T(8,128)(2,1)S(1)}, u32[]{:S(2)}, u32[]{:S(2)}) collective-permute-start(bf16[128,768]{1,0:T(8,128)(2,1)} %refs_0_.1), channel_id=1, source_target_pairs={{0,16},{16,32},{32,48},{48,64},{64,80},{80,96},{96,112},{112,0},{1... | collective-permute-start | bytes 589832 | tf_op jit(solution)/shard_map/ppermute | solution.py:176
  2.6 11.9 %collective-permute-start.5 = (bf16[128,768]{1,0:T(8,128)(2,1)}, bf16[128,768]{1,0:T(8,128)(2,1)S(1)}, u32[]{:S(2)}, u32[]{:S(2)}) collective-permute-start(bf16[128,768]{1,0:T(8,128)(2,1)} %refs_0_.1), channel_id=1, source_target_pairs={{0,112},{16,0},{32,16},{48,32},{64,48},{80,64},{96,80},{112,96},{1... | collective-permute-start | bytes 589832 | tf_op jit(solution)/shard_map/ppermute | solution.py:177
  6.7 32.7 %collective-permute-start = (bf16[128,768]{1,0:T(8,128)(2,1)}, bf16[128,768]{1,0:T(8,128)(2,1)}, u32[]{:S(2)}, u32[]{:S(2)}) collective-permute-start(bf16[128,768]{1,0:T(8,128)(2,1)} %refs_0_.1), channel_id=1, source_target_pairs={{0,8},{8,0},{1,9},{9,1},{2,10},{10,2},{3,11},{11,3},{4,12},{12,4},... | collective-permute-start | bytes 589832 | tf_op jit(solution)/shard_map/ppermute | solution.py:33
  6.7 3.8 %collective-permute-start.3 = (f32[512]{0:T(512)}, f32[512]{0:T(512)S(1)}, u32[]{:S(2)}, u32[]{:S(2)}) collective-permute-start(f32[512]{0:T(512)} %param.5), channel_id=1, source_target_pairs={{0,128},{128,0},{1,129},{129,1},{2,130},{130,2},{3,131},{131,3},{4... | collective-permute-start | bytes 6152 | tf_op jit(solution)/shard_map/ppermute | solution.py:199
  9.3 14.0 %collective-permute-start.1 = (bf16[256,768]{1,0:T(8,128)(2,1)S(1)}, bf16[256,768]{1,0:T(8,128)(2,1)S(1)}, u32[]{:S(2)}, u32[]{:S(2)}) collective-permute-start(bf16[256,768]{1,0:T(8,128)(2,1)S(1)} %get-tuple-element.50), channel_id=1, source_target_pairs={{0,128},{128,1},{1,129},{129,0},{2,130},{130,3},{3,131},{131,2},{4... | collective-permute-start | bytes 1179656 | tf_op jit(solution)/shard_map/ppermute | solution.py:195
  10.5 12.8 %collective-permute-start.2 = (bf16[256,768]{1,0:T(8,128)(2,1)S(1)}, bf16[256,768]{1,0:T(8,128)(2,1)}, u32[]{:S(2)}, u32[]{:S(2)}) collective-permute-start(bf16[256,768]{1,0:T(8,128)(2,1)S(1)} %get-tuple-element.51), channel_id=1, source_target_pairs={{0,129},{128,0},{1,128},{129,1},{2,131},{130,2},{3,130},{131,3},{4... | collective-permute-start | bytes 1179656 | tf_op jit(solution)/shard_map/ppermute | solution.py:196
  14.5 7.5 %collective-permute-start.7 = (bf16[128,768]{1,0:T(8,128)(2,1)S(1)}, bf16[128,768]{1,0:T(8,128)(2,1)S(1)}, u32[]{:S(2)}, u32[]{:S(2)}) collective-permute-start(bf16[128,768]{1,0:T(8,128)(2,1)S(1)} %collective-permute-done.4.refs_0_), channel_id=1, source_target_pairs={{0,16},{16,32},{32,48},{48,64},{64,80},{80,96},{96,112},{112,0},{1... | collective-permute-start | bytes 589832 | tf_op jit(solution)/shard_map/ppermute | solution.py:176
  14.6 7.4 %collective-permute-start.8 = (bf16[128,768]{1,0:T(8,128)(2,1)S(1)}, bf16[128,768]{1,0:T(8,128)(2,1)S(1)}, u32[]{:S(2)}, u32[]{:S(2)}) collective-permute-start(bf16[128,768]{1,0:T(8,128)(2,1)S(1)} %collective-permute-done.5.refs_1_), channel_id=1, source_target_pairs={{0,112},{16,0},{32,16},{48,32},{64,48},{80,64},{96,80},{112,96},{1... | collective-permute-start | bytes 589832 | tf_op jit(solution)/shard_map/ppermute | solution.py:177
  21.9 17.1 %copy-start = (bf16[128,768]{1,0:T(8,128)(2,1)}, bf16[128,768]{1,0:T(8,128)(2,1)S(1)}, u32[]{:S(2)}) copy-start(bf16[128,768]{1,0:T(8,128)(2,1)S(1)} %collective-permute-done.7.refs_0_) | copy-start | bytes 589828
  21.9 20.9 %collective-permute-start.6 = (bf16[256,768]{1,0:T(8,128)(2,1)}, bf16[256,768]{1,0:T(8,128)(2,1)}, u32[]{:S(2)}, u32[]{:S(2)}) collective-permute-start(bf16[256,768]{1,0:T(8,128)(2,1)} %pad_maximum_fusion), channel_id=1, source_target_pairs={{0,8},{8,0},{1,9},{9,1},{2,10},{10,2},{3,11},{11,3},{4,12},{12,4},... | collective-permute-start | bytes 1179656 | tf_op jit(solution)/shard_map/ppermute | solution.py:33
  22.8 23.8 %collective-permute-start.9 = (bf16[256,768]{1,0:T(8,128)(2,1)}, bf16[256,768]{1,0:T(8,128)(2,1)}, u32[]{:S(2)}, u32[]{:S(2)}) collective-permute-start(bf16[256,768]{1,0:T(8,128)(2,1)} %pad_maximum_fusion.1), channel_id=1, source_target_pairs={{0,8},{8,0},{1,9},{9,1},{2,10},{10,2},{3,11},{11,3},{4,12},{12,4},... | collective-permute-start | bytes 1179656 | tf_op jit(solution)/shard_map/ppermute | solution.py:33
  23.3 8.0 %collective-permute-start.10 = (bf16[128,768]{1,0:T(8,128)(2,1)S(1)}, bf16[128,768]{1,0:T(8,128)(2,1)S(1)}, u32[]{:S(2)}, u32[]{:S(2)}) collective-permute-start(bf16[128,768]{1,0:T(8,128)(2,1)S(1)} %collective-permute-done.7.refs_0_), channel_id=1, source_target_pairs={{0,16},{16,32},{32,48},{48,64},{64,80},{80,96},{96,112},{112,0},{1... | collective-permute-start | bytes 589832 | tf_op jit(solution)/shard_map/ppermute | solution.py:176
  23.3 8.1 %collective-permute-start.11 = (bf16[128,768]{1,0:T(8,128)(2,1)S(1)}, bf16[128,768]{1,0:T(8,128)(2,1)S(1)}, u32[]{:S(2)}, u32[]{:S(2)}) collective-permute-start(bf16[128,768]{1,0:T(8,128)(2,1)S(1)} %collective-permute-done.8.refs_1_), channel_id=1, source_target_pairs={{0,112},{16,0},{32,16},{48,32},{64,48},{80,64},{96,80},{112,96},{1... | collective-permute-start | bytes 589832 | tf_op jit(solution)/shard_map/ppermute | solution.py:177
  31.3 5.9 %collective-permute-start.13 = (bf16[64,768]{1,0:T(8,128)(2,1)S(1)}, bf16[64,768]{1,0:T(8,128)(2,1)S(1)}, u32[]{:S(2)}, u32[]{:S(2)}) collective-permute-start(bf16[64,768]{1,0:T(8,128)(2,1)S(1)} %slice.32), channel_id=1, source_target_pairs={{0,16},{16,32},{32,48},{48,64},{64,80},{80,96},{96,112},{112,0},{1... | collective-permute-start | bytes 294920 | tf_op jit(solution)/shard_map/ppermute | solution.py:181
  31.5 6.5 %collective-permute-start.14 = (bf16[64,768]{1,0:T(8,128)(2,1)S(1)}, bf16[64,768]{1,0:T(8,128)(2,1)S(1)}, u32[]{:S(2)}, u32[]{:S(2)}) collective-permute-start(bf16[64,768]{1,0:T(8,128)(2,1)S(1)} %slice.33), channel_id=1, source_target_pairs={{0,112},{16,0},{32,16},{48,32},{64,48},{80,64},{96,80},{112,96},{1... | collective-permute-start | bytes 294920 | tf_op jit(solution)/shard_map/ppermute | solution.py:182
  37.2 16.1 %collective-permute-start.12 = (bf16[256,768]{1,0:T(8,128)(2,1)}, bf16[256,768]{1,0:T(8,128)(2,1)}, u32[]{:S(2)}, u32[]{:S(2)}) collective-permute-start(bf16[256,768]{1,0:T(8,128)(2,1)} %pad_maximum_fusion.2), channel_id=1, source_target_pairs={{0,8},{8,0},{1,9},{9,1},{2,10},{10,2},{3,11},{11,3},{4,12},{12,4},... | collective-permute-start | bytes 1179656 | tf_op jit(solution)/shard_map/ppermute | solution.py:33
  38.6 11.9 %collective-permute-start.15 = (bf16[128,768]{1,0:T(8,128)(2,1)}, bf16[128,768]{1,0:T(8,128)(2,1)}, u32[]{:S(2)}, u32[]{:S(2)}) collective-permute-start(bf16[128,768]{1,0:T(8,128)(2,1)} %constant_dynamic-update-slice_fusion.refs_0_), channel_id=1, source_target_pairs={{0,8},{8,0},{1,9},{9,1},{2,10},{10,2},{3,11},{11,3},{4,12},{12,4},... | collective-permute-start | bytes 589832 | tf_op jit(solution)/shard_map/ppermute | solution.py:33
  50.4 28.4 %copy-start.21 = (bf16[256,768]{1,0:T(8,128)(2,1)S(1)}, bf16[256,768]{1,0:T(8,128)(2,1)}, u32[]{:S(2)}) copy-start(bf16[256,768]{1,0:T(8,128)(2,1)} %copy-done.20) | copy-start | bytes 1179652
  60.0 1.4 collective-permute-start.16
  62.1 4.9 %collective-permute-start.17 = (f32[16,128]{1,0:T(8,128)S(1)}, f32[16,128]{1,0:T(8,128)S(1)}, u32[]{:S(2)}, u32[]{:S(2)}) collective-permute-start(f32[16,128]{1,0:T(8,128)S(1)} %log_add_fusion.2), channel_id=1, source_target_pairs={{0,16},{16,32},{32,48},{48,64},{64,80},{80,96},{96,112},{112,0},{1... | collective-permute-start | bytes 24584 | tf_op jit(solution)/shard_map/ppermute | solution.py:214
  67.0 8.7 %collective-permute-start.18 = (f32[16,128]{1,0:T(8,128)S(1)}, f32[16,128]{1,0:T(8,128)S(1)}, u32[]{:S(2)}, u32[]{:S(2)}) collective-permute-start(f32[16,128]{1,0:T(8,128)S(1)} %log_add_fusion.1), channel_id=1, source_target_pairs={{0,32},{16,48},{32,64},{48,80},{64,96},{80,112},{96,0},{112,16},{1... | collective-permute-start | bytes 24584 | tf_op jit(solution)/shard_map/ppermute | solution.py:215
  68.3 7.4 %collective-permute-start.19 = (f32[16,128]{1,0:T(8,128)S(1)}, f32[16,128]{1,0:T(8,128)S(1)}, u32[]{:S(2)}, u32[]{:S(2)}) collective-permute-start(f32[16,128]{1,0:T(8,128)S(1)} %log_add_fusion.1), channel_id=1, source_target_pairs={{0,96},{16,112},{32,0},{48,16},{64,32},{80,48},{96,64},{112,80},{1... | collective-permute-start | bytes 24584 | tf_op jit(solution)/shard_map/ppermute | solution.py:215
  71.2 7.6 %collective-permute-start.20 = (f32[16,128]{1,0:T(8,128)S(1)}, f32[16,128]{1,0:T(8,128)S(1)}, u32[]{:S(2)}, u32[]{:S(2)}) collective-permute-start(f32[16,128]{1,0:T(8,128)S(1)} %log_add_fusion.1), channel_id=1, source_target_pairs={{0,64},{16,80},{32,96},{48,112},{64,0},{80,16},{96,32},{112,48},{1... | collective-permute-start | bytes 24584 | tf_op jit(solution)/shard_map/ppermute | solution.py:215
  100.2 28.3 %all-to-all-start = ((f16[16,64,896]{2,1,0:T(8,128)(2,1)}), f16[16,64,896]{2,1,0:T(8,128)(2,1)S(1)}, u32[]{:S(2)}, u32[]{:S(2)}) async-start(f16[16,64,896]{2,1,0:T(8,128)(2,1)} %concatenate.68), calls=%async_computation | async-start | bytes 3670016 | tf_op jit(solution)/shard_map/all_to_all | solution.py:233
  (25 other events, 101.6 us)

commit v2 on v0

v2 whole, which is shorter than its diff:
```python
import functools
import math

import jax
import jax.numpy as jnp
from jax import lax
from jax.experimental import pallas as pl
from jax.experimental.pallas import tpu as pltpu
from jax.sharding import Mesh
from jax.sharding import PartitionSpec as P

prior_mass = 1.0

AXES = ("x_lo", "z", "core", "y", "x_hi")
XS = ("x_lo", "x_hi")
OWNERS = ("x_lo", "y", "x_hi")
NZ, NX, N_OWNERS = 8, 4, 16
LANES = 128
VMEM = pl.BlockSpec(memory_space=pltpu.VMEM)
EXTRA = 8


def along_z(step):
    return [(i, (i + step) % NZ) for i in range(NZ)]


def along_x(step):
    place = [(x % 2) * 2 + x // 2 for x in range(NX)]
    return [(place[x], place[(x + step) % NX]) for x in range(NX)]


def other_core(array):
    return lax.ppermute(array, "core", [(0, 1), (1, 0)])


def call(kernel, outs, args, name, flops=0, transcendentals=0, vmem=24):
    size = sum(a.size * a.dtype.itemsize for a in (*args, *outs))
    return pl.pallas_call(
        kernel,
        out_shape=outs,
        in_specs=[VMEM] * len(args),
        out_specs=(VMEM,) * len(outs),
        compiler_params=pltpu.CompilerParams(vmem_limit_bytes=vmem * 1024 * 1024),
        cost_estimate=pl.CostEstimate(
            flops=flops, bytes_accessed=size, transcendentals=transcendentals
        ),
        name=name,
    )(*args)


def shape(dims, dtype=jnp.float32):
    return jax.ShapeDtypeStruct(dims, dtype)


def column(row):
    n = row.shape[1]
    return jnp.concatenate(
        [jnp.broadcast_to(row[:, i : i + LANES], (LANES, LANES)).T[:, :1] for i in range(0, n, LANES)]
    )


def centroid_kernel(scale_root, mine_ref, up_ref, down_ref, weight_ref, beside_ref, cent_ref, bias_ref):
    n = mine_ref.shape[0]
    x_lo = lax.axis_index("x_lo")
    first, second = pl.multiple_of(x_lo * n, n), pl.multiple_of((1 - x_lo) * n, n)
    beside = jnp.concatenate([up_ref[...], down_ref[...]])
    for at, block, weight in ((first, mine_ref[...], weight_ref), (second, beside, beside_ref)):
        cent_ref[pl.ds(at, n), :] = block
        wide = block.astype(jnp.float32)
        half_sq = 0.5 * jnp.sum(wide * wide, axis=1, keepdims=True)
        bias_ref[pl.ds(at, n), :] = column(weight[...]) - half_sq * (1.0 / scale_root)


def row_of(step):
    z, core = lax.axis_index("z"), lax.axis_index("core")
    first = lax.rem(z + step, NZ) * 2
    return first + core, first + 1 - core


def score_kernel(scale_root, n_parts, *refs):
    parts = refs[:n_parts]
    cent_ref, bias_ref, rows_ref, logits_ref, lse_ref = refs[n_parts:]
    at = 0
    for part in parts:
        rows_ref[at : at + part.shape[0], :] = part[...]
        at += part.shape[0]
    tile = 256
    for k in range(0, at, tile):
        dots = lax.dot_general(
            cent_ref[...], rows_ref[k : k + tile, :], (((1,), (1,)), ((), ())),
            preferred_element_type=jnp.float32,
        )
        logits = dots * (1.0 / scale_root) + bias_ref[...]
        logits_ref[:, k : k + tile] = logits
        peak = jnp.max(logits, axis=0, keepdims=True)
        lse = peak + jnp.log(jnp.sum(jnp.exp(logits - peak), axis=0, keepdims=True))
        for i in range(tile // LANES):
            row = k // LANES + i
            lse_ref[row : row + 1, :] = lse[:, i * LANES : (i + 1) * LANES]


def score(parts, cents, bias, scale_root):
    count, depth = sum(p.shape[0] for p in parts), cents.shape[1]
    n_cent = cents.shape[0]
    return call(
        functools.partial(score_kernel, scale_root, len(parts)),
        (
            shape((count, depth), jnp.bfloat16),
            shape((n_cent, count)),
            shape((count // LANES, LANES)),
        ),
        (*parts, cents, bias),
        "score",
        2 * n_cent * count * depth,
        n_cent * count,
    )


def table_kernel(orders, *refs):
    table_ref = refs[-1]
    for order, lse in zip(orders, refs[:-1]):
        for i, (dist, side) in enumerate(order):
            table_ref[pl.ds(row_of(dist)[side], 1), :] = lse[i : i + 1, :]


def joined(*tables):
    top = functools.reduce(jnp.maximum, tables)
    return top + jnp.log(sum(jnp.exp(t - top) for t in tables))


def spread_kernel(orders, *refs):
    n = len(orders)
    logits, rows = refs[:n], refs[n : 2 * n]
    norm_ref, packed_ref, own_ref = refs[2 * n :]
    n_cent, depth, tile = logits[0].shape[0], rows[0].shape[1], 256
    owned = n_cent // N_OWNERS
    for k in range(0, n_cent, tile):
        total, count = None, None
        for order, logits_ref, rows_ref in zip(orders, logits, rows):
            resp = []
            for i, (dist, side) in enumerate(order):
                norm = norm_ref[pl.ds(row_of(dist)[side], 1), :]
                r = jnp.exp(logits_ref[k : k + tile, i * LANES : (i + 1) * LANES] - norm)
                count = r if count is None else count + r
                resp.append(r.astype(jnp.bfloat16))
            part = jnp.dot(
                jnp.concatenate(resp, axis=1), rows_ref[...], preferred_element_type=jnp.float32
            )
            total = part if total is None else total + part
        count = jnp.sum(count, axis=1, keepdims=True)
        top = jnp.max(jnp.abs(total), axis=1, keepdims=True)
        scale = jnp.maximum(top * 2.0**-14, 2.0**-14).astype(jnp.bfloat16).astype(jnp.float32)
        total = total * (1.0 / scale)
        high = count.astype(jnp.bfloat16).astype(jnp.float32)
        middle = (count - high).astype(jnp.bfloat16).astype(jnp.float32)
        low = count - high - middle
        lane = lax.broadcasted_iota(jnp.int32, (tile, LANES), 1)
        extra = jnp.zeros((tile, LANES), jnp.float32)
        for i, value in enumerate((scale, high, middle * 2.0**8, low * 2.0**16)):
            extra = jnp.where(lane == i, value, extra)
        extra = extra.T[:EXTRA, :]
        for b in range(tile // owned):
            owner = k // owned + b
            for j in range(depth // LANES):
                packed_ref[owner, j * owned : (j + 1) * owned, :] = total[
                    b * owned : (b + 1) * owned, j * LANES : (j + 1) * LANES
                ]
            at = depth // LANES * owned
            packed_ref[owner, at : at + EXTRA, :] = jnp.concatenate(
                [
                    extra[:, b * owned : (b + 1) * owned],
                    jnp.zeros((EXTRA, LANES - owned), jnp.float32),
                ],
                axis=1,
            )
    own_ref[...] = norm_ref[pl.ds(row_of(0)[0], 1), :]


def update_kernel(came_ref, cent_ref, updated_ref, counts_ref):
    owned, depth = updated_ref.shape
    at = depth // LANES * owned
    extra = jnp.concatenate([came_ref[i, at : at + EXTRA, :] for i in range(N_OWNERS)])
    counts = None
    for i in range(N_OWNERS):
        e = i * EXTRA
        c = extra[e + 1 : e + 2] + (extra[e + 2 : e + 3] * 2.0**-8 + extra[e + 3 : e + 4] * 2.0**-16)
        counts = c if counts is None else counts + c
    counts_ref[...] = counts[:, :owned]
    turned = extra.T
    mass = jnp.broadcast_to(counts, (LANES, LANES)).T[:owned, :1] + prior_mass
    first = lax.axis_index("y") * 2 + lax.axis_index("x_hi")
    own = cent_ref[pl.ds(pl.multiple_of(first * owned, owned), owned), :].astype(jnp.float32)
    for j in range(depth // LANES):
        total = None
        for i in range(N_OWNERS):
            scale = turned[:owned, i * EXTRA : i * EXTRA + 1]
            part = came_ref[i, j * owned : (j + 1) * owned, :] * scale
            total = part if total is None else total + part
        here = slice(j * LANES, (j + 1) * LANES)
        updated_ref[:, here] = (total + prior_mass * own[:, here]) / mass


def local(embeddings, centroids, log_weight):
    local_count, feat_dim = centroids.shape
    n_rows = embeddings.shape[0]
    scale_root = math.sqrt(feat_dim)
    half = local_count // 2
    owned = local_count // 8

    other = other_core(embeddings)
    beside = (
        lax.ppermute(centroids[:half], XS, along_x(1)),
        lax.ppermute(centroids[half:], XS, along_x(-1)),
    )
    weight = log_weight[None, :]
    weight_beside = lax.ppermute(weight, "x_lo", [(0, 1), (1, 0)])
    cents, bias = call(
        functools.partial(centroid_kernel, scale_root),
        (shape((2 * local_count, feat_dim), jnp.bfloat16), shape((2 * local_count, 1))),
        (centroids, *beside, weight, weight_beside),
        "centroid_blocks",
        4 * local_count * feat_dim,
    )

    waiting, order = [embeddings, other], [(0, 0), (0, 1)]
    orders, scored = [], []
    up = down = embeddings
    for step in range(1, 4):
        up = lax.ppermute(up, "z", along_z(1))
        down = lax.ppermute(down, "z", along_z(-1))
        if step > 1:
            scored.append(score(waiting, cents, bias, scale_root))
            orders.append(order)
            up, down, _ = lax.optimization_barrier((up, down, scored[-1][2]))
            waiting, order = [], []
        if step == 2:
            waiting += swapped
            order += [(NZ - 1, 1), (1, 1)]
        if step == 3:
            waiting += swapped
            order += [(NZ - 2, 1), (2, 1)]
        waiting += [up, down]
        order += [(NZ - step, 0), (step, 0)]
        swapped = [other_core(up), other_core(down)]
    piece = n_rows // 2
    far = [
        lax.ppermute(up[:piece], "z", along_z(1)),
        lax.ppermute(down[piece:], "z", along_z(-1)),
    ]
    scored.append(score(waiting, cents, bias, scale_root))
    orders.append(order)
    scored.append(score(swapped, cents, bias, scale_root))
    orders.append([(NZ - 3, 1), (3, 1)])
    far = lax.optimization_barrier((*far, scored[-2][2], scored[-1][2]))[:2]
    far_other = other_core(jnp.concatenate(far))
    scored.append(score([*far, far_other], cents, bias, scale_root))
    orders.append([(4, 0), (4, 1)])
    rows, logits, lses = zip(*scored)

    (table,) = call(
        functools.partial(table_kernel, orders), (shape((2 * NZ, LANES)),), lses, "row_table"
    )
    table = joined(table, other_core(table))
    table = joined(table, lax.ppermute(table, "z", along_z(1)))
    table = joined(table, *(lax.ppermute(table, "z", along_z(s)) for s in (2, -2, 4)))

    n_all = 2 * NZ * n_rows
    packed, log_norm = call(
        functools.partial(spread_kernel, orders),
        (
            shape((N_OWNERS, owned * feat_dim // LANES + EXTRA, LANES)),
            shape((1, LANES)),
        ),
        (*logits, *rows, table),
        "spread",
        4 * local_count * n_all * feat_dim,
        2 * local_count * n_all,
    )
    came = lax.all_to_all(packed.astype(jnp.float16), OWNERS, 0, 0, tiled=True)
    updated, counts = call(
        update_kernel,
        (shape((owned, feat_dim)), shape((1, owned))),
        (came.astype(jnp.float32), centroids),
        "update",
    )
    return (updated, counts.reshape(-1), log_norm.reshape(-1))


def solution(mesh):
    split = Mesh(mesh.devices.reshape(2, NZ, 2, 4, 2), AXES)
    block = ("x_lo", "z", "core")
    return jax.shard_map(
        local,
        mesh=split,
        in_specs=(P(AXES, None), P(block, None), P(block)),
        out_specs=(P(AXES, None), P(AXES), P(AXES)),
        check_vma=False,
    )
```

time: 192 us -> 94.6 us (0.49); the launches traced: 188 us -> 94.3 us
  waiting for transfers between devices: 90.7 us -> 22.8 us
  matrix products: 15.8 us -> 0 us
  starting transfers between devices: 14.2 us -> 28.4 us
  between operations: 14.3 us -> 0.77 us
  Pallas kernels: 0 us -> 12.6 us
  other arithmetic: 10.7 us -> 0.48 us
  blocking collectives: 34.5 us -> 27.3 us
  local copies, waits for them, and re-layouts: 8.15 us -> 1.96 us
    all_gather x1 -> x0, waiting for transfers between devices: 73.7 us -> none  [local(): row_block = lax.all_gather(embeddings, 'blk', axis=0, tiled=True)]
    ppermute x0 -> x24, starting transfers between devices: none -> 28.4 us  [the longest x3 10.9 us: local(): down = lax.ppermute(down, 'z', along_z(-1))]
    ppermute x0 -> x24, waiting for transfers between devices: none -> 22.8 us  [the longest x3 6.07 us: local(): up = lax.ppermute(up, 'z', along_z(1))]
    all_to_all x2 -> x0, waiting for transfers between devices: 16.3 us -> none  [sent_and_summed(): tiles = lax.all_to_all(cut_along(array, dim, count), axis, 0, 0, tiled=True)]
    dot_general x2 -> x0, matrix products: 15.8 us -> none  [the longest x1 9.89 us: local(): lax.dot_general(resp_vals.astype(jnp.bfloat16), row_block, (((0,), (0,)),...]
    all_to_all x2 -> x0, starting transfers between devices: 14.2 us -> none  [sent_and_summed(): tiles = lax.all_to_all(cut_along(array, dim, count), axis, 0, 0, tiled=True)]
    pallas_call x0 -> x9, Pallas kernels: none -> 12.6 us  [call(): pl.pallas_call(kernel, out_shape=outs, in_specs=[VMEM] * len(args), out_s...]
    reduce_sum x5 -> x0, other arithmetic: 7.37 us -> none  [the longest x1 4.57 us: local(): contrib, count_part = (contrib, jnp.sum(resp_vals, axis=0))]
  transfers between devices with their start and end apart: 3 -> 24, of which waited for: 2 -> 11; matrix products, arithmetic and copies ran while one was open for 7% -> 0% of each run, Pallas kernels for 0% -> 6%
where the time goes in v2:
time: 94.6 us; the launch traced here: 94.3 us
  starting transfers between devices  28.4 us (30%)
  blocking collectives  27.3 us (29%)
  waiting for transfers between devices  22.8 us (24%)
  Pallas kernels  12.6 us (13%)
  local copies, waits for them, and re-layouts  1.96 us (2%)
    all_to_all x1, blocking collectives, local(): came = lax.all_to_all(packed.astype(jnp.float16), OWNERS, 0, 0, tiled=True)  27.3 us
    pallas_call x9, Pallas kernels, call(): pl.pallas_call(kernel, out_shape=outs, in_specs=[VMEM] * len(args), out_s...  12.6 us
    ppermute x3, starting transfers between devices, local(): down = lax.ppermute(down, 'z', along_z(-1))  10.9 us
    ppermute x3, starting transfers between devices, local(): lax.ppermute(table, 'z', along_z(s))  7.1 us
    ppermute x3, waiting for transfers between devices, local(): up = lax.ppermute(up, 'z', along_z(1))  6.07 us
    ppermute x1, waiting for transfers between devices, local(): table = joined(table, lax.ppermute(table, 'z', along_z(1)))  4.85 us
    ppermute x1, waiting for transfers between devices, local(): lax.ppermute(up[:piece], 'z', along_z(1))  3.53 us
    ppermute x1, waiting for transfers between devices, local(): weight_beside = lax.ppermute(weight, 'x_lo', [(0, 1), (1, 0)])  3.04 us
  transfers between devices with their start and end apart: 24, of which 11 were waited for; matrix products, arithmetic and copies ran while one was open for 0% of the time, Pallas kernels for 6%

profile of v2, /device:TPU:8, one launch (start us, length us, event | category | flops | bytes accessed | tf_op | source)
XLA Modules:
  0.0 94.3 jit_solution(9370196615832095600)
XLA Ops:
  0.7 1.2 %fusion.2 = (bf16[256,768]{1,0:T(8,128)(2,1)S(1)}, bf16[256,768]{1,0:T(8,128)(2,1)S(1)}) fusion(bf16[512,768]{1,0:T(8,128)(2,1)} %cent_ref.1), kind=kLoop, calls=%fused_computation.8 | loop fusion | bytes 1572864 | tf_op jit(solution)/shard_map/slice | solution.py:213
  1.9 2.8 %collective-permute-start.4 = (bf16[256,768]{1,0:T(8,128)(2,1)S(1)}, bf16[256,768]{1,0:T(8,128)(2,1)S(1)}, u32[]{:S(2)}, u32[]{:S(2)}) collective-permute-start(bf16[256,768]{1,0:T(8,128)(2,1)S(1)} %get-tuple-element.57), channel_id=1, source_target_pairs={{0,129},{128,0},{1,128},{129,1},{2,131},{130,2},{3,130},{131,3},{4... | collective-permute-start | bytes 1179656 | tf_op jit(solution)/shard_map/ppermute | solution.py:213
  4.7 1.9 %collective-permute-start.1 = (bf16[128,768]{1,0:T(8,128)(2,1)}, bf16[128,768]{1,0:T(8,128)(2,1)S(1)}, u32[]{:S(2)}, u32[]{:S(2)}) collective-permute-start(bf16[128,768]{1,0:T(8,128)(2,1)} %refs_0_.1), channel_id=1, source_target_pairs={{0,16},{16,32},{32,48},{48,64},{64,80},{80,96},{96,112},{112,0},{1... | collective-permute-start | bytes 589832 | tf_op jit(solution)/shard_map/ppermute | solution.py:229
  6.7 3.9 %collective-permute-start.2 = (bf16[128,768]{1,0:T(8,128)(2,1)}, bf16[128,768]{1,0:T(8,128)(2,1)S(1)}, u32[]{:S(2)}, u32[]{:S(2)}) collective-permute-start(bf16[128,768]{1,0:T(8,128)(2,1)} %refs_0_.1), channel_id=1, source_target_pairs={{0,112},{16,0},{32,16},{48,32},{64,48},{80,64},{96,80},{112,96},{1... | collective-permute-start | bytes 589832 | tf_op jit(solution)/shard_map/ppermute | solution.py:230
  11.4 3.0 %collective-permute-done.5.beside_ref = f32[1,512]{1,0:T(1,128)S(1)} collective-permute-done((f32[1,512]{1,0:T(1,128)}, f32[1,512]{1,0:T(1,128)S(1)}, u32[]{:S(2)}, u32[]{:S(2)}) %collective-permute-start.5) | collective-permute-done | bytes 2080 | tf_op jit(solution)/shard_map/ppermute | solution.py:216
  15.4 3.7 %collective-permute-start.9 = (bf16[128,768]{1,0:T(8,128)(2,1)S(1)}, bf16[128,768]{1,0:T(8,128)(2,1)S(1)}, u32[]{:S(2)}, u32[]{:S(2)}) collective-permute-start(bf16[128,768]{1,0:T(8,128)(2,1)S(1)} %collective-permute-done.2.refs_3_), channel_id=1, source_target_pairs={{0,112},{16,0},{32,16},{48,32},{64,48},{80,64},{96,80},{112,96},{1... | collective-permute-start | bytes 589832 | tf_op jit(solution)/shard_map/ppermute | solution.py:230
  20.9 1.4 %score.5 = (bf16[512,768]{1,0:T(8,128)(2,1)S(1)}, f32[1024,512]{1,0:T(8,128)S(1)}, f32[4,128]{1,0:T(4,128)S(1)}) custom-call(bf16[128,768]{1,0:T(8,128)(2,1)S(1)} %copy-done.2, bf16[128,768]{1,0:T(8,128)(2,1)S(1)} %collective-permute-done.refs_1_, bf16[128,768]{1,0:T(8,128)(2,1)S(1)} %collective-permute-done.1.refs_2_, ...), custom_call_target="tpu_custom_call" | custom-call | flops 805306368 | bytes 5249024 | tf_op jit(solution)/shard_map/score/pallas_call | solution.py:38
  22.3 2.3 %collective-permute-done.8.refs_2_ = bf16[128,768]{1,0:T(8,128)(2,1)S(1)} collective-permute-done((bf16[128,768]{1,0:T(8,128)(2,1)S(1)}, bf16[128,768]{1,0:T(8,128)(2,1)S(1)}, u32[]{:S(2)}, u32[]{:S(2)}) %collective-permute-start.8) | collective-permute-done | bytes 196640 | tf_op jit(solution)/shard_map/ppermute | solution.py:229
  24.6 3.2 %collective-permute-start.13 = (bf16[128,768]{1,0:T(8,128)(2,1)S(1)}, bf16[128,768]{1,0:T(8,128)(2,1)S(1)}, u32[]{:S(2)}, u32[]{:S(2)}) collective-permute-start(bf16[128,768]{1,0:T(8,128)(2,1)S(1)} %collective-permute-done.9.refs_3_), channel_id=1, source_target_pairs={{0,112},{16,0},{32,16},{48,32},{64,48},{80,64},{96,80},{112,96},{1... | collective-permute-start | bytes 589832 | tf_op jit(solution)/shard_map/ppermute | solution.py:230
  28.4 1.4 %score.6 = (bf16[512,768]{1,0:T(8,128)(2,1)S(1)}, f32[1024,512]{1,0:T(8,128)S(1)}, f32[4,128]{1,0:T(4,128)S(1)}) custom-call(bf16[128,768]{1,0:T(8,128)(2,1)S(1)} %collective-permute-done.6.refs_0_, bf16[128,768]{1,0:T(8,128)(2,1)S(1)} %collective-permute-done.7.refs_1_, bf16[128,768]{1,0:T(8,128)(2,1)S(1)} %collective-permute-done.8.refs_2_, ...), custom_call_target="tpu_custom_call" | custom-call | flops 805306368 | bytes 5249024 | tf_op jit(solution)/shard_map/score/pallas_call | solution.py:38
  29.8 2.8 %collective-permute-done.12.refs_2_ = bf16[128,768]{1,0:T(8,128)(2,1)S(1)} collective-permute-done((bf16[128,768]{1,0:T(8,128)(2,1)S(1)}, bf16[128,768]{1,0:T(8,128)(2,1)S(1)}, u32[]{:S(2)}, u32[]{:S(2)}) %collective-permute-start.12) | collective-permute-done | bytes 196640 | tf_op jit(solution)/shard_map/ppermute | solution.py:229
  33.1 3.0 %collective-permute-start.17 = (bf16[64,768]{1,0:T(8,128)(2,1)S(1)}, bf16[64,768]{1,0:T(8,128)(2,1)S(1)}, u32[]{:S(2)}, u32[]{:S(2)}) collective-permute-start(bf16[64,768]{1,0:T(8,128)(2,1)S(1)} %slice.15), channel_id=1, source_target_pairs={{0,112},{16,0},{32,16},{48,32},{64,48},{80,64},{96,80},{112,96},{1... | collective-permute-start | bytes 294920 | tf_op jit(solution)/shard_map/ppermute | solution.py:248
  36.1 1.4 %score.7 = (bf16[512,768]{1,0:T(8,128)(2,1)S(1)}, f32[1024,512]{1,0:T(8,128)S(1)}, f32[4,128]{1,0:T(4,128)S(1)}) custom-call(bf16[128,768]{1,0:T(8,128)(2,1)S(1)} %collective-permute-done.10.refs_0_, bf16[128,768]{1,0:T(8,128)(2,1)S(1)} %collective-permute-done.11.refs_1_, bf16[128,768]{1,0:T(8,128)(2,1)S(1)} %collective-permute-done.12.refs_2_, ...), custom_call_target="tpu_custom_call" | custom-call | flops 805306368 | bytes 5249024 | tf_op jit(solution)/shard_map/score/pallas_call | solution.py:38
  38.4 3.5 %collective-permute-done.16.refs_0_ = bf16[64,768]{1,0:T(8,128)(2,1)S(1)} collective-permute-done((bf16[64,768]{1,0:T(8,128)(2,1)S(1)}, bf16[64,768]{1,0:T(8,128)(2,1)S(1)}, u32[]{:S(2)}, u32[]{:S(2)}) %collective-permute-start.16) | collective-permute-done | bytes 98336 | tf_op jit(solution)/shard_map/ppermute | solution.py:247
  42.1 1.4 %collective-permute-done.18.refs_2_ = bf16[128,768]{1,0:T(8,128)(2,1)S(1)} collective-permute-done((bf16[128,768]{1,0:T(8,128)(2,1)S(1)}, bf16[128,768]{1,0:T(8,128)(2,1)S(1)}, u32[]{:S(2)}, u32[]{:S(2)}) %collective-permute-start.18) | collective-permute-done | bytes 196640 | tf_op jit(solution)/shard_map/ppermute | solution.py:33
  44.6 1.0 %collective-permute-done.19 = f32[16,128]{1,0:T(8,128)S(1)} collective-permute-done((f32[16,128]{1,0:T(8,128)S(1)}, f32[16,128]{1,0:T(8,128)S(1)}, u32[]{:S(2)}, u32[]{:S(2)}) %collective-permute-start.19) | collective-permute-done | bytes 8224 | tf_op jit(solution)/shard_map/ppermute | solution.py:33
  45.8 4.8 %collective-permute-done.20 = f32[16,128]{1,0:T(8,128)S(1)} collective-permute-done((f32[16,128]{1,0:T(8,128)S(1)}, f32[16,128]{1,0:T(8,128)S(1)}, u32[]{:S(2)}, u32[]{:S(2)}) %collective-permute-start.20) | collective-permute-done | bytes 8224 | tf_op jit(solution)/shard_map/ppermute | solution.py:264
  50.6 4.2 %collective-permute-start.23 = (f32[16,128]{1,0:T(8,128)S(1)}, f32[16,128]{1,0:T(8,128)S(1)}, u32[]{:S(2)}, u32[]{:S(2)}) collective-permute-start(f32[16,128]{1,0:T(8,128)S(1)} %log_add_fusion.1), channel_id=1, source_target_pairs={{0,64},{16,80},{32,96},{48,112},{64,0},{80,16},{96,32},{112,48},{1... | collective-permute-start | bytes 24584 | tf_op jit(solution)/shard_map/ppermute | solution.py:265
  54.8 2.9 %collective-permute-start.21 = (f32[16,128]{1,0:T(8,128)S(1)}, f32[16,128]{1,0:T(8,128)S(1)}, u32[]{:S(2)}, u32[]{:S(2)}) collective-permute-start(f32[16,128]{1,0:T(8,128)S(1)} %log_add_fusion.1), channel_id=1, source_target_pairs={{0,32},{16,48},{32,64},{48,80},{64,96},{80,112},{96,0},{112,16},{1... | collective-permute-start | bytes 24584 | tf_op jit(solution)/shard_map/ppermute | solution.py:265
  58.3 1.1 %collective-permute-done.22 = f32[16,128]{1,0:T(8,128)S(1)} collective-permute-done((f32[16,128]{1,0:T(8,128)S(1)}, f32[16,128]{1,0:T(8,128)S(1)}, u32[]{:S(2)}, u32[]{:S(2)}) %collective-permute-start.22) | collective-permute-done | bytes 8224 | tf_op jit(solution)/shard_map/ppermute | solution.py:265
  59.3 1.2 %collective-permute-done.21 = f32[16,128]{1,0:T(8,128)S(1)} collective-permute-done((f32[16,128]{1,0:T(8,128)S(1)}, f32[16,128]{1,0:T(8,128)S(1)}, u32[]{:S(2)}, u32[]{:S(2)}) %collective-permute-start.21) | collective-permute-done | bytes 8224 | tf_op jit(solution)/shard_map/ppermute | solution.py:265
  60.6 5.0 %spread.1 = (f32[16,392,128]{2,1,0:T(8,128)S(1)}, f32[1,128]{1,0:T(1,128)}) custom-call(f32[1024,512]{1,0:T(8,128)S(1)} %get-tuple-element.32.refs_0_, f32[1024,512]{1,0:T(8,128)S(1)} %get-tuple-element.36.refs_1_, f32[1024,512]{1,0:T(8,128)S(1)} %get-tuple-element.40.refs_2_, f32[1024,256]{1,0:T(8,128)S(1)} %get-tuple-element.41.refs_3_, ...), custom_call_target="tpu_custom_call" | custom-call | flops 3221225472 | bytes 14754304 | tf_op jit(solution)/shard_map/spread/pallas_call | solution.py:38
  65.8 27.3 %all_to_all.5 = f16[16,392,128]{2,1,0:T(8,128)(2,1)S(1)} all-to-all(f16[16,392,128]{2,1,0:T(8,128)(2,1)S(1)} %convert_element_type.6), channel_id=1, replica_groups=mesh['x_lo'=2,'z'=8,'core'=2,'y'=4,'x_hi'=2] {'x_lo','y','x_hi'}, dimensions={0} | all-to-all | bytes 3211264 | tf_op jit(solution)/shard_map/all_to_all | solution.py:279
  93.2 1.1 %update.1 = (f32[64,768]{1,0:T(8,128)}, f32[1,64]{1,0:T(1,128)}) custom-call(f32[16,392,128]{2,1,0:T(8,128)S(1)} %convert_element_type.7.came_ref, bf16[512,768]{1,0:T(8,128)(2,1)S(1)} %copy-done), custom_call_target="tpu_custom_call" | custom-call | bytes 4194560 | tf_op jit(solution)/shard_map/update/pallas_call | solution.py:38
  (49 shorter events, 7.8 us)
Async XLA Ops:
  1.9 17.2 %collective-permute-start.4 = (bf16[256,768]{1,0:T(8,128)(2,1)S(1)}, bf16[256,768]{1,0:T(8,128)(2,1)S(1)}, u32[]{:S(2)}, u32[]{:S(2)}) collective-permute-start(bf16[256,768]{1,0:T(8,128)(2,1)S(1)} %get-tuple-element.57), channel_id=1, source_target_pairs={{0,129},{128,0},{1,128},{129,1},{2,131},{130,2},{3,130},{131,3},{4... | collective-permute-start | bytes 1179656 | tf_op jit(solution)/shard_map/ppermute | solution.py:213
  4.7 14.6 %collective-permute-start.3 = (bf16[256,768]{1,0:T(8,128)(2,1)S(1)}, bf16[256,768]{1,0:T(8,128)(2,1)S(1)}, u32[]{:S(2)}, u32[]{:S(2)}) collective-permute-start(bf16[256,768]{1,0:T(8,128)(2,1)S(1)} %get-tuple-element.58), channel_id=1, source_target_pairs={{0,128},{128,1},{1,129},{129,0},{2,130},{130,3},{3,131},{131,2},{4... | collective-permute-start | bytes 1179656 | tf_op jit(solution)/shard_map/ppermute | solution.py:212
  4.7 10.7 %collective-permute-start.1 = (bf16[128,768]{1,0:T(8,128)(2,1)}, bf16[128,768]{1,0:T(8,128)(2,1)S(1)}, u32[]{:S(2)}, u32[]{:S(2)}) collective-permute-start(bf16[128,768]{1,0:T(8,128)(2,1)} %refs_0_.1), channel_id=1, source_target_pairs={{0,16},{16,32},{32,48},{48,64},{64,80},{80,96},{96,112},{112,0},{1... | collective-permute-start | bytes 589832 | tf_op jit(solution)/shard_map/ppermute | solution.py:229
  6.7 8.8 %collective-permute-start.2 = (bf16[128,768]{1,0:T(8,128)(2,1)}, bf16[128,768]{1,0:T(8,128)(2,1)S(1)}, u32[]{:S(2)}, u32[]{:S(2)}) collective-permute-start(bf16[128,768]{1,0:T(8,128)(2,1)} %refs_0_.1), channel_id=1, source_target_pairs={{0,112},{16,0},{32,16},{48,32},{64,48},{80,64},{96,80},{112,96},{1... | collective-permute-start | bytes 589832 | tf_op jit(solution)/shard_map/ppermute | solution.py:230
  10.6 3.8 %collective-permute-start.5 = (f32[1,512]{1,0:T(1,128)}, f32[1,512]{1,0:T(1,128)S(1)}, u32[]{:S(2)}, u32[]{:S(2)}) collective-permute-start(f32[1,512]{1,0:T(1,128)} %bitcast.3), channel_id=1, source_target_pairs={{0,128},{128,0},{1,129},{129,1},{2,130},{130,2},{3,131},{131,3},{4... | collective-permute-start | bytes 6152 | tf_op jit(solution)/shard_map/ppermute | solution.py:216
  14.4 6.5 %collective-permute-start = (bf16[128,768]{1,0:T(8,128)(2,1)}, bf16[128,768]{1,0:T(8,128)(2,1)S(1)}, u32[]{:S(2)}, u32[]{:S(2)}) collective-permute-start(bf16[128,768]{1,0:T(8,128)(2,1)} %refs_0_.1), channel_id=1, source_target_pairs={{0,8},{8,0},{1,9},{9,1},{2,10},{10,2},{3,11},{11,3},{4,12},{12,4},... | collective-permute-start | bytes 589832 | tf_op jit(solution)/shard_map/ppermute | solution.py:33
  15.4 9.2 %collective-permute-start.8 = (bf16[128,768]{1,0:T(8,128)(2,1)S(1)}, bf16[128,768]{1,0:T(8,128)(2,1)S(1)}, u32[]{:S(2)}, u32[]{:S(2)}) collective-permute-start(bf16[128,768]{1,0:T(8,128)(2,1)S(1)} %collective-permute-done.1.refs_2_), channel_id=1, source_target_pairs={{0,16},{16,32},{32,48},{48,64},{64,80},{80,96},{96,112},{112,0},{1... | collective-permute-start | bytes 589832 | tf_op jit(solution)/shard_map/ppermute | solution.py:229
  15.4 9.2 %collective-permute-start.9 = (bf16[128,768]{1,0:T(8,128)(2,1)S(1)}, bf16[128,768]{1,0:T(8,128)(2,1)S(1)}, u32[]{:S(2)}, u32[]{:S(2)}) collective-permute-start(bf16[128,768]{1,0:T(8,128)(2,1)S(1)} %collective-permute-done.2.refs_3_), channel_id=1, source_target_pairs={{0,112},{16,0},{32,16},{48,32},{64,48},{80,64},{96,80},{112,96},{1... | collective-permute-start | bytes 589832 | tf_op jit(solution)/shard_map/ppermute | solution.py:230
  19.1 8.7 %collective-permute-start.6 = (bf16[128,768]{1,0:T(8,128)(2,1)S(1)}, bf16[128,768]{1,0:T(8,128)(2,1)S(1)}, u32[]{:S(2)}, u32[]{:S(2)}) collective-permute-start(bf16[128,768]{1,0:T(8,128)(2,1)S(1)} %collective-permute-done.1.refs_2_), channel_id=1, source_target_pairs={{0,8},{8,0},{1,9},{9,1},{2,10},{10,2},{3,11},{11,3},{4,12},{12,4},... | collective-permute-start | bytes 589832 | tf_op jit(solution)/shard_map/ppermute | solution.py:33
  19.3 9.0 %collective-permute-start.7 = (bf16[128,768]{1,0:T(8,128)(2,1)S(1)}, bf16[128,768]{1,0:T(8,128)(2,1)S(1)}, u32[]{:S(2)}, u32[]{:S(2)}) collective-permute-start(bf16[128,768]{1,0:T(8,128)(2,1)S(1)} %collective-permute-done.2.refs_3_), channel_id=1, source_target_pairs={{0,8},{8,0},{1,9},{9,1},{2,10},{10,2},{3,11},{11,3},{4,12},{12,4},... | collective-permute-start | bytes 589832 | tf_op jit(solution)/shard_map/ppermute | solution.py:33
  24.6 7.9 %collective-permute-start.12 = (bf16[128,768]{1,0:T(8,128)(2,1)S(1)}, bf16[128,768]{1,0:T(8,128)(2,1)S(1)}, u32[]{:S(2)}, u32[]{:S(2)}) collective-permute-start(bf16[128,768]{1,0:T(8,128)(2,1)S(1)} %collective-permute-done.8.refs_2_), channel_id=1, source_target_pairs={{0,16},{16,32},{32,48},{48,64},{64,80},{80,96},{96,112},{112,0},{1... | collective-permute-start | bytes 589832 | tf_op jit(solution)/shard_map/ppermute | solution.py:229
  24.6 7.9 %collective-permute-start.13 = (bf16[128,768]{1,0:T(8,128)(2,1)S(1)}, bf16[128,768]{1,0:T(8,128)(2,1)S(1)}, u32[]{:S(2)}, u32[]{:S(2)}) collective-permute-start(bf16[128,768]{1,0:T(8,128)(2,1)S(1)} %collective-permute-done.9.refs_3_), channel_id=1, source_target_pairs={{0,112},{16,0},{32,16},{48,32},{64,48},{80,64},{96,80},{112,96},{1... | collective-permute-start | bytes 589832 | tf_op jit(solution)/shard_map/ppermute | solution.py:230
  27.8 8.3 %collective-permute-start.10 = (bf16[128,768]{1,0:T(8,128)(2,1)S(1)}, bf16[128,768]{1,0:T(8,128)(2,1)S(1)}, u32[]{:S(2)}, u32[]{:S(2)}) collective-permute-start(bf16[128,768]{1,0:T(8,128)(2,1)S(1)} %collective-permute-done.8.refs_2_), channel_id=1, source_target_pairs={{0,8},{8,0},{1,9},{9,1},{2,10},{10,2},{3,11},{11,3},{4,12},{12,4},... | collective-permute-start | bytes 589832 | tf_op jit(solution)/shard_map/ppermute | solution.py:33
  27.8 8.3 %collective-permute-start.11 = (bf16[128,768]{1,0:T(8,128)(2,1)S(1)}, bf16[128,768]{1,0:T(8,128)(2,1)S(1)}, u32[]{:S(2)}, u32[]{:S(2)}) collective-permute-start(bf16[128,768]{1,0:T(8,128)(2,1)S(1)} %collective-permute-done.9.refs_3_), channel_id=1, source_target_pairs={{0,8},{8,0},{1,9},{9,1},{2,10},{10,2},{3,11},{11,3},{4,12},{12,4},... | collective-permute-start | bytes 589832 | tf_op jit(solution)/shard_map/ppermute | solution.py:33
  32.5 5.0 %collective-permute-start.14 = (bf16[128,768]{1,0:T(8,128)(2,1)S(1)}, bf16[128,768]{1,0:T(8,128)(2,1)S(1)}, u32[]{:S(2)}, u32[]{:S(2)}) collective-permute-start(bf16[128,768]{1,0:T(8,128)(2,1)S(1)} %collective-permute-done.12.refs_2_), channel_id=1, source_target_pairs={{0,8},{8,0},{1,9},{9,1},{2,10},{10,2},{3,11},{11,3},{4,12},{12,4},... | collective-permute-start | bytes 589832 | tf_op jit(solution)/shard_map/ppermute | solution.py:33
  32.6 5.0 %collective-permute-start.15 = (bf16[128,768]{1,0:T(8,128)(2,1)S(1)}, bf16[128,768]{1,0:T(8,128)(2,1)S(1)}, u32[]{:S(2)}, u32[]{:S(2)}) collective-permute-start(bf16[128,768]{1,0:T(8,128)(2,1)S(1)} %collective-permute-done.13.refs_3_), channel_id=1, source_target_pairs={{0,8},{8,0},{1,9},{9,1},{2,10},{10,2},{3,11},{11,3},{4,12},{12,4},... | collective-permute-start | bytes 589832 | tf_op jit(solution)/shard_map/ppermute | solution.py:33
  33.1 5.3 %collective-permute-start.17 = (bf16[64,768]{1,0:T(8,128)(2,1)S(1)}, bf16[64,768]{1,0:T(8,128)(2,1)S(1)}, u32[]{:S(2)}, u32[]{:S(2)}) collective-permute-start(bf16[64,768]{1,0:T(8,128)(2,1)S(1)} %slice.15), channel_id=1, source_target_pairs={{0,112},{16,0},{32,16},{48,32},{64,48},{80,64},{96,80},{112,96},{1... | collective-permute-start | bytes 294920 | tf_op jit(solution)/shard_map/ppermute | solution.py:248
  36.1 5.8 %collective-permute-start.16 = (bf16[64,768]{1,0:T(8,128)(2,1)S(1)}, bf16[64,768]{1,0:T(8,128)(2,1)S(1)}, u32[]{:S(2)}, u32[]{:S(2)}) collective-permute-start(bf16[64,768]{1,0:T(8,128)(2,1)S(1)} %slice.14), channel_id=1, source_target_pairs={{0,16},{16,32},{32,48},{48,64},{64,80},{80,96},{96,112},{112,0},{1... | collective-permute-start | bytes 294920 | tf_op jit(solution)/shard_map/ppermute | solution.py:247
  42.0 1.5 %collective-permute-start.18 = (bf16[128,768]{1,0:T(8,128)(2,1)S(1)}, bf16[128,768]{1,0:T(8,128)(2,1)S(1)}, u32[]{:S(2)}, u32[]{:S(2)}) collective-permute-start(bf16[128,768]{1,0:T(8,128)(2,1)S(1)} %pad_maximum_fusion), channel_id=1, source_target_pairs={{0,8},{8,0},{1,9},{9,1},{2,10},{10,2},{3,11},{11,3},{4,12},{12,4},... | collective-permute-start | bytes 589832 | tf_op jit(solution)/shard_map/ppermute | solution.py:33
  44.4 1.3 %collective-permute-start.19 = (f32[16,128]{1,0:T(8,128)S(1)}, f32[16,128]{1,0:T(8,128)S(1)}, u32[]{:S(2)}, u32[]{:S(2)}) collective-permute-start(f32[16,128]{1,0:T(8,128)S(1)} %row_table.1), channel_id=1, source_target_pairs={{0,8},{8,0},{1,9},{9,1},{2,10},{10,2},{3,11},{11,3},{4,12},{12,4},... | collective-permute-start | bytes 24584 | tf_op jit(solution)/shard_map/ppermute | solution.py:33
  45.7 4.9 %collective-permute-start.20 = (f32[16,128]{1,0:T(8,128)S(1)}, f32[16,128]{1,0:T(8,128)S(1)}, u32[]{:S(2)}, u32[]{:S(2)}) collective-permute-start(f32[16,128]{1,0:T(8,128)S(1)} %log_add_fusion.2), channel_id=1, source_target_pairs={{0,16},{16,32},{32,48},{48,64},{64,80},{80,96},{96,112},{112,0},{1... | collective-permute-start | bytes 24584 | tf_op jit(solution)/shard_map/ppermute | solution.py:264
  50.6 7.6 %collective-permute-start.23 = (f32[16,128]{1,0:T(8,128)S(1)}, f32[16,128]{1,0:T(8,128)S(1)}, u32[]{:S(2)}, u32[]{:S(2)}) collective-permute-start(f32[16,128]{1,0:T(8,128)S(1)} %log_add_fusion.1), channel_id=1, source_target_pairs={{0,64},{16,80},{32,96},{48,112},{64,0},{80,16},{96,32},{112,48},{1... | collective-permute-start | bytes 24584 | tf_op jit(solution)/shard_map/ppermute | solution.py:265
  54.8 4.5 %collective-permute-start.22 = (f32[16,128]{1,0:T(8,128)S(1)}, f32[16,128]{1,0:T(8,128)S(1)}, u32[]{:S(2)}, u32[]{:S(2)}) collective-permute-start(f32[16,128]{1,0:T(8,128)S(1)} %log_add_fusion.1), channel_id=1, source_target_pairs={{0,96},{16,112},{32,0},{48,16},{64,32},{80,48},{96,64},{112,80},{1... | collective-permute-start | bytes 24584 | tf_op jit(solution)/shard_map/ppermute | solution.py:265
  54.8 5.8 %collective-permute-start.21 = (f32[16,128]{1,0:T(8,128)S(1)}, f32[16,128]{1,0:T(8,128)S(1)}, u32[]{:S(2)}, u32[]{:S(2)}) collective-permute-start(f32[16,128]{1,0:T(8,128)S(1)} %log_add_fusion.1), channel_id=1, source_target_pairs={{0,32},{16,48},{32,64},{48,80},{64,96},{80,112},{96,0},{112,16},{1... | collective-permute-start | bytes 24584 | tf_op jit(solution)/shard_map/ppermute | solution.py:265
  (3 other events, 40.0 us)

commit v3 on v2

--- a/solution.py
+++ b/solution.py
@@ -12,9 +12,8 @@
 prior_mass = 1.0
 
 AXES = ("x_lo", "z", "core", "y", "x_hi")
-XS = ("x_lo", "x_hi")
 OWNERS = ("x_lo", "y", "x_hi")
-NZ, NX, N_OWNERS = 8, 4, 16
+NZ, N_OWNERS = 8, 16
 LANES = 128
 VMEM = pl.BlockSpec(memory_space=pltpu.VMEM)
 EXTRA = 8
@@ -24,17 +23,12 @@
     return [(i, (i + step) % NZ) for i in range(NZ)]
 
 
-def along_x(step):
-    place = [(x % 2) * 2 + x // 2 for x in range(NX)]
-    return [(place[x], place[(x + step) % NX]) for x in range(NX)]
-
-
 def other_core(array):
     return lax.ppermute(array, "core", [(0, 1), (1, 0)])
 
 
-def call(kernel, outs, args, name, flops=0, transcendentals=0, vmem=24):
-    size = sum(a.size * a.dtype.itemsize for a in (*args, *outs))
+def call(kernel, outs, args, name, flops=0, transcendentals=0, share=1, vmem=24):
+    size = sum(a.size * a.dtype.itemsize for a in (*args, *outs)) // share
     return pl.pallas_call(
         kernel,
         out_shape=outs,
@@ -42,7 +36,7 @@
         out_specs=(VMEM,) * len(outs),
         compiler_params=pltpu.CompilerParams(vmem_limit_bytes=vmem * 1024 * 1024),
         cost_estimate=pl.CostEstimate(
-            flops=flops, bytes_accessed=size, transcendentals=transcendentals
+            flops=flops // share, bytes_accessed=size, transcendentals=transcendentals // share
         ),
         name=name,
     )(*args)
@@ -59,16 +53,18 @@
     )
 
 
-def centroid_kernel(scale_root, mine_ref, up_ref, down_ref, weight_ref, beside_ref, cent_ref, bias_ref):
+def centroid_kernel(scale_root, mine_ref, weight_ref, other_ref, other_weight_ref, cent_ref, bias_ref):
     n = mine_ref.shape[0]
     x_lo = lax.axis_index("x_lo")
-    first, second = pl.multiple_of(x_lo * n, n), pl.multiple_of((1 - x_lo) * n, n)
-    beside = jnp.concatenate([up_ref[...], down_ref[...]])
-    for at, block, weight in ((first, mine_ref[...], weight_ref), (second, beside, beside_ref)):
-        cent_ref[pl.ds(at, n), :] = block
-        wide = block.astype(jnp.float32)
+    for at, block_ref, row_ref in (
+        (x_lo, mine_ref, weight_ref),
+        (1 - x_lo, other_ref, other_weight_ref),
+    ):
+        here = pl.ds(pl.multiple_of(at * n, n), n)
+        cent_ref[here, :] = block_ref[...]
+        wide = block_ref[...].astype(jnp.float32)
         half_sq = 0.5 * jnp.sum(wide * wide, axis=1, keepdims=True)
-        bias_ref[pl.ds(at, n), :] = column(weight[...]) - half_sq * (1.0 / scale_root)
+        bias_ref[here, :] = column(row_ref[...]) - half_sq * (1.0 / scale_root)
 
 
 def row_of(step):
@@ -113,6 +109,7 @@
         "score",
         2 * n_cent * count * depth,
         n_cent * count,
+        4,
     )
 
 
@@ -204,65 +201,62 @@
     local_count, feat_dim = centroids.shape
     n_rows = embeddings.shape[0]
     scale_root = math.sqrt(feat_dim)
-    half = local_count // 2
     owned = local_count // 8
 
+    up = lax.ppermute(embeddings, "z", along_z(1))
+    down = lax.ppermute(embeddings, "z", along_z(-1))
     other = other_core(embeddings)
-    beside = (
-        lax.ppermute(centroids[:half], XS, along_x(1)),
-        lax.ppermute(centroids[half:], XS, along_x(-1)),
-    )
+    beside = lax.ppermute(centroids, "x_lo", [(0, 1), (1, 0)])
     weight = log_weight[None, :]
     weight_beside = lax.ppermute(weight, "x_lo", [(0, 1), (1, 0)])
-    cents, bias = call(
-        functools.partial(centroid_kernel, scale_root),
-        (shape((2 * local_count, feat_dim), jnp.bfloat16), shape((2 * local_count, 1))),
-        (centroids, *beside, weight, weight_beside),
-        "centroid_blocks",
-        4 * local_count * feat_dim,
-    )
-
-    waiting, order = [embeddings, other], [(0, 0), (0, 1)]
-    orders, scored = [], []
-    up = down = embeddings
-    for step in range(1, 4):
-        up = lax.ppermute(up, "z", along_z(1))
-        down = lax.ppermute(down, "z", along_z(-1))
-        if step > 1:
-            scored.append(score(waiting, cents, bias, scale_root))
-            orders.append(order)
-            up, down, _ = lax.optimization_barrier((up, down, scored[-1][2]))
-            waiting, order = [], []
-        if step == 2:
-            waiting += swapped
-            order += [(NZ - 1, 1), (1, 1)]
-        if step == 3:
-            waiting += swapped
-            order += [(NZ - 2, 1), (2, 1)]
-        waiting += [up, down]
-        order += [(NZ - step, 0), (step, 0)]
-        swapped = [other_core(up), other_core(down)]
+
+    def blocks(after):
+        beside_now, weight_now, _ = lax.optimization_barrier((beside, weight_beside, after))
+        return call(
+            functools.partial(centroid_kernel, scale_root),
+            (shape((2 * local_count, feat_dim), jnp.bfloat16), shape((2 * local_count, 1))),
+            (centroids, weight, beside_now, weight_now),
+            "centroid_blocks",
+            4 * local_count * feat_dim,
+            share=4,
+        )
+
+    scored, orders = [], []
+
+    def scores(order, *parts):
+        scored.append(score(parts, cents, bias, scale_root))
+        orders.append(order)
+        return scored[-1][2]
+
+    def moved(first, second):
+        return lax.ppermute(first, "z", along_z(1)), lax.ppermute(second, "z", along_z(-1))
+
+    def both(step):
+        return [(NZ - step, 0), (step, 0), (NZ - step, 1), (step, 1)]
+
     piece = n_rows // 2
-    far = [
-        lax.ppermute(up[:piece], "z", along_z(1)),
-        lax.ppermute(down[piece:], "z", along_z(-1)),
-    ]
-    scored.append(score(waiting, cents, bias, scale_root))
-    orders.append(order)
-    scored.append(score(swapped, cents, bias, scale_root))
-    orders.append([(NZ - 3, 1), (3, 1)])
-    far = lax.optimization_barrier((*far, scored[-2][2], scored[-1][2]))[:2]
-    far_other = other_core(jnp.concatenate(far))
-    scored.append(score([*far, far_other], cents, bias, scale_root))
-    orders.append([(4, 0), (4, 1)])
+    came = [[embeddings, other, up, down, other_core(up), other_core(down)]]
+    for _ in range(2):
+        up, down = moved(up, down)
+        came.append([up, down, other_core(up), other_core(down)])
+        if len(came) == 2:
+            cents, bias = blocks(up)
+    up, down = moved(up[:piece], down[piece:])
+    done = (
+        scores([(0, 0), (0, 1), *both(1)], *came[0]),
+        scores(both(2), *came[1]),
+        scores(both(3), *came[2]),
+    )
+    up, down, _ = lax.optimization_barrier((up, down, done))
+    scores([(4, 0), (4, 1)], up, down, other_core(jnp.concatenate([up, down])))
     rows, logits, lses = zip(*scored)
 
     (table,) = call(
         functools.partial(table_kernel, orders), (shape((2 * NZ, LANES)),), lses, "row_table"
     )
     table = joined(table, other_core(table))
-    table = joined(table, lax.ppermute(table, "z", along_z(1)))
-    table = joined(table, *(lax.ppermute(table, "z", along_z(s)) for s in (2, -2, 4)))
+    tables = jnp.broadcast_to(table, (NZ, *table.shape))
+    table = joined(*lax.all_to_all(tables, "z", 0, 0, tiled=True))
 
     n_all = 2 * NZ * n_rows
     packed, log_norm = call(

time: 94.6 us -> 91.9 us (0.971)
  blocking collectives: 27.3 us -> 41.9 us
  waiting for transfers between devices: 22.8 us -> 13 us
  starting transfers between devices: 28.4 us -> 20.5 us
    all_to_all x0 -> x1, blocking collectives: none -> 13.6 us  [local(): table = joined(*lax.all_to_all(tables, 'z', 0, 0, tiled=True))]
    ppermute x14 -> x9, waiting for transfers between devices: 17.3 us -> 7.61 us  [the longest x3 4.06 us: moved(): lax.ppermute(first, 'z', along_z(1))]
    ppermute x14 -> x9, starting transfers between devices: 25.8 us -> 17.3 us  [the longest x3 9.69 us: moved(): lax.ppermute(second, 'z', along_z(-1))]
    unnamed x6 -> x8, local copies, waits for them, and re-layouts: 0.69 us -> 2.74 us
    slice x3 -> x2, local copies, waits for them, and re-layouts: 1.26 us -> 0.01 us  [local(): up, down = moved(up[:piece], down[piece:])]
    all_to_all x1, blocking collectives: 27.3 us -> 28.4 us  [local(): came = lax.all_to_all(packed.astype(jnp.float16), OWNERS, 0, 0, tiled=True)]
    pallas_call x9 -> x8, Pallas kernels: 12.6 us -> 12.3 us  [call(): pl.pallas_call(kernel, out_shape=outs, in_specs=[VMEM] * len(args), out_s...]
  transfers between devices with their start and end apart: 24 -> 19, of which waited for: 11 -> 7; matrix products, arithmetic and copies ran while one was open for 0% -> 0% of each run, Pallas kernels for 6% -> 6%
where the time goes in v3:
time: 91.9 us; the launch traced here: 91.7 us
  blocking collectives  41.9 us (46%)
  starting transfers between devices  20.5 us (22%)
  waiting for transfers between devices  13 us (14%)
  Pallas kernels  12.3 us (13%)
  local copies, waits for them, and re-layouts  2.76 us (3%)
    all_to_all x1, blocking collectives, local(): came = lax.all_to_all(packed.astype(jnp.float16), OWNERS, 0, 0, tiled=True)  28.4 us
    all_to_all x1, blocking collectives, local(): table = joined(*lax.all_to_all(tables, 'z', 0, 0, tiled=True))  13.6 us
    pallas_call x8, Pallas kernels, call(): pl.pallas_call(kernel, out_shape=outs, in_specs=[VMEM] * len(args), out_s...  12.3 us
    ppermute x3, starting transfers between devices, moved(): lax.ppermute(second, 'z', along_z(-1))  9.69 us
    ppermute x3, waiting for transfers between devices, moved(): lax.ppermute(first, 'z', along_z(1))  4.06 us
    ppermute x1, starting transfers between devices, local(): down = lax.ppermute(embeddings, 'z', along_z(-1))  4.03 us
    ppermute x1, waiting for transfers between devices, local(): up = lax.ppermute(embeddings, 'z', along_z(1))  3.53 us
    ppermute x9, waiting for transfers between devices, other_core(): return lax.ppermute(array, 'core', [(0, 1), (1, 0)])  3.05 us
  transfers between devices with their start and end apart: 19, of which 7 were waited for; matrix products, arithmetic and copies ran while one was open for 0% of the time, Pallas kernels for 6%

profile of v3, /device:TPU:8, one launch (start us, length us, event | category | flops | bytes accessed | tf_op | source)
XLA Modules:
  0.0 91.7 jit_solution(7247653570509004834)
XLA Ops:
  0.6 2.0 %collective-permute-start.1 = (bf16[128,768]{1,0:T(8,128)(2,1)}, bf16[128,768]{1,0:T(8,128)(2,1)S(1)}, u32[]{:S(2)}, u32[]{:S(2)}) collective-permute-start(bf16[128,768]{1,0:T(8,128)(2,1)} %refs_0_.1), channel_id=1, source_target_pairs={{0,16},{16,32},{32,48},{48,64},{64,80},{80,96},{96,112},{112,0},{1... | collective-permute-start | bytes 589832 | tf_op jit(solution)/shard_map/ppermute | solution.py:206
  2.6 4.0 %collective-permute-start.2 = (bf16[128,768]{1,0:T(8,128)(2,1)}, bf16[128,768]{1,0:T(8,128)(2,1)S(1)}, u32[]{:S(2)}, u32[]{:S(2)}) collective-permute-start(bf16[128,768]{1,0:T(8,128)(2,1)} %refs_0_.1), channel_id=1, source_target_pairs={{0,112},{16,0},{32,16},{48,32},{64,48},{80,64},{96,80},{112,96},{1... | collective-permute-start | bytes 589832 | tf_op jit(solution)/shard_map/ppermute | solution.py:207
  6.7 1.5 %collective-permute-start.5 = (bf16[512,768]{1,0:T(8,128)(2,1)}, bf16[512,768]{1,0:T(8,128)(2,1)S(1)}, u32[]{:S(2)}, u32[]{:S(2)}) collective-permute-start(bf16[512,768]{1,0:T(8,128)(2,1)} %cent_ref.1), channel_id=1, source_target_pairs={{0,128},{128,0},{1,129},{129,1},{2,130},{130,2},{3,131},{131,3},{4... | collective-permute-start | bytes 2359304 | tf_op jit(solution)/shard_map/ppermute | solution.py:209
  8.1 3.5 %collective-permute-done.1.refs_2_ = bf16[128,768]{1,0:T(8,128)(2,1)S(1)} collective-permute-done((bf16[128,768]{1,0:T(8,128)(2,1)}, bf16[128,768]{1,0:T(8,128)(2,1)S(1)}, u32[]{:S(2)}, u32[]{:S(2)}) %collective-permute-start.1) | collective-permute-done | bytes 196640 | tf_op jit(solution)/shard_map/ppermute | solution.py:206
  11.7 3.2 %collective-permute-start.8 = (bf16[128,768]{1,0:T(8,128)(2,1)S(1)}, bf16[128,768]{1,0:T(8,128)(2,1)S(1)}, u32[]{:S(2)}, u32[]{:S(2)}) collective-permute-start(bf16[128,768]{1,0:T(8,128)(2,1)S(1)} %collective-permute-done.2.refs_3_), channel_id=1, source_target_pairs={{0,112},{16,0},{32,16},{48,32},{64,48},{80,64},{96,80},{112,96},{1... | collective-permute-start | bytes 589832 | tf_op jit(solution)/shard_map/ppermute | solution.py:232
  14.9 4.1 %collective-permute-done.7.refs_0_ = bf16[128,768]{1,0:T(8,128)(2,1)S(1)} collective-permute-done((bf16[128,768]{1,0:T(8,128)(2,1)S(1)}, bf16[128,768]{1,0:T(8,128)(2,1)S(1)}, u32[]{:S(2)}, u32[]{:S(2)}) %collective-permute-start.7) | collective-permute-done | bytes 196640 | tf_op jit(solution)/shard_map/ppermute | solution.py:232
  19.0 3.2 %collective-permute-start.12 = (bf16[128,768]{1,0:T(8,128)(2,1)S(1)}, bf16[128,768]{1,0:T(8,128)(2,1)S(1)}, u32[]{:S(2)}, u32[]{:S(2)}) collective-permute-start(bf16[128,768]{1,0:T(8,128)(2,1)S(1)} %collective-permute-done.8.refs_1_), channel_id=1, source_target_pairs={{0,112},{16,0},{32,16},{48,32},{64,48},{80,64},{96,80},{112,96},{1... | collective-permute-start | bytes 589832 | tf_op jit(solution)/shard_map/ppermute | solution.py:232
  22.2 1.5 %collective-permute-start.6 = (f32[1,512]{1,0:T(1,128)}, f32[1,512]{1,0:T(1,128)S(1)}, u32[]{:S(2)}, u32[]{:S(2)}) collective-permute-start(f32[1,512]{1,0:T(1,128)} %bitcast.35), channel_id=1, source_target_pairs={{0,128},{128,0},{1,129},{129,1},{2,130},{130,2},{3,131},{131,3},{4... | collective-permute-start | bytes 6152 | tf_op jit(solution)/shard_map/ppermute | solution.py:211
  23.7 2.3 %collective-permute-done.6.other_weight_ref = f32[1,512]{1,0:T(1,128)S(1)} collective-permute-done((f32[1,512]{1,0:T(1,128)}, f32[1,512]{1,0:T(1,128)S(1)}, u32[]{:S(2)}, u32[]{:S(2)}) %collective-permute-start.6) | collective-permute-done | bytes 2080 | tf_op jit(solution)/shard_map/ppermute | solution.py:211
  28.1 3.2 %collective-permute-start.16 = (bf16[64,768]{1,0:T(8,128)(2,1)S(1)}, bf16[64,768]{1,0:T(8,128)(2,1)S(1)}, u32[]{:S(2)}, u32[]{:S(2)}) collective-permute-start(bf16[64,768]{1,0:T(8,128)(2,1)S(1)} %slice.9), channel_id=1, source_target_pairs={{0,112},{16,0},{32,16},{48,32},{64,48},{80,64},{96,80},{112,96},{1... | collective-permute-start | bytes 294920 | tf_op jit(solution)/shard_map/ppermute | solution.py:232
  31.3 1.1 %copy-done = bf16[512,768]{1,0:T(8,128)(2,1)S(1)} copy-done((bf16[512,768]{1,0:T(8,128)(2,1)S(1)}, bf16[512,768]{1,0:T(8,128)(2,1)}, u32[]{:S(2)}) %copy-start) | copy-done | bytes 786456
  32.5 0.7 copy-done.3
  33.1 0.5 centroid_blocks.1
  33.7 1.4 %score.6 = (bf16[512,768]{1,0:T(8,128)(2,1)S(1)}, f32[1024,512]{1,0:T(8,128)S(1)}, f32[4,128]{1,0:T(4,128)S(1)}) custom-call(bf16[128,768]{1,0:T(8,128)(2,1)S(1)} %collective-permute-done.11.refs_0_, bf16[128,768]{1,0:T(8,128)(2,1)S(1)} %collective-permute-done.12.refs_1_, bf16[128,768]{1,0:T(8,128)(2,1)S(1)} %collective-permute-done.13.refs_2_, ...), custom_call_target="tpu_custom_call" | custom-call | flops 201326592 | bytes 1312256 | tf_op jit(solution)/shard_map/score/pallas_call | solution.py:32
  35.1 1.4 %score.5 = (bf16[512,768]{1,0:T(8,128)(2,1)S(1)}, f32[1024,512]{1,0:T(8,128)S(1)}, f32[4,128]{1,0:T(4,128)S(1)}) custom-call(bf16[128,768]{1,0:T(8,128)(2,1)S(1)} %collective-permute-done.7.refs_0_, bf16[128,768]{1,0:T(8,128)(2,1)S(1)} %collective-permute-done.8.refs_1_, bf16[128,768]{1,0:T(8,128)(2,1)S(1)} %collective-permute-done.9.refs_2_, ...), custom_call_target="tpu_custom_call" | custom-call | flops 201326592 | bytes 1312256 | tf_op jit(solution)/shard_map/score/pallas_call | solution.py:32
  36.5 1.9 %score.4 = (bf16[768,768]{1,0:T(8,128)(2,1)S(1)}, f32[1024,768]{1,0:T(8,128)S(1)}, f32[6,128]{1,0:T(8,128)S(1)}) custom-call(bf16[128,768]{1,0:T(8,128)(2,1)S(1)} %copy-done.2, bf16[128,768]{1,0:T(8,128)(2,1)S(1)} %collective-permute-done.refs_1_, bf16[128,768]{1,0:T(8,128)(2,1)S(1)} %collective-permute-done.1.refs_2_, ...), custom_call_target="tpu_custom_call" | custom-call | flops 301989888 | bytes 1771264 | tf_op jit(solution)/shard_map/score/pallas_call | solution.py:32
  38.6 1.4 %collective-permute-done.17.refs_2_ = bf16[128,768]{1,0:T(8,128)(2,1)S(1)} collective-permute-done((bf16[128,768]{1,0:T(8,128)(2,1)S(1)}, bf16[128,768]{1,0:T(8,128)(2,1)S(1)}, u32[]{:S(2)}, u32[]{:S(2)}) %collective-permute-start.17) | collective-permute-done | bytes 196640 | tf_op jit(solution)/shard_map/ppermute | solution.py:27
  40.0 0.8 score.7
  41.2 1.0 %collective-permute-done.18 = f32[16,128]{1,0:T(8,128)S(1)} collective-permute-done((f32[16,128]{1,0:T(8,128)S(1)}, f32[16,128]{1,0:T(8,128)S(1)}, u32[]{:S(2)}, u32[]{:S(2)}) %collective-permute-start.18) | collective-permute-done | bytes 8224 | tf_op jit(solution)/shard_map/ppermute | solution.py:27
  42.2 13.6 %all_to_all.10 = f32[8,16,128]{2,1,0:T(8,128)S(1)} all-to-all(f32[8,16,128]{2,1,0:T(8,128)S(1)} %broadcast_in_dim.7), channel_id=1, replica_groups=mesh['x_lo'=2,'z'=8,'core'=2,'y'=4,'x_hi'=2] {'z'}, dimensions={0} | all-to-all | bytes 131072 | tf_op jit(solution)/shard_map/all_to_all | solution.py:259
  55.8 5.0 %spread.1 = (f32[16,392,128]{2,1,0:T(8,128)S(1)}, f32[1,128]{1,0:T(1,128)}) custom-call(f32[1024,768]{1,0:T(8,128)S(1)} %get-tuple-element.29.refs_0_, f32[1024,512]{1,0:T(8,128)S(1)} %get-tuple-element.30.refs_1_, f32[1024,512]{1,0:T(8,128)S(1)} %get-tuple-element.31.refs_2_, f32[1024,256]{1,0:T(8,128)S(1)} %get-tuple-element.37.refs_3_, ...), custom_call_target="tpu_custom_call" | custom-call | flops 3221225472 | bytes 14754304 | tf_op jit(solution)/shard_map/spread/pallas_call | solution.py:32
  61.0 28.4 %all_to_all.11 = f16[16,392,128]{2,1,0:T(8,128)(2,1)S(1)} all-to-all(f16[16,392,128]{2,1,0:T(8,128)(2,1)S(1)} %convert_element_type.6), channel_id=1, replica_groups=mesh['x_lo'=2,'z'=8,'core'=2,'y'=4,'x_hi'=2] {'x_lo','y','x_hi'}, dimensions={0} | all-to-all | bytes 3211264 | tf_op jit(solution)/shard_map/all_to_all | solution.py:273
  89.6 0.9 %copy-done.1 = bf16[512,768]{1,0:T(8,128)(2,1)S(1)} copy-done((bf16[512,768]{1,0:T(8,128)(2,1)S(1)}, bf16[512,768]{1,0:T(8,128)(2,1)}, u32[]{:S(2)}) %copy-start.1) | copy-done | bytes 786456
  90.6 1.1 %update.1 = (f32[64,768]{1,0:T(8,128)}, f32[1,64]{1,0:T(1,128)}) custom-call(f32[16,392,128]{2,1,0:T(8,128)S(1)} %convert_element_type.7.came_ref, bf16[512,768]{1,0:T(8,128)(2,1)S(1)} %copy-done.1), custom_call_target="tpu_custom_call" | custom-call | bytes 4194560 | tf_op jit(solution)/shard_map/update/pallas_call | solution.py:32
  (40 shorter events, 2.9 us)
Async XLA Ops:
  0.6 11.0 %collective-permute-start.1 = (bf16[128,768]{1,0:T(8,128)(2,1)}, bf16[128,768]{1,0:T(8,128)(2,1)S(1)}, u32[]{:S(2)}, u32[]{:S(2)}) collective-permute-start(bf16[128,768]{1,0:T(8,128)(2,1)} %refs_0_.1), channel_id=1, source_target_pairs={{0,16},{16,32},{32,48},{48,64},{64,80},{80,96},{96,112},{112,0},{1... | collective-permute-start | bytes 589832 | tf_op jit(solution)/shard_map/ppermute | solution.py:206
  2.6 9.1 %collective-permute-start.2 = (bf16[128,768]{1,0:T(8,128)(2,1)}, bf16[128,768]{1,0:T(8,128)(2,1)S(1)}, u32[]{:S(2)}, u32[]{:S(2)}) collective-permute-start(bf16[128,768]{1,0:T(8,128)(2,1)} %refs_0_.1), channel_id=1, source_target_pairs={{0,112},{16,0},{32,16},{48,32},{64,48},{80,64},{96,80},{112,96},{1... | collective-permute-start | bytes 589832 | tf_op jit(solution)/shard_map/ppermute | solution.py:207
  6.7 21.4 %collective-permute-start.5 = (bf16[512,768]{1,0:T(8,128)(2,1)}, bf16[512,768]{1,0:T(8,128)(2,1)S(1)}, u32[]{:S(2)}, u32[]{:S(2)}) collective-permute-start(bf16[512,768]{1,0:T(8,128)(2,1)} %cent_ref.1), channel_id=1, source_target_pairs={{0,128},{128,0},{1,129},{129,1},{2,130},{130,2},{3,131},{131,3},{4... | collective-permute-start | bytes 2359304 | tf_op jit(solution)/shard_map/ppermute | solution.py:209
  11.7 7.3 %collective-permute-start.7 = (bf16[128,768]{1,0:T(8,128)(2,1)S(1)}, bf16[128,768]{1,0:T(8,128)(2,1)S(1)}, u32[]{:S(2)}, u32[]{:S(2)}) collective-permute-start(bf16[128,768]{1,0:T(8,128)(2,1)S(1)} %collective-permute-done.1.refs_2_), channel_id=1, source_target_pairs={{0,16},{16,32},{32,48},{48,64},{64,80},{80,96},{96,112},{112,0},{1... | collective-permute-start | bytes 589832 | tf_op jit(solution)/shard_map/ppermute | solution.py:232
  11.7 7.3 %collective-permute-start.8 = (bf16[128,768]{1,0:T(8,128)(2,1)S(1)}, bf16[128,768]{1,0:T(8,128)(2,1)S(1)}, u32[]{:S(2)}, u32[]{:S(2)}) collective-permute-start(bf16[128,768]{1,0:T(8,128)(2,1)S(1)} %collective-permute-done.2.refs_3_), channel_id=1, source_target_pairs={{0,112},{16,0},{32,16},{48,32},{64,48},{80,64},{96,80},{112,96},{1... | collective-permute-start | bytes 589832 | tf_op jit(solution)/shard_map/ppermute | solution.py:232
  19.0 7.0 %collective-permute-start.11 = (bf16[128,768]{1,0:T(8,128)(2,1)S(1)}, bf16[128,768]{1,0:T(8,128)(2,1)S(1)}, u32[]{:S(2)}, u32[]{:S(2)}) collective-permute-start(bf16[128,768]{1,0:T(8,128)(2,1)S(1)} %collective-permute-done.7.refs_0_), channel_id=1, source_target_pairs={{0,16},{16,32},{32,48},{48,64},{64,80},{80,96},{96,112},{112,0},{1... | collective-permute-start | bytes 589832 | tf_op jit(solution)/shard_map/ppermute | solution.py:232
  19.0 7.5 %collective-permute-start.12 = (bf16[128,768]{1,0:T(8,128)(2,1)S(1)}, bf16[128,768]{1,0:T(8,128)(2,1)S(1)}, u32[]{:S(2)}, u32[]{:S(2)}) collective-permute-start(bf16[128,768]{1,0:T(8,128)(2,1)S(1)} %collective-permute-done.8.refs_1_), channel_id=1, source_target_pairs={{0,112},{16,0},{32,16},{48,32},{64,48},{80,64},{96,80},{112,96},{1... | collective-permute-start | bytes 589832 | tf_op jit(solution)/shard_map/ppermute | solution.py:232
  22.2 3.8 %collective-permute-start.6 = (f32[1,512]{1,0:T(1,128)}, f32[1,512]{1,0:T(1,128)S(1)}, u32[]{:S(2)}, u32[]{:S(2)}) collective-permute-start(f32[1,512]{1,0:T(1,128)} %bitcast.35), channel_id=1, source_target_pairs={{0,128},{128,0},{1,129},{129,1},{2,130},{130,2},{3,131},{131,3},{4... | collective-permute-start | bytes 6152 | tf_op jit(solution)/shard_map/ppermute | solution.py:211
  23.7 2.9 %collective-permute-start.9 = (bf16[128,768]{1,0:T(8,128)(2,1)S(1)}, bf16[128,768]{1,0:T(8,128)(2,1)S(1)}, u32[]{:S(2)}, u32[]{:S(2)}) collective-permute-start(bf16[128,768]{1,0:T(8,128)(2,1)S(1)} %collective-permute-done.7.refs_0_), channel_id=1, source_target_pairs={{0,8},{8,0},{1,9},{9,1},{2,10},{10,2},{3,11},{11,3},{4,12},{12,4},... | collective-permute-start | bytes 589832 | tf_op jit(solution)/shard_map/ppermute | solution.py:27
  26.0 1.4 %collective-permute-start.10 = (bf16[128,768]{1,0:T(8,128)(2,1)S(1)}, bf16[128,768]{1,0:T(8,128)(2,1)S(1)}, u32[]{:S(2)}, u32[]{:S(2)}) collective-permute-start(bf16[128,768]{1,0:T(8,128)(2,1)S(1)} %collective-permute-done.8.refs_1_), channel_id=1, source_target_pairs={{0,8},{8,0},{1,9},{9,1},{2,10},{10,2},{3,11},{11,3},{4,12},{12,4},... | collective-permute-start | bytes 589832 | tf_op jit(solution)/shard_map/ppermute | solution.py:27
  26.0 1.7 %collective-permute-start.13 = (bf16[128,768]{1,0:T(8,128)(2,1)S(1)}, bf16[128,768]{1,0:T(8,128)(2,1)S(1)}, u32[]{:S(2)}, u32[]{:S(2)}) collective-permute-start(bf16[128,768]{1,0:T(8,128)(2,1)S(1)} %collective-permute-done.11.refs_0_), channel_id=1, source_target_pairs={{0,8},{8,0},{1,9},{9,1},{2,10},{10,2},{3,11},{11,3},{4,12},{12,4},... | collective-permute-start | bytes 589832 | tf_op jit(solution)/shard_map/ppermute | solution.py:27
  26.5 1.5 %collective-permute-start.14 = (bf16[128,768]{1,0:T(8,128)(2,1)S(1)}, bf16[128,768]{1,0:T(8,128)(2,1)S(1)}, u32[]{:S(2)}, u32[]{:S(2)}) collective-permute-start(bf16[128,768]{1,0:T(8,128)(2,1)S(1)} %collective-permute-done.12.refs_1_), channel_id=1, source_target_pairs={{0,8},{8,0},{1,9},{9,1},{2,10},{10,2},{3,11},{11,3},{4,12},{12,4},... | collective-permute-start | bytes 589832 | tf_op jit(solution)/shard_map/ppermute | solution.py:27
  26.6 9.9 %collective-permute-start = (bf16[128,768]{1,0:T(8,128)(2,1)}, bf16[128,768]{1,0:T(8,128)(2,1)S(1)}, u32[]{:S(2)}, u32[]{:S(2)}) collective-permute-start(bf16[128,768]{1,0:T(8,128)(2,1)} %refs_0_.1), channel_id=1, source_target_pairs={{0,8},{8,0},{1,9},{9,1},{2,10},{10,2},{3,11},{11,3},{4,12},{12,4},... | collective-permute-start | bytes 589832 | tf_op jit(solution)/shard_map/ppermute | solution.py:27
  27.5 9.0 %collective-permute-start.3 = (bf16[128,768]{1,0:T(8,128)(2,1)S(1)}, bf16[128,768]{1,0:T(8,128)(2,1)S(1)}, u32[]{:S(2)}, u32[]{:S(2)}) collective-permute-start(bf16[128,768]{1,0:T(8,128)(2,1)S(1)} %collective-permute-done.1.refs_2_), channel_id=1, source_target_pairs={{0,8},{8,0},{1,9},{9,1},{2,10},{10,2},{3,11},{11,3},{4,12},{12,4},... | collective-permute-start | bytes 589832 | tf_op jit(solution)/shard_map/ppermute | solution.py:27
  27.7 8.8 %collective-permute-start.4 = (bf16[128,768]{1,0:T(8,128)(2,1)S(1)}, bf16[128,768]{1,0:T(8,128)(2,1)S(1)}, u32[]{:S(2)}, u32[]{:S(2)}) collective-permute-start(bf16[128,768]{1,0:T(8,128)(2,1)S(1)} %collective-permute-done.2.refs_3_), channel_id=1, source_target_pairs={{0,8},{8,0},{1,9},{9,1},{2,10},{10,2},{3,11},{11,3},{4,12},{12,4},... | collective-permute-start | bytes 589832 | tf_op jit(solution)/shard_map/ppermute | solution.py:27
  28.0 10.4 %collective-permute-start.15 = (bf16[64,768]{1,0:T(8,128)(2,1)S(1)}, bf16[64,768]{1,0:T(8,128)(2,1)S(1)}, u32[]{:S(2)}, u32[]{:S(2)}) collective-permute-start(bf16[64,768]{1,0:T(8,128)(2,1)S(1)} %slice.8), channel_id=1, source_target_pairs={{0,16},{16,32},{32,48},{48,64},{64,80},{80,96},{96,112},{112,0},{1... | collective-permute-start | bytes 294920 | tf_op jit(solution)/shard_map/ppermute | solution.py:232
  28.1 10.4 %collective-permute-start.16 = (bf16[64,768]{1,0:T(8,128)(2,1)S(1)}, bf16[64,768]{1,0:T(8,128)(2,1)S(1)}, u32[]{:S(2)}, u32[]{:S(2)}) collective-permute-start(bf16[64,768]{1,0:T(8,128)(2,1)S(1)} %slice.9), channel_id=1, source_target_pairs={{0,112},{16,0},{32,16},{48,32},{64,48},{80,64},{96,80},{112,96},{1... | collective-permute-start | bytes 294920 | tf_op jit(solution)/shard_map/ppermute | solution.py:232
  31.3 1.1 %copy-start = (bf16[512,768]{1,0:T(8,128)(2,1)S(1)}, bf16[512,768]{1,0:T(8,128)(2,1)}, u32[]{:S(2)}) copy-start(bf16[512,768]{1,0:T(8,128)(2,1)} %cent_ref.1) | copy-start | bytes 2359300
  32.5 0.7 copy-start.3
  35.1 1.4 %copy-start.2 = (bf16[128,768]{1,0:T(8,128)(2,1)S(1)}, bf16[128,768]{1,0:T(8,128)(2,1)}, u32[]{:S(2)}) copy-start(bf16[128,768]{1,0:T(8,128)(2,1)} %refs_0_.1) | copy-start | bytes 589828
  38.5 1.5 %collective-permute-start.17 = (bf16[128,768]{1,0:T(8,128)(2,1)S(1)}, bf16[128,768]{1,0:T(8,128)(2,1)S(1)}, u32[]{:S(2)}, u32[]{:S(2)}) collective-permute-start(bf16[128,768]{1,0:T(8,128)(2,1)S(1)} %pad_maximum_fusion), channel_id=1, source_target_pairs={{0,8},{8,0},{1,9},{9,1},{2,10},{10,2},{3,11},{11,3},{4,12},{12,4},... | collective-permute-start | bytes 589832 | tf_op jit(solution)/shard_map/ppermute | solution.py:27
  40.9 1.3 %collective-permute-start.18 = (f32[16,128]{1,0:T(8,128)S(1)}, f32[16,128]{1,0:T(8,128)S(1)}, u32[]{:S(2)}, u32[]{:S(2)}) collective-permute-start(f32[16,128]{1,0:T(8,128)S(1)} %row_table.1), channel_id=1, source_target_pairs={{0,8},{8,0},{1,9},{9,1},{2,10},{10,2},{3,11},{11,3},{4,12},{12,4},... | collective-permute-start | bytes 24584 | tf_op jit(solution)/shard_map/ppermute | solution.py:27
  89.4 1.1 %copy-start.1 = (bf16[512,768]{1,0:T(8,128)(2,1)S(1)}, bf16[512,768]{1,0:T(8,128)(2,1)}, u32[]{:S(2)}) copy-start(bf16[512,768]{1,0:T(8,128)(2,1)} %cent_ref.1) | copy-start | bytes 2359300

commit v4 on v3

--- a/solution.py
+++ b/solution.py
@@ -12,7 +12,7 @@
 prior_mass = 1.0
 
 AXES = ("x_lo", "z", "core", "y", "x_hi")
-OWNERS = ("x_lo", "y", "x_hi")
+PLANE = ("x_lo", "y", "x_hi")
 NZ, N_OWNERS = 8, 16
 LANES = 128
 VMEM = pl.BlockSpec(memory_space=pltpu.VMEM)
@@ -21,6 +21,13 @@
 
 def along_z(step):
     return [(i, (i + step) % NZ) for i in range(NZ)]
+
+
+def in_plane(step_x, step_y):
+    place = lambda x, y: (x % 2 * 4 + y % 4) * 2 + x % 4 // 2
+    return [
+        (place(x, y), place(x + step_x, y + step_y)) for x in range(4) for y in range(4)
+    ]
 
 
 def other_core(array):
@@ -53,18 +60,39 @@
     )
 
 
-def centroid_kernel(scale_root, mine_ref, weight_ref, other_ref, other_weight_ref, cent_ref, bias_ref):
-    n = mine_ref.shape[0]
+def in_three(value):
+    high = value.astype(jnp.bfloat16)
+    rest = value - high.astype(jnp.float32)
+    middle = rest.astype(jnp.bfloat16)
+    return high, middle, (rest - middle.astype(jnp.float32)).astype(jnp.bfloat16)
+
+
+def parcel_kernel(cent_ref, weight_ref, *parcels):
+    half = cent_ref.shape[0] // 2
+    for i, parcel_ref in enumerate(parcels):
+        here = slice(i * half, (i + 1) * half)
+        parcel_ref[:half, :] = cent_ref[here, :]
+        row = jnp.concatenate(in_three(weight_ref[:, here]), axis=1)
+        parcel_ref[half:, :] = jnp.broadcast_to(row, (EXTRA, row.shape[1]))
+
+
+def centroid_kernel(scale_root, *refs):
+    parcels = refs[:4]
+    cent_ref, bias_ref, own_ref = refs[4:]
+    half = parcels[0].shape[0] - EXTRA
     x_lo = lax.axis_index("x_lo")
-    for at, block_ref, row_ref in (
-        (x_lo, mine_ref, weight_ref),
-        (1 - x_lo, other_ref, other_weight_ref),
-    ):
-        here = pl.ds(pl.multiple_of(at * n, n), n)
-        cent_ref[here, :] = block_ref[...]
-        wide = block_ref[...].astype(jnp.float32)
+    for i, parcel_ref in enumerate(parcels):
+        block = x_lo if i < 2 else 1 - x_lo
+        here = pl.ds(pl.multiple_of(block * (2 * half) + i % 2 * half, half), half)
+        cent_ref[here, :] = parcel_ref[:half, :]
+        wide = parcel_ref[:half, :].astype(jnp.float32)
         half_sq = 0.5 * jnp.sum(wide * wide, axis=1, keepdims=True)
-        bias_ref[here, :] = column(row_ref[...]) - half_sq * (1.0 / scale_root)
+        parts = parcel_ref[half:, :].astype(jnp.float32)[:1]
+        weight = parts[:, :half] + parts[:, half : 2 * half] + parts[:, 2 * half :]
+        bias_ref[here, :] = column(weight) - half_sq * (1.0 / scale_root)
+    owned = own_ref.shape[0]
+    first = x_lo * (2 * half) + (lax.axis_index("y") * 2 + lax.axis_index("x_hi")) * owned
+    own_ref[...] = cent_ref[pl.ds(pl.multiple_of(first, owned), owned), :].astype(jnp.float32)
 
 
 def row_of(step):
@@ -129,7 +157,7 @@
     n = len(orders)
     logits, rows = refs[:n], refs[n : 2 * n]
     norm_ref, packed_ref, own_ref = refs[2 * n :]
-    n_cent, depth, tile = logits[0].shape[0], rows[0].shape[1], 256
+    n_cent, depth, tile = logits[0].shape[0], rows[0].shape[1], 512
     owned = n_cent // N_OWNERS
     for k in range(0, n_cent, tile):
         total, count = None, None
@@ -173,7 +201,7 @@
     own_ref[...] = norm_ref[pl.ds(row_of(0)[0], 1), :]
 
 
-def update_kernel(came_ref, cent_ref, updated_ref, counts_ref):
+def update_kernel(came_ref, own_ref, updated_ref, counts_ref):
     owned, depth = updated_ref.shape
     at = depth // LANES * owned
     extra = jnp.concatenate([came_ref[i, at : at + EXTRA, :] for i in range(N_OWNERS)])
@@ -185,8 +213,6 @@
     counts_ref[...] = counts[:, :owned]
     turned = extra.T
     mass = jnp.broadcast_to(counts, (LANES, LANES)).T[:owned, :1] + prior_mass
-    first = lax.axis_index("y") * 2 + lax.axis_index("x_hi")
-    own = cent_ref[pl.ds(pl.multiple_of(first * owned, owned), owned), :].astype(jnp.float32)
     for j in range(depth // LANES):
         total = None
         for i in range(N_OWNERS):
@@ -194,7 +220,7 @@
             part = came_ref[i, j * owned : (j + 1) * owned, :] * scale
             total = part if total is None else total + part
         here = slice(j * LANES, (j + 1) * LANES)
-        updated_ref[:, here] = (total + prior_mass * own[:, here]) / mass
+        updated_ref[:, here] = (total + prior_mass * own_ref[:, here]) / mass
 
 
 def local(embeddings, centroids, log_weight):
@@ -206,16 +232,29 @@
     up = lax.ppermute(embeddings, "z", along_z(1))
     down = lax.ppermute(embeddings, "z", along_z(-1))
     other = other_core(embeddings)
-    beside = lax.ppermute(centroids, "x_lo", [(0, 1), (1, 0)])
-    weight = log_weight[None, :]
-    weight_beside = lax.ppermute(weight, "x_lo", [(0, 1), (1, 0)])
+    half = local_count // 2
+    mine = call(
+        parcel_kernel,
+        (shape((half + EXTRA, feat_dim), jnp.bfloat16),) * 2,
+        (centroids, log_weight[None, :]),
+        "centroid_parcels",
+        share=4,
+    )
+    beside = (
+        lax.ppermute(mine[0], PLANE, in_plane(1, 1)),
+        lax.ppermute(mine[1], PLANE, in_plane(-1, 0)),
+    )
 
     def blocks(after):
-        beside_now, weight_now, _ = lax.optimization_barrier((beside, weight_beside, after))
+        ready = lax.optimization_barrier((*beside, after))
         return call(
             functools.partial(centroid_kernel, scale_root),
-            (shape((2 * local_count, feat_dim), jnp.bfloat16), shape((2 * local_count, 1))),
-            (centroids, weight, beside_now, weight_now),
+            (
+                shape((2 * local_count, feat_dim), jnp.bfloat16),
+                shape((2 * local_count, 1)),
+                shape((owned, feat_dim)),
+            ),
+            (*mine, *ready[:2]),
             "centroid_blocks",
             4 * local_count * feat_dim,
             share=4,
@@ -240,7 +279,7 @@
         up, down = moved(up, down)
         came.append([up, down, other_core(up), other_core(down)])
         if len(came) == 2:
-            cents, bias = blocks(up)
+            cents, bias, own_cents = blocks(up)
     up, down = moved(up[:piece], down[piece:])
     done = (
         scores([(0, 0), (0, 1), *both(1)], *came[0]),
@@ -270,11 +309,11 @@
         4 * local_count * n_all * feat_dim,
         2 * local_count * n_all,
     )
-    came = lax.all_to_all(packed.astype(jnp.float16), OWNERS, 0, 0, tiled=True)
+    came = lax.all_to_all(packed.astype(jnp.float16), PLANE, 0, 0, tiled=True)
     updated, counts = call(
         update_kernel,
         (shape((owned, feat_dim)), shape((1, owned))),
-        (came.astype(jnp.float32), centroids),
+        (came.astype(jnp.float32), own_cents),
         "update",
     )
     return (updated, counts.reshape(-1), log_norm.reshape(-1))

time: 91.9 us -> 93.4 us (1.016)
  starting transfers between devices: 20.5 us -> 22.5 us
    ppermute x3, waiting for transfers between devices: 0.01 us -> 5.25 us  [moved(): lax.ppermute(second, 'z', along_z(-1))]
    ppermute x3, waiting for transfers between devices: 4.06 us -> 1.26 us  [moved(): lax.ppermute(first, 'z', along_z(1))]
    ppermute x2, waiting for transfers between devices: 2.3 us -> 0.01 us  [the longest x1 0.01 us: local(): lax.ppermute(mine[0], PLANE, in_plane(1, 1))]
    ppermute x1, waiting for transfers between devices: 3.53 us -> 5.02 us  [local(): up = lax.ppermute(embeddings, 'z', along_z(1))]
    ppermute x2, starting transfers between devices: 2.98 us -> 4.32 us  [the longest x1 2.58 us: local(): lax.ppermute(mine[0], PLANE, in_plane(1, 1))]
    unnamed x8 -> x6, local copies, waits for them, and re-layouts: 2.74 us -> 1.82 us
    pallas_call x8 -> x9, Pallas kernels: 12.3 us -> 12.3 us  [call(): pl.pallas_call(kernel, out_shape=outs, in_specs=[VMEM] * len(args), out_s...]
  transfers between devices with their start and end apart: 19 -> 19, of which waited for: 7 -> 6; matrix products, arithmetic and copies ran while one was open for 0% -> 0% of each run, Pallas kernels for 6% -> 6%
where the time goes in v4:
time: 93.4 us; the launch traced here: 93.2 us
  blocking collectives  41.5 us (44%)
  starting transfers between devices  22.5 us (24%)
  waiting for transfers between devices  13.7 us (15%)
  Pallas kernels  12.3 us (13%)
  local copies, waits for them, and re-layouts  1.84 us (2%)
    all_to_all x1, blocking collectives, local(): came = lax.all_to_all(packed.astype(jnp.float16), PLANE, 0, 0, tiled=True)  27.8 us
    all_to_all x1, blocking collectives, local(): table = joined(*lax.all_to_all(tables, 'z', 0, 0, tiled=True))  13.7 us
    pallas_call x9, Pallas kernels, call(): pl.pallas_call(kernel, out_shape=outs, in_specs=[VMEM] * len(args), out_s...  12.3 us
    ppermute x3, starting transfers between devices, moved(): lax.ppermute(second, 'z', along_z(-1))  10.2 us
    ppermute x3, waiting for transfers between devices, moved(): lax.ppermute(second, 'z', along_z(-1))  5.25 us
    ppermute x1, waiting for transfers between devices, local(): up = lax.ppermute(embeddings, 'z', along_z(1))  5.02 us
    ppermute x1, starting transfers between devices, local(): down = lax.ppermute(embeddings, 'z', along_z(-1))  4.03 us
    ppermute x1, starting transfers between devices, local(): lax.ppermute(mine[0], PLANE, in_plane(1, 1))  2.58 us
  transfers between devices with their start and end apart: 19, of which 6 were waited for; matrix products, arithmetic and copies ran while one was open for 0% of the time, Pallas kernels for 6%

profile of v4, /device:TPU:8, one launch (start us, length us, event | category | flops | bytes accessed | tf_op | source)
XLA Modules:
  0.0 93.2 jit_solution(10097599968111411117)
XLA Ops:
  0.6 2.0 %collective-permute-start.1 = (bf16[128,768]{1,0:T(8,128)(2,1)}, bf16[128,768]{1,0:T(8,128)(2,1)S(1)}, u32[]{:S(2)}, u32[]{:S(2)}) collective-permute-start(bf16[128,768]{1,0:T(8,128)(2,1)} %refs_0_.1), channel_id=1, source_target_pairs={{0,16},{16,32},{32,48},{48,64},{64,80},{80,96},{96,112},{112,0},{1... | collective-permute-start | bytes 589832 | tf_op jit(solution)/shard_map/ppermute | solution.py:232
  2.6 4.0 %collective-permute-start.2 = (bf16[128,768]{1,0:T(8,128)(2,1)}, bf16[128,768]{1,0:T(8,128)(2,1)S(1)}, u32[]{:S(2)}, u32[]{:S(2)}) collective-permute-start(bf16[128,768]{1,0:T(8,128)(2,1)} %refs_0_.1), channel_id=1, source_target_pairs={{0,112},{16,0},{32,16},{48,32},{64,48},{80,64},{96,80},{112,96},{1... | collective-permute-start | bytes 589832 | tf_op jit(solution)/shard_map/ppermute | solution.py:233
  6.7 5.0 %collective-permute-done.1.refs_2_ = bf16[128,768]{1,0:T(8,128)(2,1)S(1)} collective-permute-done((bf16[128,768]{1,0:T(8,128)(2,1)}, bf16[128,768]{1,0:T(8,128)(2,1)S(1)}, u32[]{:S(2)}, u32[]{:S(2)}) %collective-permute-start.1) | collective-permute-done | bytes 196640 | tf_op jit(solution)/shard_map/ppermute | solution.py:232
  11.7 1.1 %copy-done = bf16[512,768]{1,0:T(8,128)(2,1)S(1)} copy-done((bf16[512,768]{1,0:T(8,128)(2,1)S(1)}, bf16[512,768]{1,0:T(8,128)(2,1)}, u32[]{:S(2)}) %copy-start) | copy-done | bytes 786456
  12.8 0.7 copy-done.2
  13.6 2.6 %collective-permute-start.5 = (bf16[264,768]{1,0:T(8,128)(2,1)S(1)}, bf16[264,768]{1,0:T(8,128)(2,1)S(1)}, u32[]{:S(2)}, u32[]{:S(2)}) collective-permute-start(bf16[264,768]{1,0:T(8,128)(2,1)S(1)} %get-tuple-element.28.refs_0_), channel_id=1, source_target_pairs={{0,130},{2,132},{4,134},{6,128},{128,3},{130,5},{132,7},{134,1},{1... | collective-permute-start | bytes 1216520 | tf_op jit(solution)/shard_map/ppermute | solution.py:244
  16.2 3.2 %collective-permute-start.8 = (bf16[128,768]{1,0:T(8,128)(2,1)S(1)}, bf16[128,768]{1,0:T(8,128)(2,1)S(1)}, u32[]{:S(2)}, u32[]{:S(2)}) collective-permute-start(bf16[128,768]{1,0:T(8,128)(2,1)S(1)} %collective-permute-done.2.refs_3_), channel_id=1, source_target_pairs={{0,112},{16,0},{32,16},{48,32},{64,48},{80,64},{96,80},{112,96},{1... | collective-permute-start | bytes 589832 | tf_op jit(solution)/shard_map/ppermute | solution.py:271
  19.4 1.7 %collective-permute-start.6 = (bf16[264,768]{1,0:T(8,128)(2,1)S(1)}, bf16[264,768]{1,0:T(8,128)(2,1)S(1)}, u32[]{:S(2)}, u32[]{:S(2)}) collective-permute-start(bf16[264,768]{1,0:T(8,128)(2,1)S(1)} %get-tuple-element.29.refs_1_), channel_id=1, source_target_pairs={{0,129},{2,131},{4,133},{6,135},{128,0},{130,2},{132,4},{134,6},{1... | collective-permute-start | bytes 1216520 | tf_op jit(solution)/shard_map/ppermute | solution.py:245
  21.2 3.0 %collective-permute-done.8.refs_1_ = bf16[128,768]{1,0:T(8,128)(2,1)S(1)} collective-permute-done((bf16[128,768]{1,0:T(8,128)(2,1)S(1)}, bf16[128,768]{1,0:T(8,128)(2,1)S(1)}, u32[]{:S(2)}, u32[]{:S(2)}) %collective-permute-start.8) | collective-permute-done | bytes 196640 | tf_op jit(solution)/shard_map/ppermute | solution.py:271
  24.2 3.7 %collective-permute-start.12 = (bf16[128,768]{1,0:T(8,128)(2,1)S(1)}, bf16[128,768]{1,0:T(8,128)(2,1)S(1)}, u32[]{:S(2)}, u32[]{:S(2)}) collective-permute-start(bf16[128,768]{1,0:T(8,128)(2,1)S(1)} %collective-permute-done.8.refs_1_), channel_id=1, source_target_pairs={{0,112},{16,0},{32,16},{48,32},{64,48},{80,64},{96,80},{112,96},{1... | collective-permute-start | bytes 589832 | tf_op jit(solution)/shard_map/ppermute | solution.py:271
  28.4 1.3 %collective-permute-done.11.refs_0_ = bf16[128,768]{1,0:T(8,128)(2,1)S(1)} collective-permute-done((bf16[128,768]{1,0:T(8,128)(2,1)S(1)}, bf16[128,768]{1,0:T(8,128)(2,1)S(1)}, u32[]{:S(2)}, u32[]{:S(2)}) %collective-permute-start.11) | collective-permute-done | bytes 196640 | tf_op jit(solution)/shard_map/ppermute | solution.py:271
  29.7 2.3 %collective-permute-done.12.refs_1_ = bf16[128,768]{1,0:T(8,128)(2,1)S(1)} collective-permute-done((bf16[128,768]{1,0:T(8,128)(2,1)S(1)}, bf16[128,768]{1,0:T(8,128)(2,1)S(1)}, u32[]{:S(2)}, u32[]{:S(2)}) %collective-permute-start.12) | collective-permute-done | bytes 196640 | tf_op jit(solution)/shard_map/ppermute | solution.py:271
  32.0 0.8 collective-permute-start.15
  32.8 3.2 %collective-permute-start.16 = (bf16[64,768]{1,0:T(8,128)(2,1)S(1)}, bf16[64,768]{1,0:T(8,128)(2,1)S(1)}, u32[]{:S(2)}, u32[]{:S(2)}) collective-permute-start(bf16[64,768]{1,0:T(8,128)(2,1)S(1)} %slice.9), channel_id=1, source_target_pairs={{0,112},{16,0},{32,16},{48,32},{64,48},{80,64},{96,80},{112,96},{1... | collective-permute-start | bytes 294920 | tf_op jit(solution)/shard_map/ppermute | solution.py:271
  36.6 1.9 %score.4 = (bf16[768,768]{1,0:T(8,128)(2,1)S(1)}, f32[1024,768]{1,0:T(8,128)S(1)}, f32[6,128]{1,0:T(8,128)S(1)}) custom-call(bf16[128,768]{1,0:T(8,128)(2,1)S(1)} %copy-done.1, bf16[128,768]{1,0:T(8,128)(2,1)S(1)} %collective-permute-done.refs_1_, bf16[128,768]{1,0:T(8,128)(2,1)S(1)} %collective-permute-done.1.refs_2_, ...), custom_call_target="tpu_custom_call" | custom-call | flops 301989888 | bytes 1771264 | tf_op jit(solution)/shard_map/score/pallas_call | solution.py:39
  38.6 1.4 %score.5 = (bf16[512,768]{1,0:T(8,128)(2,1)S(1)}, f32[1024,512]{1,0:T(8,128)S(1)}, f32[4,128]{1,0:T(4,128)S(1)}) custom-call(bf16[128,768]{1,0:T(8,128)(2,1)S(1)} %collective-permute-done.7.refs_0_, bf16[128,768]{1,0:T(8,128)(2,1)S(1)} %collective-permute-done.8.refs_1_, bf16[128,768]{1,0:T(8,128)(2,1)S(1)} %collective-permute-done.9.refs_2_, ...), custom_call_target="tpu_custom_call" | custom-call | flops 201326592 | bytes 1312256 | tf_op jit(solution)/shard_map/score/pallas_call | solution.py:39
  40.0 1.4 %score.6 = (bf16[512,768]{1,0:T(8,128)(2,1)S(1)}, f32[1024,512]{1,0:T(8,128)S(1)}, f32[4,128]{1,0:T(4,128)S(1)}) custom-call(bf16[128,768]{1,0:T(8,128)(2,1)S(1)} %collective-permute-done.11.refs_0_, bf16[128,768]{1,0:T(8,128)(2,1)S(1)} %collective-permute-done.12.refs_1_, bf16[128,768]{1,0:T(8,128)(2,1)S(1)} %collective-permute-done.13.refs_2_, ...), custom_call_target="tpu_custom_call" | custom-call | flops 201326592 | bytes 1312256 | tf_op jit(solution)/shard_map/score/pallas_call | solution.py:39
  41.8 1.2 %collective-permute-done.17.refs_2_ = bf16[128,768]{1,0:T(8,128)(2,1)S(1)} collective-permute-done((bf16[128,768]{1,0:T(8,128)(2,1)S(1)}, bf16[128,768]{1,0:T(8,128)(2,1)S(1)}, u32[]{:S(2)}, u32[]{:S(2)}) %collective-permute-start.17) | collective-permute-done | bytes 196640 | tf_op jit(solution)/shard_map/ppermute | solution.py:34
  43.0 0.8 score.7
  44.2 1.0 %collective-permute-done.18 = f32[16,128]{1,0:T(8,128)S(1)} collective-permute-done((f32[16,128]{1,0:T(8,128)S(1)}, f32[16,128]{1,0:T(8,128)S(1)}, u32[]{:S(2)}, u32[]{:S(2)}) %collective-permute-start.18) | collective-permute-done | bytes 8224 | tf_op jit(solution)/shard_map/ppermute | solution.py:34
  45.2 13.7 %all_to_all.10 = f32[8,16,128]{2,1,0:T(8,128)S(1)} all-to-all(f32[8,16,128]{2,1,0:T(8,128)S(1)} %broadcast_in_dim.7), channel_id=1, replica_groups=mesh['x_lo'=2,'z'=8,'core'=2,'y'=4,'x_hi'=2] {'z'}, dimensions={0} | all-to-all | bytes 131072 | tf_op jit(solution)/shard_map/all_to_all | solution.py:298
  59.0 4.9 %spread.1 = (f32[16,392,128]{2,1,0:T(8,128)S(1)}, f32[1,128]{1,0:T(1,128)}) custom-call(f32[1024,768]{1,0:T(8,128)S(1)} %get-tuple-element.34.refs_0_, f32[1024,512]{1,0:T(8,128)S(1)} %get-tuple-element.35.refs_1_, f32[1024,512]{1,0:T(8,128)S(1)} %get-tuple-element.36.refs_2_, f32[1024,256]{1,0:T(8,128)S(1)} %get-tuple-element.42.refs_3_, ...), custom_call_target="tpu_custom_call" | custom-call | flops 3221225472 | bytes 14754304 | tf_op jit(solution)/shard_map/spread/pallas_call | solution.py:39
  64.1 27.8 %all_to_all.11 = f16[16,392,128]{2,1,0:T(8,128)(2,1)S(1)} all-to-all(f16[16,392,128]{2,1,0:T(8,128)(2,1)S(1)} %convert_element_type.6), channel_id=1, replica_groups=mesh['x_lo'=2,'z'=8,'core'=2,'y'=4,'x_hi'=2] {'x_lo','y','x_hi'}, dimensions={0} | all-to-all | bytes 3211264 | tf_op jit(solution)/shard_map/all_to_all | solution.py:312
  92.1 1.1 %update.1 = (f32[64,768]{1,0:T(8,128)}, f32[1,64]{1,0:T(1,128)}) custom-call(f32[16,392,128]{2,1,0:T(8,128)S(1)} %convert_element_type.7.came_ref, f32[64,768]{1,0:T(8,128)S(1)} %get-tuple-element.49.own_ref), custom_call_target="tpu_custom_call" | custom-call | bytes 3604736 | tf_op jit(solution)/shard_map/update/pallas_call | solution.py:39
  (39 shorter events, 2.5 us)
Async XLA Ops:
  0.6 11.0 %collective-permute-start.1 = (bf16[128,768]{1,0:T(8,128)(2,1)}, bf16[128,768]{1,0:T(8,128)(2,1)S(1)}, u32[]{:S(2)}, u32[]{:S(2)}) collective-permute-start(bf16[128,768]{1,0:T(8,128)(2,1)} %refs_0_.1), channel_id=1, source_target_pairs={{0,16},{16,32},{32,48},{48,64},{64,80},{80,96},{96,112},{112,0},{1... | collective-permute-start | bytes 589832 | tf_op jit(solution)/shard_map/ppermute | solution.py:232
  2.6 13.5 %collective-permute-start.2 = (bf16[128,768]{1,0:T(8,128)(2,1)}, bf16[128,768]{1,0:T(8,128)(2,1)S(1)}, u32[]{:S(2)}, u32[]{:S(2)}) collective-permute-start(bf16[128,768]{1,0:T(8,128)(2,1)} %refs_0_.1), channel_id=1, source_target_pairs={{0,112},{16,0},{32,16},{48,32},{64,48},{80,64},{96,80},{112,96},{1... | collective-permute-start | bytes 589832 | tf_op jit(solution)/shard_map/ppermute | solution.py:233
  6.7 12.7 %collective-permute-start = (bf16[128,768]{1,0:T(8,128)(2,1)}, bf16[128,768]{1,0:T(8,128)(2,1)S(1)}, u32[]{:S(2)}, u32[]{:S(2)}) collective-permute-start(bf16[128,768]{1,0:T(8,128)(2,1)} %refs_0_.1), channel_id=1, source_target_pairs={{0,8},{8,0},{1,9},{9,1},{2,10},{10,2},{3,11},{11,3},{4,12},{12,4},... | collective-permute-start | bytes 589832 | tf_op jit(solution)/shard_map/ppermute | solution.py:34
  11.7 9.5 %collective-permute-start.7 = (bf16[128,768]{1,0:T(8,128)(2,1)S(1)}, bf16[128,768]{1,0:T(8,128)(2,1)S(1)}, u32[]{:S(2)}, u32[]{:S(2)}) collective-permute-start(bf16[128,768]{1,0:T(8,128)(2,1)S(1)} %collective-permute-done.1.refs_2_), channel_id=1, source_target_pairs={{0,16},{16,32},{32,48},{48,64},{64,80},{80,96},{96,112},{112,0},{1... | collective-permute-start | bytes 589832 | tf_op jit(solution)/shard_map/ppermute | solution.py:271
  11.7 1.1 %copy-start = (bf16[512,768]{1,0:T(8,128)(2,1)S(1)}, bf16[512,768]{1,0:T(8,128)(2,1)}, u32[]{:S(2)}) copy-start(bf16[512,768]{1,0:T(8,128)(2,1)} %cent_ref.1) | copy-start | bytes 2359300
  12.8 0.7 copy-start.2
  13.5 23.1 %copy-start.1 = (bf16[128,768]{1,0:T(8,128)(2,1)S(1)}, bf16[128,768]{1,0:T(8,128)(2,1)}, u32[]{:S(2)}) copy-start(bf16[128,768]{1,0:T(8,128)(2,1)} %refs_0_.1) | copy-start | bytes 589828
  13.6 14.3 %collective-permute-start.5 = (bf16[264,768]{1,0:T(8,128)(2,1)S(1)}, bf16[264,768]{1,0:T(8,128)(2,1)S(1)}, u32[]{:S(2)}, u32[]{:S(2)}) collective-permute-start(bf16[264,768]{1,0:T(8,128)(2,1)S(1)} %get-tuple-element.28.refs_0_), channel_id=1, source_target_pairs={{0,130},{2,132},{4,134},{6,128},{128,3},{130,5},{132,7},{134,1},{1... | collective-permute-start | bytes 1216520 | tf_op jit(solution)/shard_map/ppermute | solution.py:244
  16.1 5.0 %collective-permute-start.3 = (bf16[128,768]{1,0:T(8,128)(2,1)S(1)}, bf16[128,768]{1,0:T(8,128)(2,1)S(1)}, u32[]{:S(2)}, u32[]{:S(2)}) collective-permute-start(bf16[128,768]{1,0:T(8,128)(2,1)S(1)} %collective-permute-done.1.refs_2_), channel_id=1, source_target_pairs={{0,8},{8,0},{1,9},{9,1},{2,10},{10,2},{3,11},{11,3},{4,12},{12,4},... | collective-permute-start | bytes 589832 | tf_op jit(solution)/shard_map/ppermute | solution.py:34
  16.2 8.1 %collective-permute-start.8 = (bf16[128,768]{1,0:T(8,128)(2,1)S(1)}, bf16[128,768]{1,0:T(8,128)(2,1)S(1)}, u32[]{:S(2)}, u32[]{:S(2)}) collective-permute-start(bf16[128,768]{1,0:T(8,128)(2,1)S(1)} %collective-permute-done.2.refs_3_), channel_id=1, source_target_pairs={{0,112},{16,0},{32,16},{48,32},{64,48},{80,64},{96,80},{112,96},{1... | collective-permute-start | bytes 589832 | tf_op jit(solution)/shard_map/ppermute | solution.py:271
  19.4 12.6 %collective-permute-start.6 = (bf16[264,768]{1,0:T(8,128)(2,1)S(1)}, bf16[264,768]{1,0:T(8,128)(2,1)S(1)}, u32[]{:S(2)}, u32[]{:S(2)}) collective-permute-start(bf16[264,768]{1,0:T(8,128)(2,1)S(1)} %get-tuple-element.29.refs_1_), channel_id=1, source_target_pairs={{0,129},{2,131},{4,133},{6,135},{128,0},{130,2},{132,4},{134,6},{1... | collective-permute-start | bytes 1216520 | tf_op jit(solution)/shard_map/ppermute | solution.py:245
  21.1 6.8 %collective-permute-start.4 = (bf16[128,768]{1,0:T(8,128)(2,1)S(1)}, bf16[128,768]{1,0:T(8,128)(2,1)S(1)}, u32[]{:S(2)}, u32[]{:S(2)}) collective-permute-start(bf16[128,768]{1,0:T(8,128)(2,1)S(1)} %collective-permute-done.2.refs_3_), channel_id=1, source_target_pairs={{0,8},{8,0},{1,9},{9,1},{2,10},{10,2},{3,11},{11,3},{4,12},{12,4},... | collective-permute-start | bytes 589832 | tf_op jit(solution)/shard_map/ppermute | solution.py:34
  21.1 8.5 %collective-permute-start.11 = (bf16[128,768]{1,0:T(8,128)(2,1)S(1)}, bf16[128,768]{1,0:T(8,128)(2,1)S(1)}, u32[]{:S(2)}, u32[]{:S(2)}) collective-permute-start(bf16[128,768]{1,0:T(8,128)(2,1)S(1)} %collective-permute-done.7.refs_0_), channel_id=1, source_target_pairs={{0,16},{16,32},{32,48},{48,64},{64,80},{80,96},{96,112},{112,0},{1... | collective-permute-start | bytes 589832 | tf_op jit(solution)/shard_map/ppermute | solution.py:271
  24.2 7.7 %collective-permute-start.12 = (bf16[128,768]{1,0:T(8,128)(2,1)S(1)}, bf16[128,768]{1,0:T(8,128)(2,1)S(1)}, u32[]{:S(2)}, u32[]{:S(2)}) collective-permute-start(bf16[128,768]{1,0:T(8,128)(2,1)S(1)} %collective-permute-done.8.refs_1_), channel_id=1, source_target_pairs={{0,112},{16,0},{32,16},{48,32},{64,48},{80,64},{96,80},{112,96},{1... | collective-permute-start | bytes 589832 | tf_op jit(solution)/shard_map/ppermute | solution.py:271
  27.9 4.9 %collective-permute-start.9 = (bf16[128,768]{1,0:T(8,128)(2,1)S(1)}, bf16[128,768]{1,0:T(8,128)(2,1)S(1)}, u32[]{:S(2)}, u32[]{:S(2)}) collective-permute-start(bf16[128,768]{1,0:T(8,128)(2,1)S(1)} %collective-permute-done.7.refs_0_), channel_id=1, source_target_pairs={{0,8},{8,0},{1,9},{9,1},{2,10},{10,2},{3,11},{11,3},{4,12},{12,4},... | collective-permute-start | bytes 589832 | tf_op jit(solution)/shard_map/ppermute | solution.py:34
  27.9 10.7 %collective-permute-start.10 = (bf16[128,768]{1,0:T(8,128)(2,1)S(1)}, bf16[128,768]{1,0:T(8,128)(2,1)S(1)}, u32[]{:S(2)}, u32[]{:S(2)}) collective-permute-start(bf16[128,768]{1,0:T(8,128)(2,1)S(1)} %collective-permute-done.8.refs_1_), channel_id=1, source_target_pairs={{0,8},{8,0},{1,9},{9,1},{2,10},{10,2},{3,11},{11,3},{4,12},{12,4},... | collective-permute-start | bytes 589832 | tf_op jit(solution)/shard_map/ppermute | solution.py:34
  29.7 10.3 %collective-permute-start.13 = (bf16[128,768]{1,0:T(8,128)(2,1)S(1)}, bf16[128,768]{1,0:T(8,128)(2,1)S(1)}, u32[]{:S(2)}, u32[]{:S(2)}) collective-permute-start(bf16[128,768]{1,0:T(8,128)(2,1)S(1)} %collective-permute-done.11.refs_0_), channel_id=1, source_target_pairs={{0,8},{8,0},{1,9},{9,1},{2,10},{10,2},{3,11},{11,3},{4,12},{12,4},... | collective-permute-start | bytes 589832 | tf_op jit(solution)/shard_map/ppermute | solution.py:34
  32.0 8.1 %collective-permute-start.14 = (bf16[128,768]{1,0:T(8,128)(2,1)S(1)}, bf16[128,768]{1,0:T(8,128)(2,1)S(1)}, u32[]{:S(2)}, u32[]{:S(2)}) collective-permute-start(bf16[128,768]{1,0:T(8,128)(2,1)S(1)} %collective-permute-done.12.refs_1_), channel_id=1, source_target_pairs={{0,8},{8,0},{1,9},{9,1},{2,10},{10,2},{3,11},{11,3},{4,12},{12,4},... | collective-permute-start | bytes 589832 | tf_op jit(solution)/shard_map/ppermute | solution.py:34
  32.0 9.4 %collective-permute-start.15 = (bf16[64,768]{1,0:T(8,128)(2,1)S(1)}, bf16[64,768]{1,0:T(8,128)(2,1)S(1)}, u32[]{:S(2)}, u32[]{:S(2)}) collective-permute-start(bf16[64,768]{1,0:T(8,128)(2,1)S(1)} %slice.8), channel_id=1, source_target_pairs={{0,16},{16,32},{32,48},{48,64},{64,80},{80,96},{96,112},{112,0},{1... | collective-permute-start | bytes 294920 | tf_op jit(solution)/shard_map/ppermute | solution.py:271
  32.8 8.6 %collective-permute-start.16 = (bf16[64,768]{1,0:T(8,128)(2,1)S(1)}, bf16[64,768]{1,0:T(8,128)(2,1)S(1)}, u32[]{:S(2)}, u32[]{:S(2)}) collective-permute-start(bf16[64,768]{1,0:T(8,128)(2,1)S(1)} %slice.9), channel_id=1, source_target_pairs={{0,112},{16,0},{32,16},{48,32},{64,48},{80,64},{96,80},{112,96},{1... | collective-permute-start | bytes 294920 | tf_op jit(solution)/shard_map/ppermute | solution.py:271
  41.5 1.5 %collective-permute-start.17 = (bf16[128,768]{1,0:T(8,128)(2,1)S(1)}, bf16[128,768]{1,0:T(8,128)(2,1)S(1)}, u32[]{:S(2)}, u32[]{:S(2)}) collective-permute-start(bf16[128,768]{1,0:T(8,128)(2,1)S(1)} %pad_maximum_fusion), channel_id=1, source_target_pairs={{0,8},{8,0},{1,9},{9,1},{2,10},{10,2},{3,11},{11,3},{4,12},{12,4},... | collective-permute-start | bytes 589832 | tf_op jit(solution)/shard_map/ppermute | solution.py:34
  43.9 1.3 %collective-permute-start.18 = (f32[16,128]{1,0:T(8,128)S(1)}, f32[16,128]{1,0:T(8,128)S(1)}, u32[]{:S(2)}, u32[]{:S(2)}) collective-permute-start(f32[16,128]{1,0:T(8,128)S(1)} %row_table.1), channel_id=1, source_target_pairs={{0,8},{8,0},{1,9},{9,1},{2,10},{10,2},{3,11},{11,3},{4,12},{12,4},... | collective-permute-start | bytes 24584 | tf_op jit(solution)/shard_map/ppermute | solution.py:34

commit v5 on v3

v5 whole, which is shorter than its diff:
```python
import functools
import math

import jax
import jax.numpy as jnp
from jax import lax
from jax.experimental import pallas as pl
from jax.experimental.pallas import tpu as pltpu
from jax.sharding import Mesh
from jax.sharding import PartitionSpec as P

prior_mass = 1.0

AXES = ("x_lo", "z", "core", "y", "x_hi")
OWNERS = ("x_lo", "y", "x_hi")
NZ, N_OWNERS = 8, 16
LANES = 128
VMEM = pl.BlockSpec(memory_space=pltpu.VMEM)
SHARE = 4
EXTRA = 8


def along_z(step):
    return [(i, (i + step) % NZ) for i in range(NZ)]


def other_core(array):
    return lax.ppermute(array, "core", [(0, 1), (1, 0)])


def call(kernel, outs, args, name, flops=0, transcendentals=0, share=1, vmem=24):
    size = sum(a.size * a.dtype.itemsize for a in (*args, *outs)) // share
    return pl.pallas_call(
        kernel,
        out_shape=outs,
        in_specs=[VMEM] * len(args),
        out_specs=(VMEM,) * len(outs),
        compiler_params=pltpu.CompilerParams(vmem_limit_bytes=vmem * 1024 * 1024),
        cost_estimate=pl.CostEstimate(
            flops=flops // share, bytes_accessed=size, transcendentals=transcendentals // share
        ),
        name=name,
    )(*args)


def shape(dims, dtype=jnp.float32):
    return jax.ShapeDtypeStruct(dims, dtype)


def column(row):
    n = row.shape[1]
    return jnp.concatenate(
        [jnp.broadcast_to(row[:, i : i + LANES], (LANES, LANES)).T[:, :1] for i in range(0, n, LANES)]
    )


def bias_of(cents, weight_row, scale_root):
    wide = cents.astype(jnp.float32)
    half_sq = 0.5 * jnp.sum(wide * wide, axis=1, keepdims=True)
    return column(weight_row) - half_sq * (1.0 / scale_root)


def own_kernel(scale_root, cent_in, weight_ref, rows_in, cent_ref, bias_ref, rows_ref, owned_ref):
    cent_ref[...] = cent_in[...]
    bias_ref[...] = bias_of(cent_in[...], weight_ref[...], scale_root)
    rows_ref[...] = rows_in[...]
    owned = owned_ref.shape[0]
    first = (lax.axis_index("y") * 2 + lax.axis_index("x_hi")) * owned
    owned_ref[...] = cent_in[pl.ds(pl.multiple_of(first, owned), owned), :].astype(jnp.float32)


def other_kernel(scale_root, cent_ref, weight_ref, bias_ref):
    bias_ref[...] = bias_of(cent_ref[...], weight_ref[...], scale_root)


def row_of(step):
    z, core = lax.axis_index("z"), lax.axis_index("core")
    first = lax.rem(z + step, NZ) * 2
    return first + core, first + 1 - core


def score_kernel(scale_root, n_parts, n_blocks, *refs):
    parts, blocks = refs[:n_parts], refs[n_parts : n_parts + 2 * n_blocks]
    rows_ref, lse_ref = refs[n_parts + 2 * n_blocks :][:2]
    logits_refs = refs[n_parts + 2 * n_blocks + 2 :]
    at = 0
    for part in parts:
        rows_ref[at : at + part.shape[0], :] = part[...]
        at += part.shape[0]
    tile = 256
    for k in range(0, at, tile):
        peak, logits = None, []
        for i, logits_ref in enumerate(logits_refs):
            cent_ref, bias_ref = blocks[2 * i : 2 * i + 2]
            dots = lax.dot_general(
                cent_ref[...], rows_ref[k : k + tile, :], (((1,), (1,)), ((), ())),
                preferred_element_type=jnp.float32,
            )
            logits.append(dots * (1.0 / scale_root) + bias_ref[...])
            logits_ref[:, k : k + tile] = logits[-1]
            top = jnp.max(logits[-1], axis=0, keepdims=True)
            peak = top if peak is None else jnp.maximum(peak, top)
        mass = sum(jnp.sum(jnp.exp(l - peak), axis=0, keepdims=True) for l in logits)
        lse = peak + jnp.log(mass)
        for i in range(tile // LANES):
            row = k // LANES + i
            lse_ref[row : row + 1, :] = lse[:, i * LANES : (i + 1) * LANES]


def score(parts, blocks, scale_root):
    count, depth = sum(p.shape[0] for p in parts), parts[0].shape[1]
    n_cent = blocks[0][0].shape[0]
    return call(
        functools.partial(score_kernel, scale_root, len(parts), len(blocks)),
        (
            shape((count, depth), jnp.bfloat16),
            shape((count // LANES, LANES)),
            *[shape((n_cent, count))] * len(blocks),
        ),
        (*parts, *(a for block in blocks for a in block)),
        "score",
        2 * n_cent * count * depth * len(blocks),
        n_cent * count * len(blocks),
        SHARE,
    )


def table_kernel(orders, *refs):
    table_ref = refs[-1]
    seen = set()
    for order, lse in zip(orders, refs[:-1]):
        for i, (dist, side) in enumerate(order):
            here = pl.ds(row_of(dist)[side], 1)
            value = lse[i : i + 1, :]
            table_ref[here, :] = joined(table_ref[here, :], value) if (dist, side) in seen else value
            seen.add((dist, side))


def joined(*tables):
    top = functools.reduce(jnp.maximum, tables)
    return top + jnp.log(sum(jnp.exp(t - top) for t in tables))


def spread_kernel(orders, *refs):
    n = len(orders)
    logits, rows = (refs[:n], refs[n : 2 * n]), refs[2 * n : 3 * n]
    norm_ref, packed_ref, own_ref = refs[3 * n :]
    tile, depth = logits[0][0].shape[0], rows[0].shape[1]
    owned = 2 * tile // N_OWNERS
    x_lo = lax.axis_index("x_lo")
    for block in range(2):
        first = lax.rem(x_lo + block, 2) * (tile // owned)
        total, count = None, None
        for order, logits_ref, rows_ref in zip(orders, logits[block], rows):
            resp = []
            for i, (dist, side) in enumerate(order):
                norm = norm_ref[pl.ds(row_of(dist)[side], 1), :]
                r = jnp.exp(logits_ref[:, i * LANES : (i + 1) * LANES] - norm)
                count = r if count is None else count + r
                resp.append(r.astype(jnp.bfloat16))
            part = jnp.dot(
                jnp.concatenate(resp, axis=1), rows_ref[...], preferred_element_type=jnp.float32
            )
            total = part if total is None else total + part
        count = jnp.sum(count, axis=1, keepdims=True)
        top = jnp.max(jnp.abs(total), axis=1, keepdims=True)
        scale = jnp.maximum(top * 2.0**-14, 2.0**-14).astype(jnp.bfloat16).astype(jnp.float32)
        total = total * (1.0 / scale)
        high = count.astype(jnp.bfloat16).astype(jnp.float32)
        middle = (count - high).astype(jnp.bfloat16).astype(jnp.float32)
        low = count - high - middle
        lane = lax.broadcasted_iota(jnp.int32, (tile, LANES), 1)
        extra = jnp.zeros((tile, LANES), jnp.float32)
        for i, value in enumerate((scale, high, middle * 2.0**8, low * 2.0**16)):
            extra = jnp.where(lane == i, value, extra)
        extra = extra.T[:EXTRA, :]
        at = depth // LANES * owned
        for b in range(tile // owned):
            owner = first + b
            for j in range(depth // LANES):
                packed_ref[owner, j * owned : (j + 1) * owned, :] = total[
                    b * owned : (b + 1) * owned, j * LANES : (j + 1) * LANES
                ]
            packed_ref[owner, at : at + EXTRA, :] = jnp.concatenate(
                [
                    extra[:, b * owned : (b + 1) * owned],
                    jnp.zeros((EXTRA, LANES - owned), jnp.float32),
                ],
                axis=1,
            )
    own_ref[...] = norm_ref[pl.ds(row_of(0)[0], 1), :]


def update_kernel(came_ref, own_ref, updated_ref, counts_ref):
    owned, depth = updated_ref.shape
    at = depth // LANES * owned
    extra = jnp.concatenate([came_ref[i, at : at + EXTRA, :] for i in range(N_OWNERS)])
    counts = None
    for i in range(N_OWNERS):
        e = i * EXTRA
        c = extra[e + 1 : e + 2] + (extra[e + 2 : e + 3] * 2.0**-8 + extra[e + 3 : e + 4] * 2.0**-16)
        counts = c if counts is None else counts + c
    counts_ref[...] = counts[:, :owned]
    turned = extra.T
    mass = jnp.broadcast_to(counts, (LANES, LANES)).T[:owned, :1] + prior_mass
    for j in range(depth // LANES):
        total = None
        for i in range(N_OWNERS):
            scale = turned[:owned, i * EXTRA : i * EXTRA + 1]
            part = came_ref[i, j * owned : (j + 1) * owned, :] * scale
            total = part if total is None else total + part
        here = slice(j * LANES, (j + 1) * LANES)
        updated_ref[:, here] = (total + prior_mass * own_ref[:, here]) / mass


def local(embeddings, centroids, log_weight):
    local_count, feat_dim = centroids.shape
    n_rows = embeddings.shape[0]
    scale_root = math.sqrt(feat_dim)
    owned = local_count // 8

    up = lax.ppermute(embeddings, "z", along_z(1))
    down = lax.ppermute(embeddings, "z", along_z(-1))
    other = other_core(embeddings)
    weight = log_weight[None, :]
    cents_beside = lax.ppermute(centroids, "x_lo", [(0, 1), (1, 0)])
    weight_beside = lax.ppermute(weight, "x_lo", [(0, 1), (1, 0)])
    cents, bias, mine, owned_cents = call(
        functools.partial(own_kernel, scale_root),
        (
            shape(centroids.shape, jnp.bfloat16),
            shape((local_count, 1)),
            shape(embeddings.shape, jnp.bfloat16),
            shape((owned, feat_dim)),
        ),
        (centroids, weight, embeddings),
        "own_block",
        share=SHARE,
    )
    here = cents, bias
    up, down = lax.optimization_barrier((up, down, cents, bias, mine, owned_cents))[:2]
    scored, orders = [], []

    def scores(order, parts, *blocks):
        rows, lse, *logits = score(parts, blocks, scale_root)
        scored.append(lse)
        orders.append(order)
        return rows, lse, logits

    def moved(first, second):
        return lax.ppermute(first, "z", along_z(1)), lax.ppermute(second, "z", along_z(-1))

    def pair(step, side):
        return [(NZ - step, side), (step, side)]

    piece = n_rows // 2
    order1 = [(0, 0), (0, 1), *pair(1, 0)]
    first = [mine, other, up, down]
    side = [other_core(up), other_core(down)]
    up, down = moved(up, down)
    rows1, lse, (near1,) = scores(order1, first, here)
    up, down = lax.optimization_barrier((up, down, lse))[:2]
    order2 = pair(1, 1) + pair(2, 0)
    second = [*side, up, down]
    side = [other_core(up), other_core(down)]
    up, down = moved(up, down)
    rows2, lse, (near2,) = scores(order2, second, here)
    cents_beside, weight_beside = lax.optimization_barrier((cents_beside, weight_beside, up))[:2]
    (bias_beside,) = call(
        functools.partial(other_kernel, scale_root),
        (shape((local_count, 1)),),
        (cents_beside, weight_beside),
        "other_block",
        share=SHARE,
    )
    there = cents_beside, bias_beside
    order3 = pair(2, 1) + pair(3, 0)
    third = [*side, up, down]
    side = [other_core(up), other_core(down)]
    up, down = moved(up[:piece], down[piece:])
    _, lse1, (far1,) = scores(order1, [rows1], there)
    _, lse2, (far2,) = scores(order2, [rows2], there)
    rows3, lse3, (near3, far3) = scores(order3, third, here, there)
    rows4, lse4, (near4, far4) = scores(pair(3, 1), side, here, there)
    up, down = lax.optimization_barrier((up, down, lse1, lse2, lse3, lse4))[:2]
    last = [up, down, other_core(jnp.concatenate([up, down]))]
    rows5, _, (near5, far5) = scores([(4, 0), (4, 1)], last, here, there)
    groups = [
        (order1, rows1, near1, far1),
        (order2, rows2, near2, far2),
        (order3, rows3, near3, far3),
        (pair(3, 1), rows4, near4, far4),
        ([(4, 0), (4, 1)], rows5, near5, far5),
    ]

    (table,) = call(
        functools.partial(table_kernel, orders), (shape((2 * NZ, LANES)),), scored, "row_table"
    )
    table = joined(table, other_core(table))
    tables = jnp.broadcast_to(table, (NZ, *table.shape))
    table = joined(*lax.all_to_all(tables, "z", 0, 0, tiled=True))

    n_all = 2 * NZ * n_rows
    packed, log_norm = call(
        functools.partial(spread_kernel, [o for o, *_ in groups]),
        (
            shape((N_OWNERS, owned * feat_dim // LANES + EXTRA, LANES)),
            shape((1, LANES)),
        ),
        (
            *(group[2] for group in groups),
            *(group[3] for group in groups),
            *(group[1] for group in groups),
            table,
        ),
        "spread",
        4 * local_count * n_all * feat_dim,
        2 * local_count * n_all,
    )
    came = lax.all_to_all(packed.astype(jnp.float16), OWNERS, 0, 0, tiled=True)
    updated, counts = call(
        update_kernel,
        (shape((owned, feat_dim)), shape((1, owned))),
        (came.astype(jnp.float32), owned_cents),
        "update",
    )
    return (updated, counts.reshape(-1), log_norm.reshape(-1))


def solution(mesh):
    split = Mesh(mesh.devices.reshape(2, NZ, 2, 4, 2), AXES)
    block = ("x_lo", "z", "core")
    return jax.shard_map(
        local,
        mesh=split,
        in_specs=(P(AXES, None), P(block, None), P(block)),
        out_specs=(P(AXES, None), P(AXES), P(AXES)),
        check_vma=False,
    )
```

time: 91.9 us -> 89 us (0.968)
  blocking collectives: 41.9 us -> 39.6 us
  waiting for transfers between devices: 13 us -> 11.1 us
  Pallas kernels: 12.3 us -> 13.9 us
    all_to_all x1, blocking collectives: 13.6 us -> 11.4 us  [local(): table = joined(*lax.all_to_all(tables, 'z', 0, 0, tiled=True))]
    ppermute x1, starting transfers between devices: 1.99 us -> 0.01 us  [local(): up = lax.ppermute(embeddings, 'z', along_z(1))]
    ppermute x1, starting transfers between devices: 4.03 us -> 5.93 us  [local(): down = lax.ppermute(embeddings, 'z', along_z(-1))]
    pallas_call x8 -> x12, Pallas kernels: 12.3 us -> 13.9 us  [call(): pl.pallas_call(kernel, out_shape=outs, in_specs=[VMEM] * len(args), out_s...]
    ppermute x3, waiting for transfers between devices: 4.06 us -> 2.89 us  [moved(): lax.ppermute(first, 'z', along_z(1))]
    unnamed x8 -> x6, local copies, waits for them, and re-layouts: 2.74 us -> 2.77 us
  transfers between devices with their start and end apart: 19 -> 19, of which waited for: 7 -> 7; matrix products, arithmetic and copies ran while one was open for 0% -> 0% of each run, Pallas kernels for 6% -> 8%
where the time goes in v5:
time: 89 us; the launch traced here: 88.8 us
  blocking collectives  39.6 us (44%)
  starting transfers between devices  20.1 us (23%)
  Pallas kernels  13.9 us (16%)
  waiting for transfers between devices  11.1 us (12%)
  local copies, waits for them, and re-layouts  2.79 us (3%)
    all_to_all x1, blocking collectives, local(): came = lax.all_to_all(packed.astype(jnp.float16), OWNERS, 0, 0, tiled=True)  28.3 us
    pallas_call x12, Pallas kernels, call(): pl.pallas_call(kernel, out_shape=outs, in_specs=[VMEM] * len(args), out_s...  13.9 us
    all_to_all x1, blocking collectives, local(): table = joined(*lax.all_to_all(tables, 'z', 0, 0, tiled=True))  11.4 us
    ppermute x3, starting transfers between devices, moved(): lax.ppermute(second, 'z', along_z(-1))  9.69 us
    ppermute x1, starting transfers between devices, local(): down = lax.ppermute(embeddings, 'z', along_z(-1))  5.93 us
    ppermute x1, waiting for transfers between devices, local(): up = lax.ppermute(embeddings, 'z', along_z(1))  3.17 us
    ppermute x9, waiting for transfers between devices, other_core(): return lax.ppermute(array, 'core', [(0, 1), (1, 0)])  2.91 us
    ppermute x3, waiting for transfers between devices, moved(): lax.ppermute(first, 'z', along_z(1))  2.89 us
  transfers between devices with their start and end apart: 19, of which 7 were waited for; matrix products, arithmetic and copies ran while one was open for 0% of the time, Pallas kernels for 8%

profile of v5, /device:TPU:8, one launch (start us, length us, event | category | flops | bytes accessed | tf_op | source)
XLA Modules:
  0.0 88.8 jit_solution(3134724249895283792)
XLA Ops:
  0.6 5.9 %collective-permute-start.2 = (bf16[128,768]{1,0:T(8,128)(2,1)}, bf16[128,768]{1,0:T(8,128)(2,1)S(1)}, u32[]{:S(2)}, u32[]{:S(2)}) collective-permute-start(bf16[128,768]{1,0:T(8,128)(2,1)} %rows_in.1), channel_id=1, source_target_pairs={{0,112},{16,0},{32,16},{48,32},{64,48},{80,64},{96,80},{112,96},{1... | collective-permute-start | bytes 589832 | tf_op jit(solution)/shard_map/ppermute | solution.py:223
  6.6 1.5 %collective-permute-start.11 = (bf16[512,768]{1,0:T(8,128)(2,1)}, bf16[512,768]{1,0:T(8,128)(2,1)S(1)}, u32[]{:S(2)}, u32[]{:S(2)}) collective-permute-start(bf16[512,768]{1,0:T(8,128)(2,1)} %cent_in.1), channel_id=1, source_target_pairs={{0,128},{128,0},{1,129},{129,1},{2,130},{130,2},{3,131},{131,3},{4... | collective-permute-start | bytes 2359304 | tf_op jit(solution)/shard_map/ppermute | solution.py:226
  8.1 1.2 %copy-done = bf16[512,768]{1,0:T(8,128)(2,1)S(1)} copy-done((bf16[512,768]{1,0:T(8,128)(2,1)S(1)}, bf16[512,768]{1,0:T(8,128)(2,1)}, u32[]{:S(2)}) %copy-start) | copy-done | bytes 786456
  9.2 0.9 %copy-done.1 = bf16[128,768]{1,0:T(8,128)(2,1)S(1)} copy-done((bf16[128,768]{1,0:T(8,128)(2,1)S(1)}, bf16[128,768]{1,0:T(8,128)(2,1)}, u32[]{:S(2)}) %copy-start.1) | copy-done | bytes 196632
  11.2 3.2 %collective-permute-done.1.refs_2_ = bf16[128,768]{1,0:T(8,128)(2,1)S(1)} collective-permute-done((bf16[128,768]{1,0:T(8,128)(2,1)}, bf16[128,768]{1,0:T(8,128)(2,1)S(1)}, u32[]{:S(2)}, u32[]{:S(2)}) %collective-permute-start.1) | collective-permute-done | bytes 196640 | tf_op jit(solution)/shard_map/ppermute | solution.py:222
  14.3 3.2 %collective-permute-start.6 = (bf16[128,768]{1,0:T(8,128)(2,1)S(1)}, bf16[128,768]{1,0:T(8,128)(2,1)S(1)}, u32[]{:S(2)}, u32[]{:S(2)}) collective-permute-start(bf16[128,768]{1,0:T(8,128)(2,1)S(1)} %collective-permute-done.2.refs_3_), channel_id=1, source_target_pairs={{0,112},{16,0},{32,16},{48,32},{64,48},{80,64},{96,80},{112,96},{1... | collective-permute-start | bytes 589832 | tf_op jit(solution)/shard_map/ppermute | solution.py:251
  17.6 0.8 score.7
  18.4 2.8 %collective-permute-done.5.refs_2_ = bf16[128,768]{1,0:T(8,128)(2,1)S(1)} collective-permute-done((bf16[128,768]{1,0:T(8,128)(2,1)S(1)}, bf16[128,768]{1,0:T(8,128)(2,1)S(1)}, u32[]{:S(2)}, u32[]{:S(2)}) %collective-permute-start.5) | collective-permute-done | bytes 196640 | tf_op jit(solution)/shard_map/ppermute | solution.py:251
  21.2 3.2 %collective-permute-start.10 = (bf16[128,768]{1,0:T(8,128)(2,1)S(1)}, bf16[128,768]{1,0:T(8,128)(2,1)S(1)}, u32[]{:S(2)}, u32[]{:S(2)}) collective-permute-start(bf16[128,768]{1,0:T(8,128)(2,1)S(1)} %collective-permute-done.6.refs_3_), channel_id=1, source_target_pairs={{0,112},{16,0},{32,16},{48,32},{64,48},{80,64},{96,80},{112,96},{1... | collective-permute-start | bytes 589832 | tf_op jit(solution)/shard_map/ppermute | solution.py:251
  24.5 1.5 %collective-permute-start.12 = (f32[1,512]{1,0:T(1,128)S(1)}, f32[1,512]{1,0:T(1,128)S(1)}, u32[]{:S(2)}, u32[]{:S(2)}) collective-permute-start(f32[1,512]{1,0:T(1,128)S(1)} %bitcast.36), channel_id=1, source_target_pairs={{0,128},{128,0},{1,129},{129,1},{2,130},{130,2},{3,131},{131,3},{4... | collective-permute-start | bytes 6152 | tf_op jit(solution)/shard_map/ppermute | solution.py:227
  26.0 2.1 %collective-permute-done.12.weight_ref = f32[1,512]{1,0:T(1,128)S(1)} collective-permute-done((f32[1,512]{1,0:T(1,128)S(1)}, f32[1,512]{1,0:T(1,128)S(1)}, u32[]{:S(2)}, u32[]{:S(2)}) %collective-permute-start.12) | collective-permute-done | bytes 2080 | tf_op jit(solution)/shard_map/ppermute | solution.py:227
  29.8 3.2 %collective-permute-start.16 = (bf16[64,768]{1,0:T(8,128)(2,1)S(1)}, bf16[64,768]{1,0:T(8,128)(2,1)S(1)}, u32[]{:S(2)}, u32[]{:S(2)}) collective-permute-start(bf16[64,768]{1,0:T(8,128)(2,1)S(1)} %slice.9), channel_id=1, source_target_pairs={{0,112},{16,0},{32,16},{48,32},{64,48},{80,64},{96,80},{112,96},{1... | collective-permute-start | bytes 294920 | tf_op jit(solution)/shard_map/ppermute | solution.py:251
  33.0 0.8 score.8
  34.1 1.2 %score.12 = (bf16[512,768]{1,0:T(8,128)(2,1)}, f32[4,128]{1,0:T(4,128)S(1)}, f32[512,512]{1,0:T(8,128)S(1)}) custom-call(bf16[512,768]{1,0:T(8,128)(2,1)S(1)} %get-tuple-element.58.refs_0_.refs_11_, bf16[512,768]{1,0:T(8,128)(2,1)S(1)} %collective-permute-done.11.cent_ref.refs_6_.refs_4_.refs_1_.refs_5_, f32[512,1]{1,0:T(8,128)S(1)} %other_block.1.refs_7_.refs_5_.refs_2_.refs_6_), custom_call_target="tpu_custom_call" | custom-call | flops 100663296 | bytes 852992 | tf_op jit(solution)/shard_map/score/pallas_call | solution.py:33
  35.3 1.2 %score.11 = (bf16[512,768]{1,0:T(8,128)(2,1)}, f32[4,128]{1,0:T(4,128)S(1)}, f32[512,512]{1,0:T(8,128)S(1)}) custom-call(bf16[512,768]{1,0:T(8,128)(2,1)S(1)} %get-tuple-element.56.refs_0_.refs_10_, bf16[512,768]{1,0:T(8,128)(2,1)S(1)} %collective-permute-done.11.cent_ref.refs_6_.refs_4_.refs_1_.refs_5_, f32[512,1]{1,0:T(8,128)S(1)} %other_block.1.refs_7_.refs_5_.refs_2_.refs_6_), custom_call_target="tpu_custom_call" | custom-call | flops 100663296 | bytes 852992 | tf_op jit(solution)/shard_map/score/pallas_call | solution.py:33
  36.5 0.8 score.10
  37.4 1.4 %score.9 = (bf16[512,768]{1,0:T(8,128)(2,1)S(1)}, f32[4,128]{1,0:T(4,128)S(1)}, f32[512,512]{1,0:T(8,128)S(1)}, f32[512,512]{1,0:T(8,128)S(1)}) custom-call(bf16[128,768]{1,0:T(8,128)(2,1)S(1)} %collective-permute-done.7.refs_0_, bf16[128,768]{1,0:T(8,128)(2,1)S(1)} %collective-permute-done.8.refs_1_, bf16[128,768]{1,0:T(8,128)(2,1)S(1)} %collective-permute-done.9.refs_2_, ...), custom_call_target="tpu_custom_call" | custom-call | flops 201326592 | bytes 1312256 | tf_op jit(solution)/shard_map/score/pallas_call | solution.py:33
  38.9 1.4 %collective-permute-done.17.refs_2_ = bf16[128,768]{1,0:T(8,128)(2,1)S(1)} collective-permute-done((bf16[128,768]{1,0:T(8,128)(2,1)S(1)}, bf16[128,768]{1,0:T(8,128)(2,1)S(1)}, u32[]{:S(2)}, u32[]{:S(2)}) %collective-permute-start.17) | collective-permute-done | bytes 196640 | tf_op jit(solution)/shard_map/ppermute | solution.py:28
  40.3 0.8 score.13
  41.5 1.0 %collective-permute-done.18 = f32[16,128]{1,0:T(8,128)S(1)} collective-permute-done((f32[16,128]{1,0:T(8,128)S(1)}, f32[16,128]{1,0:T(8,128)S(1)}, u32[]{:S(2)}, u32[]{:S(2)}) %collective-permute-start.18) | collective-permute-done | bytes 8224 | tf_op jit(solution)/shard_map/ppermute | solution.py:28
  42.6 11.4 %all_to_all.10 = f32[8,16,128]{2,1,0:T(8,128)S(1)} all-to-all(f32[8,16,128]{2,1,0:T(8,128)S(1)} %broadcast_in_dim.7), channel_id=1, replica_groups=mesh['x_lo'=2,'z'=8,'core'=2,'y'=4,'x_hi'=2] {'z'}, dimensions={0} | all-to-all | bytes 131072 | tf_op jit(solution)/shard_map/all_to_all | solution.py:301
  54.0 5.0 %spread.1 = (f32[16,392,128]{2,1,0:T(8,128)S(1)}, f32[1,128]{1,0:T(1,128)}) custom-call(f32[512,512]{1,0:T(8,128)S(1)} %get-tuple-element.47.refs_0_, f32[512,512]{1,0:T(8,128)S(1)} %get-tuple-element.51.refs_1_, f32[512,512]{1,0:T(8,128)S(1)} %get-tuple-element.54.refs_2_, f32[512,256]{1,0:T(8,128)S(1)} %get-tuple-element.55.refs_3_, ...), custom_call_target="tpu_custom_call" | custom-call | flops 3221225472 | bytes 14754304 | tf_op jit(solution)/shard_map/spread/pallas_call | solution.py:33
  59.1 28.3 %all_to_all.11 = f16[16,392,128]{2,1,0:T(8,128)(2,1)S(1)} all-to-all(f16[16,392,128]{2,1,0:T(8,128)(2,1)S(1)} %convert_element_type.6), channel_id=1, replica_groups=mesh['x_lo'=2,'z'=8,'core'=2,'y'=4,'x_hi'=2] {'x_lo','y','x_hi'}, dimensions={0} | all-to-all | bytes 3211264 | tf_op jit(solution)/shard_map/all_to_all | solution.py:320
  87.6 1.1 %update.1 = (f32[64,768]{1,0:T(8,128)}, f32[1,64]{1,0:T(1,128)}) custom-call(f32[16,392,128]{2,1,0:T(8,128)S(1)} %convert_element_type.7.came_ref, f32[64,768]{1,0:T(8,128)S(1)} %get-tuple-element.44.own_ref), custom_call_target="tpu_custom_call" | custom-call | bytes 3604736 | tf_op jit(solution)/shard_map/update/pallas_call | solution.py:33
  (42 shorter events, 4.0 us)
Async XLA Ops:
  0.6 10.5 %collective-permute-start.2 = (bf16[128,768]{1,0:T(8,128)(2,1)}, bf16[128,768]{1,0:T(8,128)(2,1)S(1)}, u32[]{:S(2)}, u32[]{:S(2)}) collective-permute-start(bf16[128,768]{1,0:T(8,128)(2,1)} %rows_in.1), channel_id=1, source_target_pairs={{0,112},{16,0},{32,16},{48,32},{64,48},{80,64},{96,80},{112,96},{1... | collective-permute-start | bytes 589832 | tf_op jit(solution)/shard_map/ppermute | solution.py:223
  6.6 7.8 %collective-permute-start.1 = (bf16[128,768]{1,0:T(8,128)(2,1)}, bf16[128,768]{1,0:T(8,128)(2,1)S(1)}, u32[]{:S(2)}, u32[]{:S(2)}) collective-permute-start(bf16[128,768]{1,0:T(8,128)(2,1)} %rows_in.1), channel_id=1, source_target_pairs={{0,16},{16,32},{32,48},{48,64},{64,80},{80,96},{96,112},{112,0},{1... | collective-permute-start | bytes 589832 | tf_op jit(solution)/shard_map/ppermute | solution.py:222
  6.6 23.1 %collective-permute-start.11 = (bf16[512,768]{1,0:T(8,128)(2,1)}, bf16[512,768]{1,0:T(8,128)(2,1)S(1)}, u32[]{:S(2)}, u32[]{:S(2)}) collective-permute-start(bf16[512,768]{1,0:T(8,128)(2,1)} %cent_in.1), channel_id=1, source_target_pairs={{0,128},{128,0},{1,129},{129,1},{2,130},{130,2},{3,131},{131,3},{4... | collective-permute-start | bytes 2359304 | tf_op jit(solution)/shard_map/ppermute | solution.py:226
  8.1 9.5 %collective-permute-start = (bf16[128,768]{1,0:T(8,128)(2,1)}, bf16[128,768]{1,0:T(8,128)(2,1)S(1)}, u32[]{:S(2)}, u32[]{:S(2)}) collective-permute-start(bf16[128,768]{1,0:T(8,128)(2,1)} %rows_in.1), channel_id=1, source_target_pairs={{0,8},{8,0},{1,9},{9,1},{2,10},{10,2},{3,11},{11,3},{4,12},{12,4},... | collective-permute-start | bytes 589832 | tf_op jit(solution)/shard_map/ppermute | solution.py:28
  8.1 1.2 %copy-start = (bf16[512,768]{1,0:T(8,128)(2,1)S(1)}, bf16[512,768]{1,0:T(8,128)(2,1)}, u32[]{:S(2)}) copy-start(bf16[512,768]{1,0:T(8,128)(2,1)} %cent_in.1) | copy-start | bytes 2359300
  9.2 0.9 %copy-start.1 = (bf16[128,768]{1,0:T(8,128)(2,1)S(1)}, bf16[128,768]{1,0:T(8,128)(2,1)}, u32[]{:S(2)}) copy-start(bf16[128,768]{1,0:T(8,128)(2,1)} %rows_in.1) | copy-start | bytes 589828
  10.2 0.7 copy-start.2
  14.3 6.9 %collective-permute-start.5 = (bf16[128,768]{1,0:T(8,128)(2,1)S(1)}, bf16[128,768]{1,0:T(8,128)(2,1)S(1)}, u32[]{:S(2)}, u32[]{:S(2)}) collective-permute-start(bf16[128,768]{1,0:T(8,128)(2,1)S(1)} %collective-permute-done.1.refs_2_), channel_id=1, source_target_pairs={{0,16},{16,32},{32,48},{48,64},{64,80},{80,96},{96,112},{112,0},{1... | collective-permute-start | bytes 589832 | tf_op jit(solution)/shard_map/ppermute | solution.py:251
  14.3 6.9 %collective-permute-start.6 = (bf16[128,768]{1,0:T(8,128)(2,1)S(1)}, bf16[128,768]{1,0:T(8,128)(2,1)S(1)}, u32[]{:S(2)}, u32[]{:S(2)}) collective-permute-start(bf16[128,768]{1,0:T(8,128)(2,1)S(1)} %collective-permute-done.2.refs_3_), channel_id=1, source_target_pairs={{0,112},{16,0},{32,16},{48,32},{64,48},{80,64},{96,80},{112,96},{1... | collective-permute-start | bytes 589832 | tf_op jit(solution)/shard_map/ppermute | solution.py:251
  21.2 6.9 %collective-permute-start.9 = (bf16[128,768]{1,0:T(8,128)(2,1)S(1)}, bf16[128,768]{1,0:T(8,128)(2,1)S(1)}, u32[]{:S(2)}, u32[]{:S(2)}) collective-permute-start(bf16[128,768]{1,0:T(8,128)(2,1)S(1)} %collective-permute-done.5.refs_2_), channel_id=1, source_target_pairs={{0,16},{16,32},{32,48},{48,64},{64,80},{80,96},{96,112},{112,0},{1... | collective-permute-start | bytes 589832 | tf_op jit(solution)/shard_map/ppermute | solution.py:251
  21.2 7.3 %collective-permute-start.10 = (bf16[128,768]{1,0:T(8,128)(2,1)S(1)}, bf16[128,768]{1,0:T(8,128)(2,1)S(1)}, u32[]{:S(2)}, u32[]{:S(2)}) collective-permute-start(bf16[128,768]{1,0:T(8,128)(2,1)S(1)} %collective-permute-done.6.refs_3_), channel_id=1, source_target_pairs={{0,112},{16,0},{32,16},{48,32},{64,48},{80,64},{96,80},{112,96},{1... | collective-permute-start | bytes 589832 | tf_op jit(solution)/shard_map/ppermute | solution.py:251
  24.5 3.6 %collective-permute-start.12 = (f32[1,512]{1,0:T(1,128)S(1)}, f32[1,512]{1,0:T(1,128)S(1)}, u32[]{:S(2)}, u32[]{:S(2)}) collective-permute-start(f32[1,512]{1,0:T(1,128)S(1)} %bitcast.36), channel_id=1, source_target_pairs={{0,128},{128,0},{1,129},{129,1},{2,130},{130,2},{3,131},{131,3},{4... | collective-permute-start | bytes 6152 | tf_op jit(solution)/shard_map/ppermute | solution.py:227
  26.0 2.7 %collective-permute-start.3 = (bf16[128,768]{1,0:T(8,128)(2,1)S(1)}, bf16[128,768]{1,0:T(8,128)(2,1)S(1)}, u32[]{:S(2)}, u32[]{:S(2)}) collective-permute-start(bf16[128,768]{1,0:T(8,128)(2,1)S(1)} %collective-permute-done.1.refs_2_), channel_id=1, source_target_pairs={{0,8},{8,0},{1,9},{9,1},{2,10},{10,2},{3,11},{11,3},{4,12},{12,4},... | collective-permute-start | bytes 589832 | tf_op jit(solution)/shard_map/ppermute | solution.py:28
  28.1 1.4 %collective-permute-start.4 = (bf16[128,768]{1,0:T(8,128)(2,1)S(1)}, bf16[128,768]{1,0:T(8,128)(2,1)S(1)}, u32[]{:S(2)}, u32[]{:S(2)}) collective-permute-start(bf16[128,768]{1,0:T(8,128)(2,1)S(1)} %collective-permute-done.2.refs_3_), channel_id=1, source_target_pairs={{0,8},{8,0},{1,9},{9,1},{2,10},{10,2},{3,11},{11,3},{4,12},{12,4},... | collective-permute-start | bytes 589832 | tf_op jit(solution)/shard_map/ppermute | solution.py:28
  28.1 1.7 %collective-permute-start.13 = (bf16[128,768]{1,0:T(8,128)(2,1)S(1)}, bf16[128,768]{1,0:T(8,128)(2,1)S(1)}, u32[]{:S(2)}, u32[]{:S(2)}) collective-permute-start(bf16[128,768]{1,0:T(8,128)(2,1)S(1)} %collective-permute-done.9.refs_2_), channel_id=1, source_target_pairs={{0,8},{8,0},{1,9},{9,1},{2,10},{10,2},{3,11},{11,3},{4,12},{12,4},... | collective-permute-start | bytes 589832 | tf_op jit(solution)/shard_map/ppermute | solution.py:28
  28.6 7.9 %collective-permute-start.14 = (bf16[128,768]{1,0:T(8,128)(2,1)S(1)}, bf16[128,768]{1,0:T(8,128)(2,1)S(1)}, u32[]{:S(2)}, u32[]{:S(2)}) collective-permute-start(bf16[128,768]{1,0:T(8,128)(2,1)S(1)} %collective-permute-done.10.refs_3_), channel_id=1, source_target_pairs={{0,8},{8,0},{1,9},{9,1},{2,10},{10,2},{3,11},{11,3},{4,12},{12,4},... | collective-permute-start | bytes 589832 | tf_op jit(solution)/shard_map/ppermute | solution.py:28
  28.7 8.7 %collective-permute-start.7 = (bf16[128,768]{1,0:T(8,128)(2,1)S(1)}, bf16[128,768]{1,0:T(8,128)(2,1)S(1)}, u32[]{:S(2)}, u32[]{:S(2)}) collective-permute-start(bf16[128,768]{1,0:T(8,128)(2,1)S(1)} %collective-permute-done.5.refs_2_), channel_id=1, source_target_pairs={{0,8},{8,0},{1,9},{9,1},{2,10},{10,2},{3,11},{11,3},{4,12},{12,4},... | collective-permute-start | bytes 589832 | tf_op jit(solution)/shard_map/ppermute | solution.py:28
  29.5 7.9 %collective-permute-start.8 = (bf16[128,768]{1,0:T(8,128)(2,1)S(1)}, bf16[128,768]{1,0:T(8,128)(2,1)S(1)}, u32[]{:S(2)}, u32[]{:S(2)}) collective-permute-start(bf16[128,768]{1,0:T(8,128)(2,1)S(1)} %collective-permute-done.6.refs_3_), channel_id=1, source_target_pairs={{0,8},{8,0},{1,9},{9,1},{2,10},{10,2},{3,11},{11,3},{4,12},{12,4},... | collective-permute-start | bytes 589832 | tf_op jit(solution)/shard_map/ppermute | solution.py:28
  29.7 9.0 %collective-permute-start.15 = (bf16[64,768]{1,0:T(8,128)(2,1)S(1)}, bf16[64,768]{1,0:T(8,128)(2,1)S(1)}, u32[]{:S(2)}, u32[]{:S(2)}) collective-permute-start(bf16[64,768]{1,0:T(8,128)(2,1)S(1)} %slice.8), channel_id=1, source_target_pairs={{0,16},{16,32},{32,48},{48,64},{64,80},{80,96},{96,112},{112,0},{1... | collective-permute-start | bytes 294920 | tf_op jit(solution)/shard_map/ppermute | solution.py:251
  29.8 8.9 %collective-permute-start.16 = (bf16[64,768]{1,0:T(8,128)(2,1)S(1)}, bf16[64,768]{1,0:T(8,128)(2,1)S(1)}, u32[]{:S(2)}, u32[]{:S(2)}) collective-permute-start(bf16[64,768]{1,0:T(8,128)(2,1)S(1)} %slice.9), channel_id=1, source_target_pairs={{0,112},{16,0},{32,16},{48,32},{64,48},{80,64},{96,80},{112,96},{1... | collective-permute-start | bytes 294920 | tf_op jit(solution)/shard_map/ppermute | solution.py:251
  38.8 1.5 %collective-permute-start.17 = (bf16[128,768]{1,0:T(8,128)(2,1)S(1)}, bf16[128,768]{1,0:T(8,128)(2,1)S(1)}, u32[]{:S(2)}, u32[]{:S(2)}) collective-permute-start(bf16[128,768]{1,0:T(8,128)(2,1)S(1)} %pad_maximum_fusion), channel_id=1, source_target_pairs={{0,8},{8,0},{1,9},{9,1},{2,10},{10,2},{3,11},{11,3},{4,12},{12,4},... | collective-permute-start | bytes 589832 | tf_op jit(solution)/shard_map/ppermute | solution.py:28
  41.3 1.3 %collective-permute-start.18 = (f32[16,128]{1,0:T(8,128)S(1)}, f32[16,128]{1,0:T(8,128)S(1)}, u32[]{:S(2)}, u32[]{:S(2)}) collective-permute-start(f32[16,128]{1,0:T(8,128)S(1)} %row_table.1), channel_id=1, source_target_pairs={{0,8},{8,0},{1,9},{9,1},{2,10},{10,2},{3,11},{11,3},{4,12},{12,4},... | collective-permute-start | bytes 24584 | tf_op jit(solution)/shard_map/ppermute | solution.py:28

commit v6 on v5

--- a/solution.py
+++ b/solution.py
@@ -81,12 +81,14 @@
 
 def score_kernel(scale_root, n_parts, n_blocks, *refs):
     parts, blocks = refs[:n_parts], refs[n_parts : n_parts + 2 * n_blocks]
-    rows_ref, lse_ref = refs[n_parts + 2 * n_blocks :][:2]
-    logits_refs = refs[n_parts + 2 * n_blocks + 2 :]
-    at = 0
-    for part in parts:
-        rows_ref[at : at + part.shape[0], :] = part[...]
-        at += part.shape[0]
+    lse_ref, *logits_refs = refs[n_parts + 2 * n_blocks :]
+    rows_ref, at = parts[0], parts[0].shape[0]
+    if n_parts > 1:
+        *logits_refs, rows_ref = logits_refs
+        at = 0
+        for part in parts:
+            rows_ref[at : at + part.shape[0], :] = part[...]
+            at += part.shape[0]
     tile = 256
     for k in range(0, at, tile):
         peak, logits = None, []
@@ -110,19 +112,20 @@
 def score(parts, blocks, scale_root):
     count, depth = sum(p.shape[0] for p in parts), parts[0].shape[1]
     n_cent = blocks[0][0].shape[0]
-    return call(
+    outs = [shape((count // LANES, LANES))] + [shape((n_cent, count))] * len(blocks)
+    if len(parts) > 1:
+        outs.append(shape((count, depth), jnp.bfloat16))
+    found = call(
         functools.partial(score_kernel, scale_root, len(parts), len(blocks)),
-        (
-            shape((count, depth), jnp.bfloat16),
-            shape((count // LANES, LANES)),
-            *[shape((n_cent, count))] * len(blocks),
-        ),
+        tuple(outs),
         (*parts, *(a for block in blocks for a in block)),
         "score",
         2 * n_cent * count * depth * len(blocks),
         n_cent * count * len(blocks),
         SHARE,
     )
+    rows = found[-1] if len(parts) > 1 else parts[0]
+    return rows, found[0], found[1 : 1 + len(blocks)]
 
 
 def table_kernel(orders, *refs):
@@ -242,7 +245,7 @@
     scored, orders = [], []
 
     def scores(order, parts, *blocks):
-        rows, lse, *logits = score(parts, blocks, scale_root)
+        rows, lse, logits = score(parts, blocks, scale_root)
         scored.append(lse)
         orders.append(order)
         return rows, lse, logits

time: 89 us -> 88.2 us (level)
  transfers between devices with their start and end apart: 19 -> 19, of which waited for: 7 -> 7; matrix products, arithmetic and copies ran while one was open for 0% -> 0% of each run, Pallas kernels for 8% -> 7%
where the time goes in v6:
time: 88.2 us; the launch traced here: 88 us
  blocking collectives  39.6 us (45%)
  starting transfers between devices  20.1 us (23%)
  Pallas kernels  13.1 us (15%)
  waiting for transfers between devices  11.1 us (13%)
  local copies, waits for them, and re-layouts  2.79 us (3%)
    all_to_all x1, blocking collectives, local(): came = lax.all_to_all(packed.astype(jnp.float16), OWNERS, 0, 0, tiled=True)  28.3 us
    pallas_call x12, Pallas kernels, call(): pl.pallas_call(kernel, out_shape=outs, in_specs=[VMEM] * len(args), out_s...  13.1 us
    all_to_all x1, blocking collectives, local(): table = joined(*lax.all_to_all(tables, 'z', 0, 0, tiled=True))  11.3 us
    ppermute x3, starting transfers between devices, moved(): lax.ppermute(second, 'z', along_z(-1))  9.69 us
    ppermute x1, starting transfers between devices, local(): down = lax.ppermute(embeddings, 'z', along_z(-1))  5.93 us
    ppermute x1, waiting for transfers between devices, local(): up = lax.ppermute(embeddings, 'z', along_z(1))  3.17 us
    ppermute x9, waiting for transfers between devices, other_core(): return lax.ppermute(array, 'core', [(0, 1), (1, 0)])  2.9 us
    ppermute x3, waiting for transfers between devices, moved(): lax.ppermute(first, 'z', along_z(1))  2.89 us
  transfers between devices with their start and end apart: 19, of which 7 were waited for; matrix products, arithmetic and copies ran while one was open for 0% of the time, Pallas kernels for 7%

profile of v6, /device:TPU:8, one launch (start us, length us, event | category | flops | bytes accessed | tf_op | source)
XLA Modules:
  0.0 88.0 jit_solution(4930816301961333681)
XLA Ops:
  0.6 5.9 %collective-permute-start.2 = (bf16[128,768]{1,0:T(8,128)(2,1)}, bf16[128,768]{1,0:T(8,128)(2,1)S(1)}, u32[]{:S(2)}, u32[]{:S(2)}) collective-permute-start(bf16[128,768]{1,0:T(8,128)(2,1)} %rows_in.1), channel_id=1, source_target_pairs={{0,112},{16,0},{32,16},{48,32},{64,48},{80,64},{96,80},{112,96},{1... | collective-permute-start | bytes 589832 | tf_op jit(solution)/shard_map/ppermute | solution.py:226
  6.6 1.5 %collective-permute-start.11 = (bf16[512,768]{1,0:T(8,128)(2,1)}, bf16[512,768]{1,0:T(8,128)(2,1)S(1)}, u32[]{:S(2)}, u32[]{:S(2)}) collective-permute-start(bf16[512,768]{1,0:T(8,128)(2,1)} %cent_in.1), channel_id=1, source_target_pairs={{0,128},{128,0},{1,129},{129,1},{2,130},{130,2},{3,131},{131,3},{4... | collective-permute-start | bytes 2359304 | tf_op jit(solution)/shard_map/ppermute | solution.py:229
  8.1 1.2 %copy-done = bf16[512,768]{1,0:T(8,128)(2,1)S(1)} copy-done((bf16[512,768]{1,0:T(8,128)(2,1)S(1)}, bf16[512,768]{1,0:T(8,128)(2,1)}, u32[]{:S(2)}) %copy-start) | copy-done | bytes 786456
  9.2 0.9 %copy-done.1 = bf16[128,768]{1,0:T(8,128)(2,1)S(1)} copy-done((bf16[128,768]{1,0:T(8,128)(2,1)S(1)}, bf16[128,768]{1,0:T(8,128)(2,1)}, u32[]{:S(2)}) %copy-start.1) | copy-done | bytes 196632
  11.2 3.2 %collective-permute-done.1.refs_2_ = bf16[128,768]{1,0:T(8,128)(2,1)S(1)} collective-permute-done((bf16[128,768]{1,0:T(8,128)(2,1)}, bf16[128,768]{1,0:T(8,128)(2,1)S(1)}, u32[]{:S(2)}, u32[]{:S(2)}) %collective-permute-start.1) | collective-permute-done | bytes 196640 | tf_op jit(solution)/shard_map/ppermute | solution.py:225
  14.3 3.2 %collective-permute-start.6 = (bf16[128,768]{1,0:T(8,128)(2,1)S(1)}, bf16[128,768]{1,0:T(8,128)(2,1)S(1)}, u32[]{:S(2)}, u32[]{:S(2)}) collective-permute-start(bf16[128,768]{1,0:T(8,128)(2,1)S(1)} %collective-permute-done.2.refs_3_), channel_id=1, source_target_pairs={{0,112},{16,0},{32,16},{48,32},{64,48},{80,64},{96,80},{112,96},{1... | collective-permute-start | bytes 589832 | tf_op jit(solution)/shard_map/ppermute | solution.py:254
  17.6 0.8 score.7
  18.4 2.8 %collective-permute-done.5.refs_2_ = bf16[128,768]{1,0:T(8,128)(2,1)S(1)} collective-permute-done((bf16[128,768]{1,0:T(8,128)(2,1)S(1)}, bf16[128,768]{1,0:T(8,128)(2,1)S(1)}, u32[]{:S(2)}, u32[]{:S(2)}) %collective-permute-start.5) | collective-permute-done | bytes 196640 | tf_op jit(solution)/shard_map/ppermute | solution.py:254
  21.2 3.2 %collective-permute-start.10 = (bf16[128,768]{1,0:T(8,128)(2,1)S(1)}, bf16[128,768]{1,0:T(8,128)(2,1)S(1)}, u32[]{:S(2)}, u32[]{:S(2)}) collective-permute-start(bf16[128,768]{1,0:T(8,128)(2,1)S(1)} %collective-permute-done.6.refs_3_), channel_id=1, source_target_pairs={{0,112},{16,0},{32,16},{48,32},{64,48},{80,64},{96,80},{112,96},{1... | collective-permute-start | bytes 589832 | tf_op jit(solution)/shard_map/ppermute | solution.py:254
  24.5 1.5 %collective-permute-start.12 = (f32[1,512]{1,0:T(1,128)S(1)}, f32[1,512]{1,0:T(1,128)S(1)}, u32[]{:S(2)}, u32[]{:S(2)}) collective-permute-start(f32[1,512]{1,0:T(1,128)S(1)} %bitcast.36), channel_id=1, source_target_pairs={{0,128},{128,0},{1,129},{129,1},{2,130},{130,2},{3,131},{131,3},{4... | collective-permute-start | bytes 6152 | tf_op jit(solution)/shard_map/ppermute | solution.py:230
  26.0 2.1 %collective-permute-done.12.weight_ref = f32[1,512]{1,0:T(1,128)S(1)} collective-permute-done((f32[1,512]{1,0:T(1,128)S(1)}, f32[1,512]{1,0:T(1,128)S(1)}, u32[]{:S(2)}, u32[]{:S(2)}) %collective-permute-start.12) | collective-permute-done | bytes 2080 | tf_op jit(solution)/shard_map/ppermute | solution.py:230
  29.8 3.2 %collective-permute-start.16 = (bf16[64,768]{1,0:T(8,128)(2,1)S(1)}, bf16[64,768]{1,0:T(8,128)(2,1)S(1)}, u32[]{:S(2)}, u32[]{:S(2)}) collective-permute-start(bf16[64,768]{1,0:T(8,128)(2,1)S(1)} %slice.9), channel_id=1, source_target_pairs={{0,112},{16,0},{32,16},{48,32},{64,48},{80,64},{96,80},{112,96},{1... | collective-permute-start | bytes 294920 | tf_op jit(solution)/shard_map/ppermute | solution.py:254
  33.0 0.8 score.8
  34.1 0.8 score.11
  35.0 0.8 score.12
  35.8 0.8 score.10
  36.6 1.4 %score.9 = (f32[4,128]{1,0:T(4,128)S(1)}, f32[512,512]{1,0:T(8,128)S(1)}, f32[512,512]{1,0:T(8,128)S(1)}, bf16[512,768]{1,0:T(8,128)(2,1)S(1)}) custom-call(bf16[128,768]{1,0:T(8,128)(2,1)S(1)} %collective-permute-done.7.refs_0_, bf16[128,768]{1,0:T(8,128)(2,1)S(1)} %collective-permute-done.8.refs_1_, bf16[128,768]{1,0:T(8,128)(2,1)S(1)} %collective-permute-done.9.refs_2_, ...), custom_call_target="tpu_custom_call" | custom-call | flops 201326592 | bytes 1312256 | tf_op jit(solution)/shard_map/score/pallas_call | solution.py:33
  38.1 1.4 %collective-permute-done.17.refs_2_ = bf16[128,768]{1,0:T(8,128)(2,1)S(1)} collective-permute-done((bf16[128,768]{1,0:T(8,128)(2,1)S(1)}, bf16[128,768]{1,0:T(8,128)(2,1)S(1)}, u32[]{:S(2)}, u32[]{:S(2)}) %collective-permute-start.17) | collective-permute-done | bytes 196640 | tf_op jit(solution)/shard_map/ppermute | solution.py:28
  39.5 0.8 score.13
  40.8 1.0 %collective-permute-done.18 = f32[16,128]{1,0:T(8,128)S(1)} collective-permute-done((f32[16,128]{1,0:T(8,128)S(1)}, f32[16,128]{1,0:T(8,128)S(1)}, u32[]{:S(2)}, u32[]{:S(2)}) %collective-permute-start.18) | collective-permute-done | bytes 8224 | tf_op jit(solution)/shard_map/ppermute | solution.py:28
  41.8 11.3 %all_to_all.10 = f32[8,16,128]{2,1,0:T(8,128)S(1)} all-to-all(f32[8,16,128]{2,1,0:T(8,128)S(1)} %broadcast_in_dim.7), channel_id=1, replica_groups=mesh['x_lo'=2,'z'=8,'core'=2,'y'=4,'x_hi'=2] {'z'}, dimensions={0} | all-to-all | bytes 131072 | tf_op jit(solution)/shard_map/all_to_all | solution.py:304
  53.2 5.0 %spread.1 = (f32[16,392,128]{2,1,0:T(8,128)S(1)}, f32[1,128]{1,0:T(1,128)}) custom-call(f32[512,512]{1,0:T(8,128)S(1)} %get-tuple-element.47.refs_0_, f32[512,512]{1,0:T(8,128)S(1)} %get-tuple-element.51.refs_1_, f32[512,512]{1,0:T(8,128)S(1)} %get-tuple-element.54.refs_2_, f32[512,256]{1,0:T(8,128)S(1)} %get-tuple-element.55.refs_3_, ...), custom_call_target="tpu_custom_call" | custom-call | flops 3221225472 | bytes 14754304 | tf_op jit(solution)/shard_map/spread/pallas_call | solution.py:33
  58.4 28.3 %all_to_all.11 = f16[16,392,128]{2,1,0:T(8,128)(2,1)S(1)} all-to-all(f16[16,392,128]{2,1,0:T(8,128)(2,1)S(1)} %convert_element_type.6), channel_id=1, replica_groups=mesh['x_lo'=2,'z'=8,'core'=2,'y'=4,'x_hi'=2] {'x_lo','y','x_hi'}, dimensions={0} | all-to-all | bytes 3211264 | tf_op jit(solution)/shard_map/all_to_all | solution.py:323
  86.9 1.1 %update.1 = (f32[64,768]{1,0:T(8,128)}, f32[1,64]{1,0:T(1,128)}) custom-call(f32[16,392,128]{2,1,0:T(8,128)S(1)} %convert_element_type.7.came_ref, f32[64,768]{1,0:T(8,128)S(1)} %get-tuple-element.44.own_ref), custom_call_target="tpu_custom_call" | custom-call | bytes 3604736 | tf_op jit(solution)/shard_map/update/pallas_call | solution.py:33
  (42 shorter events, 4.0 us)
Async XLA Ops:
  0.6 10.5 %collective-permute-start.2 = (bf16[128,768]{1,0:T(8,128)(2,1)}, bf16[128,768]{1,0:T(8,128)(2,1)S(1)}, u32[]{:S(2)}, u32[]{:S(2)}) collective-permute-start(bf16[128,768]{1,0:T(8,128)(2,1)} %rows_in.1), channel_id=1, source_target_pairs={{0,112},{16,0},{32,16},{48,32},{64,48},{80,64},{96,80},{112,96},{1... | collective-permute-start | bytes 589832 | tf_op jit(solution)/shard_map/ppermute | solution.py:226
  6.6 7.8 %collective-permute-start.1 = (bf16[128,768]{1,0:T(8,128)(2,1)}, bf16[128,768]{1,0:T(8,128)(2,1)S(1)}, u32[]{:S(2)}, u32[]{:S(2)}) collective-permute-start(bf16[128,768]{1,0:T(8,128)(2,1)} %rows_in.1), channel_id=1, source_target_pairs={{0,16},{16,32},{32,48},{48,64},{64,80},{80,96},{96,112},{112,0},{1... | collective-permute-start | bytes 589832 | tf_op jit(solution)/shard_map/ppermute | solution.py:225
  6.6 23.1 %collective-permute-start.11 = (bf16[512,768]{1,0:T(8,128)(2,1)}, bf16[512,768]{1,0:T(8,128)(2,1)S(1)}, u32[]{:S(2)}, u32[]{:S(2)}) collective-permute-start(bf16[512,768]{1,0:T(8,128)(2,1)} %cent_in.1), channel_id=1, source_target_pairs={{0,128},{128,0},{1,129},{129,1},{2,130},{130,2},{3,131},{131,3},{4... | collective-permute-start | bytes 2359304 | tf_op jit(solution)/shard_map/ppermute | solution.py:229
  8.1 9.5 %collective-permute-start = (bf16[128,768]{1,0:T(8,128)(2,1)}, bf16[128,768]{1,0:T(8,128)(2,1)S(1)}, u32[]{:S(2)}, u32[]{:S(2)}) collective-permute-start(bf16[128,768]{1,0:T(8,128)(2,1)} %rows_in.1), channel_id=1, source_target_pairs={{0,8},{8,0},{1,9},{9,1},{2,10},{10,2},{3,11},{11,3},{4,12},{12,4},... | collective-permute-start | bytes 589832 | tf_op jit(solution)/shard_map/ppermute | solution.py:28
  8.1 1.2 %copy-start = (bf16[512,768]{1,0:T(8,128)(2,1)S(1)}, bf16[512,768]{1,0:T(8,128)(2,1)}, u32[]{:S(2)}) copy-start(bf16[512,768]{1,0:T(8,128)(2,1)} %cent_in.1) | copy-start | bytes 2359300
  9.2 0.9 %copy-start.1 = (bf16[128,768]{1,0:T(8,128)(2,1)S(1)}, bf16[128,768]{1,0:T(8,128)(2,1)}, u32[]{:S(2)}) copy-start(bf16[128,768]{1,0:T(8,128)(2,1)} %rows_in.1) | copy-start | bytes 589828
  10.2 0.7 copy-start.2
  14.3 6.9 %collective-permute-start.5 = (bf16[128,768]{1,0:T(8,128)(2,1)S(1)}, bf16[128,768]{1,0:T(8,128)(2,1)S(1)}, u32[]{:S(2)}, u32[]{:S(2)}) collective-permute-start(bf16[128,768]{1,0:T(8,128)(2,1)S(1)} %collective-permute-done.1.refs_2_), channel_id=1, source_target_pairs={{0,16},{16,32},{32,48},{48,64},{64,80},{80,96},{96,112},{112,0},{1... | collective-permute-start | bytes 589832 | tf_op jit(solution)/shard_map/ppermute | solution.py:254
  14.3 6.9 %collective-permute-start.6 = (bf16[128,768]{1,0:T(8,128)(2,1)S(1)}, bf16[128,768]{1,0:T(8,128)(2,1)S(1)}, u32[]{:S(2)}, u32[]{:S(2)}) collective-permute-start(bf16[128,768]{1,0:T(8,128)(2,1)S(1)} %collective-permute-done.2.refs_3_), channel_id=1, source_target_pairs={{0,112},{16,0},{32,16},{48,32},{64,48},{80,64},{96,80},{112,96},{1... | collective-permute-start | bytes 589832 | tf_op jit(solution)/shard_map/ppermute | solution.py:254
  21.2 6.9 %collective-permute-start.9 = (bf16[128,768]{1,0:T(8,128)(2,1)S(1)}, bf16[128,768]{1,0:T(8,128)(2,1)S(1)}, u32[]{:S(2)}, u32[]{:S(2)}) collective-permute-start(bf16[128,768]{1,0:T(8,128)(2,1)S(1)} %collective-permute-done.5.refs_2_), channel_id=1, source_target_pairs={{0,16},{16,32},{32,48},{48,64},{64,80},{80,96},{96,112},{112,0},{1... | collective-permute-start | bytes 589832 | tf_op jit(solution)/shard_map/ppermute | solution.py:254
  21.2 7.3 %collective-permute-start.10 = (bf16[128,768]{1,0:T(8,128)(2,1)S(1)}, bf16[128,768]{1,0:T(8,128)(2,1)S(1)}, u32[]{:S(2)}, u32[]{:S(2)}) collective-permute-start(bf16[128,768]{1,0:T(8,128)(2,1)S(1)} %collective-permute-done.6.refs_3_), channel_id=1, source_target_pairs={{0,112},{16,0},{32,16},{48,32},{64,48},{80,64},{96,80},{112,96},{1... | collective-permute-start | bytes 589832 | tf_op jit(solution)/shard_map/ppermute | solution.py:254
  24.5 3.6 %collective-permute-start.12 = (f32[1,512]{1,0:T(1,128)S(1)}, f32[1,512]{1,0:T(1,128)S(1)}, u32[]{:S(2)}, u32[]{:S(2)}) collective-permute-start(f32[1,512]{1,0:T(1,128)S(1)} %bitcast.36), channel_id=1, source_target_pairs={{0,128},{128,0},{1,129},{129,1},{2,130},{130,2},{3,131},{131,3},{4... | collective-permute-start | bytes 6152 | tf_op jit(solution)/shard_map/ppermute | solution.py:230
  26.0 2.7 %collective-permute-start.3 = (bf16[128,768]{1,0:T(8,128)(2,1)S(1)}, bf16[128,768]{1,0:T(8,128)(2,1)S(1)}, u32[]{:S(2)}, u32[]{:S(2)}) collective-permute-start(bf16[128,768]{1,0:T(8,128)(2,1)S(1)} %collective-permute-done.1.refs_2_), channel_id=1, source_target_pairs={{0,8},{8,0},{1,9},{9,1},{2,10},{10,2},{3,11},{11,3},{4,12},{12,4},... | collective-permute-start | bytes 589832 | tf_op jit(solution)/shard_map/ppermute | solution.py:28
  28.1 1.4 %collective-permute-start.4 = (bf16[128,768]{1,0:T(8,128)(2,1)S(1)}, bf16[128,768]{1,0:T(8,128)(2,1)S(1)}, u32[]{:S(2)}, u32[]{:S(2)}) collective-permute-start(bf16[128,768]{1,0:T(8,128)(2,1)S(1)} %collective-permute-done.2.refs_3_), channel_id=1, source_target_pairs={{0,8},{8,0},{1,9},{9,1},{2,10},{10,2},{3,11},{11,3},{4,12},{12,4},... | collective-permute-start | bytes 589832 | tf_op jit(solution)/shard_map/ppermute | solution.py:28
  28.1 1.7 %collective-permute-start.13 = (bf16[128,768]{1,0:T(8,128)(2,1)S(1)}, bf16[128,768]{1,0:T(8,128)(2,1)S(1)}, u32[]{:S(2)}, u32[]{:S(2)}) collective-permute-start(bf16[128,768]{1,0:T(8,128)(2,1)S(1)} %collective-permute-done.9.refs_2_), channel_id=1, source_target_pairs={{0,8},{8,0},{1,9},{9,1},{2,10},{10,2},{3,11},{11,3},{4,12},{12,4},... | collective-permute-start | bytes 589832 | tf_op jit(solution)/shard_map/ppermute | solution.py:28
  28.6 7.2 %collective-permute-start.14 = (bf16[128,768]{1,0:T(8,128)(2,1)S(1)}, bf16[128,768]{1,0:T(8,128)(2,1)S(1)}, u32[]{:S(2)}, u32[]{:S(2)}) collective-permute-start(bf16[128,768]{1,0:T(8,128)(2,1)S(1)} %collective-permute-done.10.refs_3_), channel_id=1, source_target_pairs={{0,8},{8,0},{1,9},{9,1},{2,10},{10,2},{3,11},{11,3},{4,12},{12,4},... | collective-permute-start | bytes 589832 | tf_op jit(solution)/shard_map/ppermute | solution.py:28
  28.7 7.9 %collective-permute-start.7 = (bf16[128,768]{1,0:T(8,128)(2,1)S(1)}, bf16[128,768]{1,0:T(8,128)(2,1)S(1)}, u32[]{:S(2)}, u32[]{:S(2)}) collective-permute-start(bf16[128,768]{1,0:T(8,128)(2,1)S(1)} %collective-permute-done.5.refs_2_), channel_id=1, source_target_pairs={{0,8},{8,0},{1,9},{9,1},{2,10},{10,2},{3,11},{11,3},{4,12},{12,4},... | collective-permute-start | bytes 589832 | tf_op jit(solution)/shard_map/ppermute | solution.py:28
  29.5 7.1 %collective-permute-start.8 = (bf16[128,768]{1,0:T(8,128)(2,1)S(1)}, bf16[128,768]{1,0:T(8,128)(2,1)S(1)}, u32[]{:S(2)}, u32[]{:S(2)}) collective-permute-start(bf16[128,768]{1,0:T(8,128)(2,1)S(1)} %collective-permute-done.6.refs_3_), channel_id=1, source_target_pairs={{0,8},{8,0},{1,9},{9,1},{2,10},{10,2},{3,11},{11,3},{4,12},{12,4},... | collective-permute-start | bytes 589832 | tf_op jit(solution)/shard_map/ppermute | solution.py:28
  29.7 8.3 %collective-permute-start.15 = (bf16[64,768]{1,0:T(8,128)(2,1)S(1)}, bf16[64,768]{1,0:T(8,128)(2,1)S(1)}, u32[]{:S(2)}, u32[]{:S(2)}) collective-permute-start(bf16[64,768]{1,0:T(8,128)(2,1)S(1)} %slice.8), channel_id=1, source_target_pairs={{0,16},{16,32},{32,48},{48,64},{64,80},{80,96},{96,112},{112,0},{1... | collective-permute-start | bytes 294920 | tf_op jit(solution)/shard_map/ppermute | solution.py:254
  29.8 8.2 %collective-permute-start.16 = (bf16[64,768]{1,0:T(8,128)(2,1)S(1)}, bf16[64,768]{1,0:T(8,128)(2,1)S(1)}, u32[]{:S(2)}, u32[]{:S(2)}) collective-permute-start(bf16[64,768]{1,0:T(8,128)(2,1)S(1)} %slice.9), channel_id=1, source_target_pairs={{0,112},{16,0},{32,16},{48,32},{64,48},{80,64},{96,80},{112,96},{1... | collective-permute-start | bytes 294920 | tf_op jit(solution)/shard_map/ppermute | solution.py:254
  38.0 1.5 %collective-permute-start.17 = (bf16[128,768]{1,0:T(8,128)(2,1)S(1)}, bf16[128,768]{1,0:T(8,128)(2,1)S(1)}, u32[]{:S(2)}, u32[]{:S(2)}) collective-permute-start(bf16[128,768]{1,0:T(8,128)(2,1)S(1)} %pad_maximum_fusion), channel_id=1, source_target_pairs={{0,8},{8,0},{1,9},{9,1},{2,10},{10,2},{3,11},{11,3},{4,12},{12,4},... | collective-permute-start | bytes 589832 | tf_op jit(solution)/shard_map/ppermute | solution.py:28
  40.5 1.3 %collective-permute-start.18 = (f32[16,128]{1,0:T(8,128)S(1)}, f32[16,128]{1,0:T(8,128)S(1)}, u32[]{:S(2)}, u32[]{:S(2)}) collective-permute-start(f32[16,128]{1,0:T(8,128)S(1)} %row_table.1), channel_id=1, source_target_pairs={{0,8},{8,0},{1,9},{9,1},{2,10},{10,2},{3,11},{11,3},{4,12},{12,4},... | collective-permute-start | bytes 24584 | tf_op jit(solution)/shard_map/ppermute | solution.py:28

commit v7 on v6

--- a/solution.py
+++ b/solution.py
@@ -151,14 +151,15 @@
     tile, depth = logits[0][0].shape[0], rows[0].shape[1]
     owned = 2 * tile // N_OWNERS
     x_lo = lax.axis_index("x_lo")
-    for block in range(2):
-        first = lax.rem(x_lo + block, 2) * (tile // owned)
+    part_tile = tile // 2
+    for block, k in ((0, 0), (0, part_tile), (1, 0), (1, part_tile)):
+        first = lax.rem(x_lo + block, 2) * (tile // owned) + k // owned
         total, count = None, None
         for order, logits_ref, rows_ref in zip(orders, logits[block], rows):
             resp = []
             for i, (dist, side) in enumerate(order):
                 norm = norm_ref[pl.ds(row_of(dist)[side], 1), :]
-                r = jnp.exp(logits_ref[:, i * LANES : (i + 1) * LANES] - norm)
+                r = jnp.exp(logits_ref[k : k + part_tile, i * LANES : (i + 1) * LANES] - norm)
                 count = r if count is None else count + r
                 resp.append(r.astype(jnp.bfloat16))
             part = jnp.dot(
@@ -172,13 +173,13 @@
         high = count.astype(jnp.bfloat16).astype(jnp.float32)
         middle = (count - high).astype(jnp.bfloat16).astype(jnp.float32)
         low = count - high - middle
-        lane = lax.broadcasted_iota(jnp.int32, (tile, LANES), 1)
-        extra = jnp.zeros((tile, LANES), jnp.float32)
+        lane = lax.broadcasted_iota(jnp.int32, (part_tile, LANES), 1)
+        extra = jnp.zeros((part_tile, LANES), jnp.float32)
         for i, value in enumerate((scale, high, middle * 2.0**8, low * 2.0**16)):
             extra = jnp.where(lane == i, value, extra)
         extra = extra.T[:EXTRA, :]
         at = depth // LANES * owned
-        for b in range(tile // owned):
+        for b in range(part_tile // owned):
             owner = first + b
             for j in range(depth // LANES):
                 packed_ref[owner, j * owned : (j + 1) * owned, :] = total[
@@ -268,7 +269,7 @@
     side = [other_core(up), other_core(down)]
     up, down = moved(up, down)
     rows2, lse, (near2,) = scores(order2, second, here)
-    cents_beside, weight_beside = lax.optimization_barrier((cents_beside, weight_beside, up))[:2]
+    cents_beside, weight_beside = lax.optimization_barrier((cents_beside, weight_beside, up, down))[:2]
     (bias_beside,) = call(
         functools.partial(other_kernel, scale_root),
         (shape((local_count, 1)),),
@@ -286,7 +287,7 @@
     rows3, lse3, (near3, far3) = scores(order3, third, here, there)
     rows4, lse4, (near4, far4) = scores(pair(3, 1), side, here, there)
     up, down = lax.optimization_barrier((up, down, lse1, lse2, lse3, lse4))[:2]
-    last = [up, down, other_core(jnp.concatenate([up, down]))]
+    last = [up, down, other_core(up), other_core(down)]
     rows5, _, (near5, far5) = scores([(4, 0), (4, 1)], last, here, there)
     groups = [
         (order1, rows1, near1, far1),

time: 88.2 us -> 88.1 us (level)
    ppermute x9 -> x10, starting transfers between devices: 1.43 us -> 2.15 us  [other_core(): return lax.ppermute(array, 'core', [(0, 1), (1, 0)])]
    ppermute x9 -> x10, waiting for transfers between devices: 2.9 us -> 2.21 us  [other_core(): return lax.ppermute(array, 'core', [(0, 1), (1, 0)])]
  transfers between devices with their start and end apart: 19 -> 20, of which waited for: 7 -> 8; matrix products, arithmetic and copies ran while one was open for 0% -> 0% of each run, Pallas kernels for 7% -> 7%
where the time goes in v7:
time: 88.1 us; the launch traced here: 87.8 us
  blocking collectives  39.6 us (45%)
  starting transfers between devices  20.8 us (24%)
  Pallas kernels  13 us (15%)
  waiting for transfers between devices  10.4 us (12%)
  local copies, waits for them, and re-layouts  2.79 us (3%)
    all_to_all x1, blocking collectives, local(): came = lax.all_to_all(packed.astype(jnp.float16), OWNERS, 0, 0, tiled=True)  28.3 us
    pallas_call x12, Pallas kernels, call(): pl.pallas_call(kernel, out_shape=outs, in_specs=[VMEM] * len(args), out_s...  13 us
    all_to_all x1, blocking collectives, local(): table = joined(*lax.all_to_all(tables, 'z', 0, 0, tiled=True))  11.4 us
    ppermute x3, starting transfers between devices, moved(): lax.ppermute(second, 'z', along_z(-1))  9.69 us
    ppermute x1, starting transfers between devices, local(): down = lax.ppermute(embeddings, 'z', along_z(-1))  5.93 us
    ppermute x1, waiting for transfers between devices, local(): up = lax.ppermute(embeddings, 'z', along_z(1))  3.17 us
    ppermute x3, waiting for transfers between devices, moved(): lax.ppermute(first, 'z', along_z(1))  2.89 us
    unnamed x6, local copies, waits for them, and re-layouts  2.77 us
  transfers between devices with their start and end apart: 20, of which 8 were waited for; matrix products, arithmetic and copies ran while one was open for 0% of the time, Pallas kernels for 7%

profile of v7, /device:TPU:8, one launch (start us, length us, event | category | flops | bytes accessed | tf_op | source)
XLA Modules:
  0.0 87.8 jit_solution(5650919762643351557)
XLA Ops:
  0.6 5.9 %collective-permute-start.2 = (bf16[128,768]{1,0:T(8,128)(2,1)}, bf16[128,768]{1,0:T(8,128)(2,1)S(1)}, u32[]{:S(2)}, u32[]{:S(2)}) collective-permute-start(bf16[128,768]{1,0:T(8,128)(2,1)} %rows_in.1), channel_id=1, source_target_pairs={{0,112},{16,0},{32,16},{48,32},{64,48},{80,64},{96,80},{112,96},{1... | collective-permute-start | bytes 589832 | tf_op jit(solution)/shard_map/ppermute | solution.py:227
  6.6 1.5 %collective-permute-start.11 = (bf16[512,768]{1,0:T(8,128)(2,1)}, bf16[512,768]{1,0:T(8,128)(2,1)S(1)}, u32[]{:S(2)}, u32[]{:S(2)}) collective-permute-start(bf16[512,768]{1,0:T(8,128)(2,1)} %cent_in.1), channel_id=1, source_target_pairs={{0,128},{128,0},{1,129},{129,1},{2,130},{130,2},{3,131},{131,3},{4... | collective-permute-start | bytes 2359304 | tf_op jit(solution)/shard_map/ppermute | solution.py:230
  8.1 1.2 %copy-done = bf16[512,768]{1,0:T(8,128)(2,1)S(1)} copy-done((bf16[512,768]{1,0:T(8,128)(2,1)S(1)}, bf16[512,768]{1,0:T(8,128)(2,1)}, u32[]{:S(2)}) %copy-start) | copy-done | bytes 786456
  9.2 0.9 %copy-done.1 = bf16[128,768]{1,0:T(8,128)(2,1)S(1)} copy-done((bf16[128,768]{1,0:T(8,128)(2,1)S(1)}, bf16[128,768]{1,0:T(8,128)(2,1)}, u32[]{:S(2)}) %copy-start.1) | copy-done | bytes 196632
  11.2 3.2 %collective-permute-done.1.refs_2_ = bf16[128,768]{1,0:T(8,128)(2,1)S(1)} collective-permute-done((bf16[128,768]{1,0:T(8,128)(2,1)}, bf16[128,768]{1,0:T(8,128)(2,1)S(1)}, u32[]{:S(2)}, u32[]{:S(2)}) %collective-permute-start.1) | collective-permute-done | bytes 196640 | tf_op jit(solution)/shard_map/ppermute | solution.py:226
  14.3 3.2 %collective-permute-start.6 = (bf16[128,768]{1,0:T(8,128)(2,1)S(1)}, bf16[128,768]{1,0:T(8,128)(2,1)S(1)}, u32[]{:S(2)}, u32[]{:S(2)}) collective-permute-start(bf16[128,768]{1,0:T(8,128)(2,1)S(1)} %collective-permute-done.2.refs_3_), channel_id=1, source_target_pairs={{0,112},{16,0},{32,16},{48,32},{64,48},{80,64},{96,80},{112,96},{1... | collective-permute-start | bytes 589832 | tf_op jit(solution)/shard_map/ppermute | solution.py:255
  17.6 0.8 score.7
  18.4 2.8 %collective-permute-done.5.refs_2_ = bf16[128,768]{1,0:T(8,128)(2,1)S(1)} collective-permute-done((bf16[128,768]{1,0:T(8,128)(2,1)S(1)}, bf16[128,768]{1,0:T(8,128)(2,1)S(1)}, u32[]{:S(2)}, u32[]{:S(2)}) %collective-permute-start.5) | collective-permute-done | bytes 196640 | tf_op jit(solution)/shard_map/ppermute | solution.py:255
  21.2 3.2 %collective-permute-start.10 = (bf16[128,768]{1,0:T(8,128)(2,1)S(1)}, bf16[128,768]{1,0:T(8,128)(2,1)S(1)}, u32[]{:S(2)}, u32[]{:S(2)}) collective-permute-start(bf16[128,768]{1,0:T(8,128)(2,1)S(1)} %collective-permute-done.6.refs_3_), channel_id=1, source_target_pairs={{0,112},{16,0},{32,16},{48,32},{64,48},{80,64},{96,80},{112,96},{1... | collective-permute-start | bytes 589832 | tf_op jit(solution)/shard_map/ppermute | solution.py:255
  24.5 1.5 %collective-permute-start.12 = (f32[1,512]{1,0:T(1,128)S(1)}, f32[1,512]{1,0:T(1,128)S(1)}, u32[]{:S(2)}, u32[]{:S(2)}) collective-permute-start(f32[1,512]{1,0:T(1,128)S(1)} %bitcast.36), channel_id=1, source_target_pairs={{0,128},{128,0},{1,129},{129,1},{2,130},{130,2},{3,131},{131,3},{4... | collective-permute-start | bytes 6152 | tf_op jit(solution)/shard_map/ppermute | solution.py:231
  26.0 2.1 %collective-permute-done.12.weight_ref = f32[1,512]{1,0:T(1,128)S(1)} collective-permute-done((f32[1,512]{1,0:T(1,128)S(1)}, f32[1,512]{1,0:T(1,128)S(1)}, u32[]{:S(2)}, u32[]{:S(2)}) %collective-permute-start.12) | collective-permute-done | bytes 2080 | tf_op jit(solution)/shard_map/ppermute | solution.py:231
  29.8 3.2 %collective-permute-start.16 = (bf16[64,768]{1,0:T(8,128)(2,1)S(1)}, bf16[64,768]{1,0:T(8,128)(2,1)S(1)}, u32[]{:S(2)}, u32[]{:S(2)}) collective-permute-start(bf16[64,768]{1,0:T(8,128)(2,1)S(1)} %slice.9), channel_id=1, source_target_pairs={{0,112},{16,0},{32,16},{48,32},{64,48},{80,64},{96,80},{112,96},{1... | collective-permute-start | bytes 294920 | tf_op jit(solution)/shard_map/ppermute | solution.py:255
  33.0 0.8 score.8
  34.1 0.8 score.11
  35.0 0.8 score.12
  35.8 0.8 score.10
  36.6 1.4 %score.9 = (f32[4,128]{1,0:T(4,128)S(1)}, f32[512,512]{1,0:T(8,128)S(1)}, f32[512,512]{1,0:T(8,128)S(1)}, bf16[512,768]{1,0:T(8,128)(2,1)S(1)}) custom-call(bf16[128,768]{1,0:T(8,128)(2,1)S(1)} %collective-permute-done.7.refs_0_, bf16[128,768]{1,0:T(8,128)(2,1)S(1)} %collective-permute-done.8.refs_1_, bf16[128,768]{1,0:T(8,128)(2,1)S(1)} %collective-permute-done.9.refs_2_, ...), custom_call_target="tpu_custom_call" | custom-call | flops 201326592 | bytes 1312256 | tf_op jit(solution)/shard_map/score/pallas_call | solution.py:33
  38.6 0.8 collective-permute-done.17.refs_2_
  39.5 0.8 score.13
  41.0 0.8 collective-permute-done.19
  41.8 11.4 %all_to_all.10 = f32[8,16,128]{2,1,0:T(8,128)S(1)} all-to-all(f32[8,16,128]{2,1,0:T(8,128)S(1)} %broadcast_in_dim.7), channel_id=1, replica_groups=mesh['x_lo'=2,'z'=8,'core'=2,'y'=4,'x_hi'=2] {'z'}, dimensions={0} | all-to-all | bytes 131072 | tf_op jit(solution)/shard_map/all_to_all | solution.py:305
  53.2 4.8 %spread.1 = (f32[16,392,128]{2,1,0:T(8,128)S(1)}, f32[1,128]{1,0:T(1,128)}) custom-call(f32[512,512]{1,0:T(8,128)S(1)} %get-tuple-element.47.refs_0_, f32[512,512]{1,0:T(8,128)S(1)} %get-tuple-element.51.refs_1_, f32[512,512]{1,0:T(8,128)S(1)} %get-tuple-element.54.refs_2_, f32[512,256]{1,0:T(8,128)S(1)} %get-tuple-element.55.refs_3_, ...), custom_call_target="tpu_custom_call" | custom-call | flops 3221225472 | bytes 14754304 | tf_op jit(solution)/shard_map/spread/pallas_call | solution.py:33
  58.2 28.3 %all_to_all.11 = f16[16,392,128]{2,1,0:T(8,128)(2,1)S(1)} all-to-all(f16[16,392,128]{2,1,0:T(8,128)(2,1)S(1)} %convert_element_type.6), channel_id=1, replica_groups=mesh['x_lo'=2,'z'=8,'core'=2,'y'=4,'x_hi'=2] {'x_lo','y','x_hi'}, dimensions={0} | all-to-all | bytes 3211264 | tf_op jit(solution)/shard_map/all_to_all | solution.py:324
  86.7 1.1 %update.1 = (f32[64,768]{1,0:T(8,128)}, f32[1,64]{1,0:T(1,128)}) custom-call(f32[16,392,128]{2,1,0:T(8,128)S(1)} %convert_element_type.7.came_ref, f32[64,768]{1,0:T(8,128)S(1)} %get-tuple-element.44.own_ref), custom_call_target="tpu_custom_call" | custom-call | bytes 3604736 | tf_op jit(solution)/shard_map/update/pallas_call | solution.py:33
  (43 shorter events, 4.9 us)
Async XLA Ops:
  0.6 10.5 %collective-permute-start.2 = (bf16[128,768]{1,0:T(8,128)(2,1)}, bf16[128,768]{1,0:T(8,128)(2,1)S(1)}, u32[]{:S(2)}, u32[]{:S(2)}) collective-permute-start(bf16[128,768]{1,0:T(8,128)(2,1)} %rows_in.1), channel_id=1, source_target_pairs={{0,112},{16,0},{32,16},{48,32},{64,48},{80,64},{96,80},{112,96},{1... | collective-permute-start | bytes 589832 | tf_op jit(solution)/shard_map/ppermute | solution.py:227
  6.6 7.8 %collective-permute-start.1 = (bf16[128,768]{1,0:T(8,128)(2,1)}, bf16[128,768]{1,0:T(8,128)(2,1)S(1)}, u32[]{:S(2)}, u32[]{:S(2)}) collective-permute-start(bf16[128,768]{1,0:T(8,128)(2,1)} %rows_in.1), channel_id=1, source_target_pairs={{0,16},{16,32},{32,48},{48,64},{64,80},{80,96},{96,112},{112,0},{1... | collective-permute-start | bytes 589832 | tf_op jit(solution)/shard_map/ppermute | solution.py:226
  6.6 23.1 %collective-permute-start.11 = (bf16[512,768]{1,0:T(8,128)(2,1)}, bf16[512,768]{1,0:T(8,128)(2,1)S(1)}, u32[]{:S(2)}, u32[]{:S(2)}) collective-permute-start(bf16[512,768]{1,0:T(8,128)(2,1)} %cent_in.1), channel_id=1, source_target_pairs={{0,128},{128,0},{1,129},{129,1},{2,130},{130,2},{3,131},{131,3},{4... | collective-permute-start | bytes 2359304 | tf_op jit(solution)/shard_map/ppermute | solution.py:230
  8.1 9.5 %collective-permute-start = (bf16[128,768]{1,0:T(8,128)(2,1)}, bf16[128,768]{1,0:T(8,128)(2,1)S(1)}, u32[]{:S(2)}, u32[]{:S(2)}) collective-permute-start(bf16[128,768]{1,0:T(8,128)(2,1)} %rows_in.1), channel_id=1, source_target_pairs={{0,8},{8,0},{1,9},{9,1},{2,10},{10,2},{3,11},{11,3},{4,12},{12,4},... | collective-permute-start | bytes 589832 | tf_op jit(solution)/shard_map/ppermute | solution.py:28
  8.1 1.2 %copy-start = (bf16[512,768]{1,0:T(8,128)(2,1)S(1)}, bf16[512,768]{1,0:T(8,128)(2,1)}, u32[]{:S(2)}) copy-start(bf16[512,768]{1,0:T(8,128)(2,1)} %cent_in.1) | copy-start | bytes 2359300
  9.2 0.9 %copy-start.1 = (bf16[128,768]{1,0:T(8,128)(2,1)S(1)}, bf16[128,768]{1,0:T(8,128)(2,1)}, u32[]{:S(2)}) copy-start(bf16[128,768]{1,0:T(8,128)(2,1)} %rows_in.1) | copy-start | bytes 589828
  10.2 0.7 copy-start.2
  14.3 6.9 %collective-permute-start.5 = (bf16[128,768]{1,0:T(8,128)(2,1)S(1)}, bf16[128,768]{1,0:T(8,128)(2,1)S(1)}, u32[]{:S(2)}, u32[]{:S(2)}) collective-permute-start(bf16[128,768]{1,0:T(8,128)(2,1)S(1)} %collective-permute-done.1.refs_2_), channel_id=1, source_target_pairs={{0,16},{16,32},{32,48},{48,64},{64,80},{80,96},{96,112},{112,0},{1... | collective-permute-start | bytes 589832 | tf_op jit(solution)/shard_map/ppermute | solution.py:255
  14.3 6.9 %collective-permute-start.6 = (bf16[128,768]{1,0:T(8,128)(2,1)S(1)}, bf16[128,768]{1,0:T(8,128)(2,1)S(1)}, u32[]{:S(2)}, u32[]{:S(2)}) collective-permute-start(bf16[128,768]{1,0:T(8,128)(2,1)S(1)} %collective-permute-done.2.refs_3_), channel_id=1, source_target_pairs={{0,112},{16,0},{32,16},{48,32},{64,48},{80,64},{96,80},{112,96},{1... | collective-permute-start | bytes 589832 | tf_op jit(solution)/shard_map/ppermute | solution.py:255
  21.2 6.9 %collective-permute-start.9 = (bf16[128,768]{1,0:T(8,128)(2,1)S(1)}, bf16[128,768]{1,0:T(8,128)(2,1)S(1)}, u32[]{:S(2)}, u32[]{:S(2)}) collective-permute-start(bf16[128,768]{1,0:T(8,128)(2,1)S(1)} %collective-permute-done.5.refs_2_), channel_id=1, source_target_pairs={{0,16},{16,32},{32,48},{48,64},{64,80},{80,96},{96,112},{112,0},{1... | collective-permute-start | bytes 589832 | tf_op jit(solution)/shard_map/ppermute | solution.py:255
  21.2 7.3 %collective-permute-start.10 = (bf16[128,768]{1,0:T(8,128)(2,1)S(1)}, bf16[128,768]{1,0:T(8,128)(2,1)S(1)}, u32[]{:S(2)}, u32[]{:S(2)}) collective-permute-start(bf16[128,768]{1,0:T(8,128)(2,1)S(1)} %collective-permute-done.6.refs_3_), channel_id=1, source_target_pairs={{0,112},{16,0},{32,16},{48,32},{64,48},{80,64},{96,80},{112,96},{1... | collective-permute-start | bytes 589832 | tf_op jit(solution)/shard_map/ppermute | solution.py:255
  24.5 3.6 %collective-permute-start.12 = (f32[1,512]{1,0:T(1,128)S(1)}, f32[1,512]{1,0:T(1,128)S(1)}, u32[]{:S(2)}, u32[]{:S(2)}) collective-permute-start(f32[1,512]{1,0:T(1,128)S(1)} %bitcast.36), channel_id=1, source_target_pairs={{0,128},{128,0},{1,129},{129,1},{2,130},{130,2},{3,131},{131,3},{4... | collective-permute-start | bytes 6152 | tf_op jit(solution)/shard_map/ppermute | solution.py:231
  26.0 2.7 %collective-permute-start.3 = (bf16[128,768]{1,0:T(8,128)(2,1)S(1)}, bf16[128,768]{1,0:T(8,128)(2,1)S(1)}, u32[]{:S(2)}, u32[]{:S(2)}) collective-permute-start(bf16[128,768]{1,0:T(8,128)(2,1)S(1)} %collective-permute-done.1.refs_2_), channel_id=1, source_target_pairs={{0,8},{8,0},{1,9},{9,1},{2,10},{10,2},{3,11},{11,3},{4,12},{12,4},... | collective-permute-start | bytes 589832 | tf_op jit(solution)/shard_map/ppermute | solution.py:28
  28.1 1.4 %collective-permute-start.4 = (bf16[128,768]{1,0:T(8,128)(2,1)S(1)}, bf16[128,768]{1,0:T(8,128)(2,1)S(1)}, u32[]{:S(2)}, u32[]{:S(2)}) collective-permute-start(bf16[128,768]{1,0:T(8,128)(2,1)S(1)} %collective-permute-done.2.refs_3_), channel_id=1, source_target_pairs={{0,8},{8,0},{1,9},{9,1},{2,10},{10,2},{3,11},{11,3},{4,12},{12,4},... | collective-permute-start | bytes 589832 | tf_op jit(solution)/shard_map/ppermute | solution.py:28
  28.1 1.7 %collective-permute-start.13 = (bf16[128,768]{1,0:T(8,128)(2,1)S(1)}, bf16[128,768]{1,0:T(8,128)(2,1)S(1)}, u32[]{:S(2)}, u32[]{:S(2)}) collective-permute-start(bf16[128,768]{1,0:T(8,128)(2,1)S(1)} %collective-permute-done.9.refs_2_), channel_id=1, source_target_pairs={{0,8},{8,0},{1,9},{9,1},{2,10},{10,2},{3,11},{11,3},{4,12},{12,4},... | collective-permute-start | bytes 589832 | tf_op jit(solution)/shard_map/ppermute | solution.py:28
  28.6 7.2 %collective-permute-start.14 = (bf16[128,768]{1,0:T(8,128)(2,1)S(1)}, bf16[128,768]{1,0:T(8,128)(2,1)S(1)}, u32[]{:S(2)}, u32[]{:S(2)}) collective-permute-start(bf16[128,768]{1,0:T(8,128)(2,1)S(1)} %collective-permute-done.10.refs_3_), channel_id=1, source_target_pairs={{0,8},{8,0},{1,9},{9,1},{2,10},{10,2},{3,11},{11,3},{4,12},{12,4},... | collective-permute-start | bytes 589832 | tf_op jit(solution)/shard_map/ppermute | solution.py:28
  28.7 7.9 %collective-permute-start.7 = (bf16[128,768]{1,0:T(8,128)(2,1)S(1)}, bf16[128,768]{1,0:T(8,128)(2,1)S(1)}, u32[]{:S(2)}, u32[]{:S(2)}) collective-permute-start(bf16[128,768]{1,0:T(8,128)(2,1)S(1)} %collective-permute-done.5.refs_2_), channel_id=1, source_target_pairs={{0,8},{8,0},{1,9},{9,1},{2,10},{10,2},{3,11},{11,3},{4,12},{12,4},... | collective-permute-start | bytes 589832 | tf_op jit(solution)/shard_map/ppermute | solution.py:28
  29.5 7.1 %collective-permute-start.8 = (bf16[128,768]{1,0:T(8,128)(2,1)S(1)}, bf16[128,768]{1,0:T(8,128)(2,1)S(1)}, u32[]{:S(2)}, u32[]{:S(2)}) collective-permute-start(bf16[128,768]{1,0:T(8,128)(2,1)S(1)} %collective-permute-done.6.refs_3_), channel_id=1, source_target_pairs={{0,8},{8,0},{1,9},{9,1},{2,10},{10,2},{3,11},{11,3},{4,12},{12,4},... | collective-permute-start | bytes 589832 | tf_op jit(solution)/shard_map/ppermute | solution.py:28
  29.7 8.3 %collective-permute-start.15 = (bf16[64,768]{1,0:T(8,128)(2,1)S(1)}, bf16[64,768]{1,0:T(8,128)(2,1)S(1)}, u32[]{:S(2)}, u32[]{:S(2)}) collective-permute-start(bf16[64,768]{1,0:T(8,128)(2,1)S(1)} %slice.8), channel_id=1, source_target_pairs={{0,16},{16,32},{32,48},{48,64},{64,80},{80,96},{96,112},{112,0},{1... | collective-permute-start | bytes 294920 | tf_op jit(solution)/shard_map/ppermute | solution.py:255
  29.8 8.2 %collective-permute-start.16 = (bf16[64,768]{1,0:T(8,128)(2,1)S(1)}, bf16[64,768]{1,0:T(8,128)(2,1)S(1)}, u32[]{:S(2)}, u32[]{:S(2)}) collective-permute-start(bf16[64,768]{1,0:T(8,128)(2,1)S(1)} %slice.9), channel_id=1, source_target_pairs={{0,112},{16,0},{32,16},{48,32},{64,48},{80,64},{96,80},{112,96},{1... | collective-permute-start | bytes 294920 | tf_op jit(solution)/shard_map/ppermute | solution.py:255
  38.0 1.4 %collective-permute-start.17 = (bf16[64,768]{1,0:T(8,128)(2,1)S(1)}, bf16[64,768]{1,0:T(8,128)(2,1)S(1)}, u32[]{:S(2)}, u32[]{:S(2)}) collective-permute-start(bf16[64,768]{1,0:T(8,128)(2,1)S(1)} %collective-permute-done.15.refs_0_), channel_id=1, source_target_pairs={{0,8},{8,0},{1,9},{9,1},{2,10},{10,2},{3,11},{11,3},{4,12},{12,4},... | collective-permute-start | bytes 294920 | tf_op jit(solution)/shard_map/ppermute | solution.py:28
  38.1 1.4 %collective-permute-start.18 = (bf16[64,768]{1,0:T(8,128)(2,1)S(1)}, bf16[64,768]{1,0:T(8,128)(2,1)S(1)}, u32[]{:S(2)}, u32[]{:S(2)}) collective-permute-start(bf16[64,768]{1,0:T(8,128)(2,1)S(1)} %collective-permute-done.16.refs_1_), channel_id=1, source_target_pairs={{0,8},{8,0},{1,9},{9,1},{2,10},{10,2},{3,11},{11,3},{4,12},{12,4},... | collective-permute-start | bytes 294920 | tf_op jit(solution)/shard_map/ppermute | solution.py:28
  40.5 1.3 %collective-permute-start.19 = (f32[16,128]{1,0:T(8,128)S(1)}, f32[16,128]{1,0:T(8,128)S(1)}, u32[]{:S(2)}, u32[]{:S(2)}) collective-permute-start(f32[16,128]{1,0:T(8,128)S(1)} %row_table.1), channel_id=1, source_target_pairs={{0,8},{8,0},{1,9},{9,1},{2,10},{10,2},{3,11},{11,3},{4,12},{12,4},... | collective-permute-start | bytes 24584 | tf_op jit(solution)/shard_map/ppermute | solution.py:28

commit v8 on v6

--- a/solution.py
+++ b/solution.py
@@ -89,7 +89,7 @@
         for part in parts:
             rows_ref[at : at + part.shape[0], :] = part[...]
             at += part.shape[0]
-    tile = 256
+    tile = min(256, at)
     for k in range(0, at, tile):
         peak, logits = None, []
         for i, logits_ref in enumerate(logits_refs):
@@ -286,14 +286,16 @@
     rows3, lse3, (near3, far3) = scores(order3, third, here, there)
     rows4, lse4, (near4, far4) = scores(pair(3, 1), side, here, there)
     up, down = lax.optimization_barrier((up, down, lse1, lse2, lse3, lse4))[:2]
-    last = [up, down, other_core(jnp.concatenate([up, down]))]
-    rows5, _, (near5, far5) = scores([(4, 0), (4, 1)], last, here, there)
+    beside = [other_core(up), other_core(down)]
+    rows5, _, (near5, far5) = scores([(4, 0)], [up, down], here, there)
+    rows6, _, (near6, far6) = scores([(4, 1)], beside, here, there)
     groups = [
         (order1, rows1, near1, far1),
         (order2, rows2, near2, far2),
         (order3, rows3, near3, far3),
         (pair(3, 1), rows4, near4, far4),
-        ([(4, 0), (4, 1)], rows5, near5, far5),
+        ([(4, 0)], rows5, near5, far5),
+        ([(4, 1)], rows6, near6, far6),
     ]
 
     (table,) = call(

time: 88.2 us -> 88.1 us (level)
  waiting for transfers between devices: 11.1 us -> 9.68 us
    ppermute x9 -> x10, waiting for transfers between devices: 2.9 us -> 1.52 us  [other_core(): return lax.ppermute(array, 'core', [(0, 1), (1, 0)])]
    ppermute x9 -> x10, starting transfers between devices: 1.43 us -> 2.15 us  [other_core(): return lax.ppermute(array, 'core', [(0, 1), (1, 0)])]
    pallas_call x12 -> x13, Pallas kernels: 13.1 us -> 13.6 us  [call(): pl.pallas_call(kernel, out_shape=outs, in_specs=[VMEM] * len(args), out_s...]
  transfers between devices with their start and end apart: 19 -> 20, of which waited for: 7 -> 8; matrix products, arithmetic and copies ran while one was open for 0% -> 0% of each run, Pallas kernels for 7% -> 8%
where the time goes in v8:
time: 88.1 us; the launch traced here: 87.8 us
  blocking collectives  39.6 us (45%)
  starting transfers between devices  20.8 us (24%)
  Pallas kernels  13.6 us (15%)
  waiting for transfers between devices  9.68 us (11%)
  local copies, waits for them, and re-layouts  2.79 us (3%)
    all_to_all x1, blocking collectives, local(): came = lax.all_to_all(packed.astype(jnp.float16), OWNERS, 0, 0, tiled=True)  28.3 us
    pallas_call x13, Pallas kernels, call(): pl.pallas_call(kernel, out_shape=outs, in_specs=[VMEM] * len(args), out_s...  13.6 us
    all_to_all x1, blocking collectives, local(): table = joined(*lax.all_to_all(tables, 'z', 0, 0, tiled=True))  11.4 us
    ppermute x3, starting transfers between devices, moved(): lax.ppermute(second, 'z', along_z(-1))  9.69 us
    ppermute x1, starting transfers between devices, local(): down = lax.ppermute(embeddings, 'z', along_z(-1))  5.93 us
    ppermute x1, waiting for transfers between devices, local(): up = lax.ppermute(embeddings, 'z', along_z(1))  3.17 us
    ppermute x3, waiting for transfers between devices, moved(): lax.ppermute(first, 'z', along_z(1))  2.89 us
    unnamed x6, local copies, waits for them, and re-layouts  2.77 us
  transfers between devices with their start and end apart: 20, of which 8 were waited for; matrix products, arithmetic and copies ran while one was open for 0% of the time, Pallas kernels for 8%

profile of v8, /device:TPU:8, one launch (start us, length us, event | category | flops | bytes accessed | tf_op | source)
XLA Modules:
  0.0 87.8 jit_solution(17592140896916717061)
XLA Ops:
  0.6 5.9 %collective-permute-start.2 = (bf16[128,768]{1,0:T(8,128)(2,1)}, bf16[128,768]{1,0:T(8,128)(2,1)S(1)}, u32[]{:S(2)}, u32[]{:S(2)}) collective-permute-start(bf16[128,768]{1,0:T(8,128)(2,1)} %rows_in.1), channel_id=1, source_target_pairs={{0,112},{16,0},{32,16},{48,32},{64,48},{80,64},{96,80},{112,96},{1... | collective-permute-start | bytes 589832 | tf_op jit(solution)/shard_map/ppermute | solution.py:226
  6.6 1.5 %collective-permute-start.11 = (bf16[512,768]{1,0:T(8,128)(2,1)}, bf16[512,768]{1,0:T(8,128)(2,1)S(1)}, u32[]{:S(2)}, u32[]{:S(2)}) collective-permute-start(bf16[512,768]{1,0:T(8,128)(2,1)} %cent_in.1), channel_id=1, source_target_pairs={{0,128},{128,0},{1,129},{129,1},{2,130},{130,2},{3,131},{131,3},{4... | collective-permute-start | bytes 2359304 | tf_op jit(solution)/shard_map/ppermute | solution.py:229
  8.1 1.2 %copy-done = bf16[512,768]{1,0:T(8,128)(2,1)S(1)} copy-done((bf16[512,768]{1,0:T(8,128)(2,1)S(1)}, bf16[512,768]{1,0:T(8,128)(2,1)}, u32[]{:S(2)}) %copy-start) | copy-done | bytes 786456
  9.2 0.9 %copy-done.1 = bf16[128,768]{1,0:T(8,128)(2,1)S(1)} copy-done((bf16[128,768]{1,0:T(8,128)(2,1)S(1)}, bf16[128,768]{1,0:T(8,128)(2,1)}, u32[]{:S(2)}) %copy-start.1) | copy-done | bytes 196632
  11.2 3.2 %collective-permute-done.1.refs_2_ = bf16[128,768]{1,0:T(8,128)(2,1)S(1)} collective-permute-done((bf16[128,768]{1,0:T(8,128)(2,1)}, bf16[128,768]{1,0:T(8,128)(2,1)S(1)}, u32[]{:S(2)}, u32[]{:S(2)}) %collective-permute-start.1) | collective-permute-done | bytes 196640 | tf_op jit(solution)/shard_map/ppermute | solution.py:225
  14.3 3.2 %collective-permute-start.6 = (bf16[128,768]{1,0:T(8,128)(2,1)S(1)}, bf16[128,768]{1,0:T(8,128)(2,1)S(1)}, u32[]{:S(2)}, u32[]{:S(2)}) collective-permute-start(bf16[128,768]{1,0:T(8,128)(2,1)S(1)} %collective-permute-done.2.refs_3_), channel_id=1, source_target_pairs={{0,112},{16,0},{32,16},{48,32},{64,48},{80,64},{96,80},{112,96},{1... | collective-permute-start | bytes 589832 | tf_op jit(solution)/shard_map/ppermute | solution.py:254
  17.6 0.8 score.8
  18.4 2.8 %collective-permute-done.5.refs_2_ = bf16[128,768]{1,0:T(8,128)(2,1)S(1)} collective-permute-done((bf16[128,768]{1,0:T(8,128)(2,1)S(1)}, bf16[128,768]{1,0:T(8,128)(2,1)S(1)}, u32[]{:S(2)}, u32[]{:S(2)}) %collective-permute-start.5) | collective-permute-done | bytes 196640 | tf_op jit(solution)/shard_map/ppermute | solution.py:254
  21.2 3.2 %collective-permute-start.10 = (bf16[128,768]{1,0:T(8,128)(2,1)S(1)}, bf16[128,768]{1,0:T(8,128)(2,1)S(1)}, u32[]{:S(2)}, u32[]{:S(2)}) collective-permute-start(bf16[128,768]{1,0:T(8,128)(2,1)S(1)} %collective-permute-done.6.refs_3_), channel_id=1, source_target_pairs={{0,112},{16,0},{32,16},{48,32},{64,48},{80,64},{96,80},{112,96},{1... | collective-permute-start | bytes 589832 | tf_op jit(solution)/shard_map/ppermute | solution.py:254
  24.5 1.5 %collective-permute-start.12 = (f32[1,512]{1,0:T(1,128)S(1)}, f32[1,512]{1,0:T(1,128)S(1)}, u32[]{:S(2)}, u32[]{:S(2)}) collective-permute-start(f32[1,512]{1,0:T(1,128)S(1)} %bitcast.36), channel_id=1, source_target_pairs={{0,128},{128,0},{1,129},{129,1},{2,130},{130,2},{3,131},{131,3},{4... | collective-permute-start | bytes 6152 | tf_op jit(solution)/shard_map/ppermute | solution.py:230
  26.0 2.1 %collective-permute-done.12.weight_ref = f32[1,512]{1,0:T(1,128)S(1)} collective-permute-done((f32[1,512]{1,0:T(1,128)S(1)}, f32[1,512]{1,0:T(1,128)S(1)}, u32[]{:S(2)}, u32[]{:S(2)}) %collective-permute-start.12) | collective-permute-done | bytes 2080 | tf_op jit(solution)/shard_map/ppermute | solution.py:230
  29.8 3.2 %collective-permute-start.16 = (bf16[64,768]{1,0:T(8,128)(2,1)S(1)}, bf16[64,768]{1,0:T(8,128)(2,1)S(1)}, u32[]{:S(2)}, u32[]{:S(2)}) collective-permute-start(bf16[64,768]{1,0:T(8,128)(2,1)S(1)} %slice.9), channel_id=1, source_target_pairs={{0,112},{16,0},{32,16},{48,32},{64,48},{80,64},{96,80},{112,96},{1... | collective-permute-start | bytes 294920 | tf_op jit(solution)/shard_map/ppermute | solution.py:254
  33.0 0.8 score.9
  34.1 0.8 score.12
  35.0 0.8 score.13
  35.8 0.8 score.11
  36.6 1.4 %score.10 = (f32[4,128]{1,0:T(4,128)S(1)}, f32[512,512]{1,0:T(8,128)S(1)}, f32[512,512]{1,0:T(8,128)S(1)}, bf16[512,768]{1,0:T(8,128)(2,1)S(1)}) custom-call(bf16[128,768]{1,0:T(8,128)(2,1)S(1)} %collective-permute-done.7.refs_0_, bf16[128,768]{1,0:T(8,128)(2,1)S(1)} %collective-permute-done.8.refs_1_, bf16[128,768]{1,0:T(8,128)(2,1)S(1)} %collective-permute-done.9.refs_2_, ...), custom_call_target="tpu_custom_call" | custom-call | flops 201326592 | bytes 1312256 | tf_op jit(solution)/shard_map/score/pallas_call | solution.py:33
  38.6 0.7 score.14
  39.5 0.7 score.15
  40.8 0.8 collective-permute-done.19
  41.7 11.4 %all_to_all.10 = f32[8,16,128]{2,1,0:T(8,128)S(1)} all-to-all(f32[8,16,128]{2,1,0:T(8,128)S(1)} %broadcast_in_dim.7), channel_id=1, replica_groups=mesh['x_lo'=2,'z'=8,'core'=2,'y'=4,'x_hi'=2] {'z'}, dimensions={0} | all-to-all | bytes 131072 | tf_op jit(solution)/shard_map/all_to_all | solution.py:306
  53.1 4.9 %spread.1 = (f32[16,392,128]{2,1,0:T(8,128)S(1)}, f32[1,128]{1,0:T(1,128)}) custom-call(f32[512,512]{1,0:T(8,128)S(1)} %get-tuple-element.51.refs_0_, f32[512,512]{1,0:T(8,128)S(1)} %get-tuple-element.55.refs_1_, f32[512,512]{1,0:T(8,128)S(1)} %get-tuple-element.58.refs_2_, f32[512,256]{1,0:T(8,128)S(1)} %get-tuple-element.59.refs_3_, ...), custom_call_target="tpu_custom_call" | custom-call | flops 3221225472 | bytes 14754304 | tf_op jit(solution)/shard_map/spread/pallas_call | solution.py:33
  58.2 28.3 %all_to_all.11 = f16[16,392,128]{2,1,0:T(8,128)(2,1)S(1)} all-to-all(f16[16,392,128]{2,1,0:T(8,128)(2,1)S(1)} %convert_element_type.6), channel_id=1, replica_groups=mesh['x_lo'=2,'z'=8,'core'=2,'y'=4,'x_hi'=2] {'x_lo','y','x_hi'}, dimensions={0} | all-to-all | bytes 3211264 | tf_op jit(solution)/shard_map/all_to_all | solution.py:325
  86.7 1.1 %update.1 = (f32[64,768]{1,0:T(8,128)}, f32[1,64]{1,0:T(1,128)}) custom-call(f32[16,392,128]{2,1,0:T(8,128)S(1)} %convert_element_type.7.came_ref, f32[64,768]{1,0:T(8,128)S(1)} %get-tuple-element.48.own_ref), custom_call_target="tpu_custom_call" | custom-call | bytes 3604736 | tf_op jit(solution)/shard_map/update/pallas_call | solution.py:33
  (44 shorter events, 5.0 us)
Async XLA Ops:
  0.6 10.5 %collective-permute-start.2 = (bf16[128,768]{1,0:T(8,128)(2,1)}, bf16[128,768]{1,0:T(8,128)(2,1)S(1)}, u32[]{:S(2)}, u32[]{:S(2)}) collective-permute-start(bf16[128,768]{1,0:T(8,128)(2,1)} %rows_in.1), channel_id=1, source_target_pairs={{0,112},{16,0},{32,16},{48,32},{64,48},{80,64},{96,80},{112,96},{1... | collective-permute-start | bytes 589832 | tf_op jit(solution)/shard_map/ppermute | solution.py:226
  6.6 7.8 %collective-permute-start.1 = (bf16[128,768]{1,0:T(8,128)(2,1)}, bf16[128,768]{1,0:T(8,128)(2,1)S(1)}, u32[]{:S(2)}, u32[]{:S(2)}) collective-permute-start(bf16[128,768]{1,0:T(8,128)(2,1)} %rows_in.1), channel_id=1, source_target_pairs={{0,16},{16,32},{32,48},{48,64},{64,80},{80,96},{96,112},{112,0},{1... | collective-permute-start | bytes 589832 | tf_op jit(solution)/shard_map/ppermute | solution.py:225
  6.6 23.1 %collective-permute-start.11 = (bf16[512,768]{1,0:T(8,128)(2,1)}, bf16[512,768]{1,0:T(8,128)(2,1)S(1)}, u32[]{:S(2)}, u32[]{:S(2)}) collective-permute-start(bf16[512,768]{1,0:T(8,128)(2,1)} %cent_in.1), channel_id=1, source_target_pairs={{0,128},{128,0},{1,129},{129,1},{2,130},{130,2},{3,131},{131,3},{4... | collective-permute-start | bytes 2359304 | tf_op jit(solution)/shard_map/ppermute | solution.py:229
  8.1 9.5 %collective-permute-start = (bf16[128,768]{1,0:T(8,128)(2,1)}, bf16[128,768]{1,0:T(8,128)(2,1)S(1)}, u32[]{:S(2)}, u32[]{:S(2)}) collective-permute-start(bf16[128,768]{1,0:T(8,128)(2,1)} %rows_in.1), channel_id=1, source_target_pairs={{0,8},{8,0},{1,9},{9,1},{2,10},{10,2},{3,11},{11,3},{4,12},{12,4},... | collective-permute-start | bytes 589832 | tf_op jit(solution)/shard_map/ppermute | solution.py:28
  8.1 1.2 %copy-start = (bf16[512,768]{1,0:T(8,128)(2,1)S(1)}, bf16[512,768]{1,0:T(8,128)(2,1)}, u32[]{:S(2)}) copy-start(bf16[512,768]{1,0:T(8,128)(2,1)} %cent_in.1) | copy-start | bytes 2359300
  9.2 0.9 %copy-start.1 = (bf16[128,768]{1,0:T(8,128)(2,1)S(1)}, bf16[128,768]{1,0:T(8,128)(2,1)}, u32[]{:S(2)}) copy-start(bf16[128,768]{1,0:T(8,128)(2,1)} %rows_in.1) | copy-start | bytes 589828
  10.2 0.7 copy-start.2
  14.3 6.9 %collective-permute-start.5 = (bf16[128,768]{1,0:T(8,128)(2,1)S(1)}, bf16[128,768]{1,0:T(8,128)(2,1)S(1)}, u32[]{:S(2)}, u32[]{:S(2)}) collective-permute-start(bf16[128,768]{1,0:T(8,128)(2,1)S(1)} %collective-permute-done.1.refs_2_), channel_id=1, source_target_pairs={{0,16},{16,32},{32,48},{48,64},{64,80},{80,96},{96,112},{112,0},{1... | collective-permute-start | bytes 589832 | tf_op jit(solution)/shard_map/ppermute | solution.py:254
  14.3 6.9 %collective-permute-start.6 = (bf16[128,768]{1,0:T(8,128)(2,1)S(1)}, bf16[128,768]{1,0:T(8,128)(2,1)S(1)}, u32[]{:S(2)}, u32[]{:S(2)}) collective-permute-start(bf16[128,768]{1,0:T(8,128)(2,1)S(1)} %collective-permute-done.2.refs_3_), channel_id=1, source_target_pairs={{0,112},{16,0},{32,16},{48,32},{64,48},{80,64},{96,80},{112,96},{1... | collective-permute-start | bytes 589832 | tf_op jit(solution)/shard_map/ppermute | solution.py:254
  21.2 6.9 %collective-permute-start.9 = (bf16[128,768]{1,0:T(8,128)(2,1)S(1)}, bf16[128,768]{1,0:T(8,128)(2,1)S(1)}, u32[]{:S(2)}, u32[]{:S(2)}) collective-permute-start(bf16[128,768]{1,0:T(8,128)(2,1)S(1)} %collective-permute-done.5.refs_2_), channel_id=1, source_target_pairs={{0,16},{16,32},{32,48},{48,64},{64,80},{80,96},{96,112},{112,0},{1... | collective-permute-start | bytes 589832 | tf_op jit(solution)/shard_map/ppermute | solution.py:254
  21.2 7.3 %collective-permute-start.10 = (bf16[128,768]{1,0:T(8,128)(2,1)S(1)}, bf16[128,768]{1,0:T(8,128)(2,1)S(1)}, u32[]{:S(2)}, u32[]{:S(2)}) collective-permute-start(bf16[128,768]{1,0:T(8,128)(2,1)S(1)} %collective-permute-done.6.refs_3_), channel_id=1, source_target_pairs={{0,112},{16,0},{32,16},{48,32},{64,48},{80,64},{96,80},{112,96},{1... | collective-permute-start | bytes 589832 | tf_op jit(solution)/shard_map/ppermute | solution.py:254
  24.5 3.6 %collective-permute-start.12 = (f32[1,512]{1,0:T(1,128)S(1)}, f32[1,512]{1,0:T(1,128)S(1)}, u32[]{:S(2)}, u32[]{:S(2)}) collective-permute-start(f32[1,512]{1,0:T(1,128)S(1)} %bitcast.36), channel_id=1, source_target_pairs={{0,128},{128,0},{1,129},{129,1},{2,130},{130,2},{3,131},{131,3},{4... | collective-permute-start | bytes 6152 | tf_op jit(solution)/shard_map/ppermute | solution.py:230
  26.0 2.7 %collective-permute-start.3 = (bf16[128,768]{1,0:T(8,128)(2,1)S(1)}, bf16[128,768]{1,0:T(8,128)(2,1)S(1)}, u32[]{:S(2)}, u32[]{:S(2)}) collective-permute-start(bf16[128,768]{1,0:T(8,128)(2,1)S(1)} %collective-permute-done.1.refs_2_), channel_id=1, source_target_pairs={{0,8},{8,0},{1,9},{9,1},{2,10},{10,2},{3,11},{11,3},{4,12},{12,4},... | collective-permute-start | bytes 589832 | tf_op jit(solution)/shard_map/ppermute | solution.py:28
  28.1 1.4 %collective-permute-start.4 = (bf16[128,768]{1,0:T(8,128)(2,1)S(1)}, bf16[128,768]{1,0:T(8,128)(2,1)S(1)}, u32[]{:S(2)}, u32[]{:S(2)}) collective-permute-start(bf16[128,768]{1,0:T(8,128)(2,1)S(1)} %collective-permute-done.2.refs_3_), channel_id=1, source_target_pairs={{0,8},{8,0},{1,9},{9,1},{2,10},{10,2},{3,11},{11,3},{4,12},{12,4},... | collective-permute-start | bytes 589832 | tf_op jit(solution)/shard_map/ppermute | solution.py:28
  28.1 1.7 %collective-permute-start.13 = (bf16[128,768]{1,0:T(8,128)(2,1)S(1)}, bf16[128,768]{1,0:T(8,128)(2,1)S(1)}, u32[]{:S(2)}, u32[]{:S(2)}) collective-permute-start(bf16[128,768]{1,0:T(8,128)(2,1)S(1)} %collective-permute-done.9.refs_2_), channel_id=1, source_target_pairs={{0,8},{8,0},{1,9},{9,1},{2,10},{10,2},{3,11},{11,3},{4,12},{12,4},... | collective-permute-start | bytes 589832 | tf_op jit(solution)/shard_map/ppermute | solution.py:28
  28.6 7.2 %collective-permute-start.14 = (bf16[128,768]{1,0:T(8,128)(2,1)S(1)}, bf16[128,768]{1,0:T(8,128)(2,1)S(1)}, u32[]{:S(2)}, u32[]{:S(2)}) collective-permute-start(bf16[128,768]{1,0:T(8,128)(2,1)S(1)} %collective-permute-done.10.refs_3_), channel_id=1, source_target_pairs={{0,8},{8,0},{1,9},{9,1},{2,10},{10,2},{3,11},{11,3},{4,12},{12,4},... | collective-permute-start | bytes 589832 | tf_op jit(solution)/shard_map/ppermute | solution.py:28
  28.7 7.9 %collective-permute-start.7 = (bf16[128,768]{1,0:T(8,128)(2,1)S(1)}, bf16[128,768]{1,0:T(8,128)(2,1)S(1)}, u32[]{:S(2)}, u32[]{:S(2)}) collective-permute-start(bf16[128,768]{1,0:T(8,128)(2,1)S(1)} %collective-permute-done.5.refs_2_), channel_id=1, source_target_pairs={{0,8},{8,0},{1,9},{9,1},{2,10},{10,2},{3,11},{11,3},{4,12},{12,4},... | collective-permute-start | bytes 589832 | tf_op jit(solution)/shard_map/ppermute | solution.py:28
  29.5 7.1 %collective-permute-start.8 = (bf16[128,768]{1,0:T(8,128)(2,1)S(1)}, bf16[128,768]{1,0:T(8,128)(2,1)S(1)}, u32[]{:S(2)}, u32[]{:S(2)}) collective-permute-start(bf16[128,768]{1,0:T(8,128)(2,1)S(1)} %collective-permute-done.6.refs_3_), channel_id=1, source_target_pairs={{0,8},{8,0},{1,9},{9,1},{2,10},{10,2},{3,11},{11,3},{4,12},{12,4},... | collective-permute-start | bytes 589832 | tf_op jit(solution)/shard_map/ppermute | solution.py:28
  29.7 8.3 %collective-permute-start.15 = (bf16[64,768]{1,0:T(8,128)(2,1)S(1)}, bf16[64,768]{1,0:T(8,128)(2,1)S(1)}, u32[]{:S(2)}, u32[]{:S(2)}) collective-permute-start(bf16[64,768]{1,0:T(8,128)(2,1)S(1)} %slice.8), channel_id=1, source_target_pairs={{0,16},{16,32},{32,48},{48,64},{64,80},{80,96},{96,112},{112,0},{1... | collective-permute-start | bytes 294920 | tf_op jit(solution)/shard_map/ppermute | solution.py:254
  29.8 8.2 %collective-permute-start.16 = (bf16[64,768]{1,0:T(8,128)(2,1)S(1)}, bf16[64,768]{1,0:T(8,128)(2,1)S(1)}, u32[]{:S(2)}, u32[]{:S(2)}) collective-permute-start(bf16[64,768]{1,0:T(8,128)(2,1)S(1)} %slice.9), channel_id=1, source_target_pairs={{0,112},{16,0},{32,16},{48,32},{64,48},{80,64},{96,80},{112,96},{1... | collective-permute-start | bytes 294920 | tf_op jit(solution)/shard_map/ppermute | solution.py:254
  38.0 1.4 %collective-permute-start.17 = (bf16[64,768]{1,0:T(8,128)(2,1)S(1)}, bf16[64,768]{1,0:T(8,128)(2,1)S(1)}, u32[]{:S(2)}, u32[]{:S(2)}) collective-permute-start(bf16[64,768]{1,0:T(8,128)(2,1)S(1)} %collective-permute-done.15.refs_0_), channel_id=1, source_target_pairs={{0,8},{8,0},{1,9},{9,1},{2,10},{10,2},{3,11},{11,3},{4,12},{12,4},... | collective-permute-start | bytes 294920 | tf_op jit(solution)/shard_map/ppermute | solution.py:28
  38.1 1.4 %collective-permute-start.18 = (bf16[64,768]{1,0:T(8,128)(2,1)S(1)}, bf16[64,768]{1,0:T(8,128)(2,1)S(1)}, u32[]{:S(2)}, u32[]{:S(2)}) collective-permute-start(bf16[64,768]{1,0:T(8,128)(2,1)S(1)} %collective-permute-done.16.refs_1_), channel_id=1, source_target_pairs={{0,8},{8,0},{1,9},{9,1},{2,10},{10,2},{3,11},{11,3},{4,12},{12,4},... | collective-permute-start | bytes 294920 | tf_op jit(solution)/shard_map/ppermute | solution.py:28
  40.4 1.3 %collective-permute-start.19 = (f32[16,128]{1,0:T(8,128)S(1)}, f32[16,128]{1,0:T(8,128)S(1)}, u32[]{:S(2)}, u32[]{:S(2)}) collective-permute-start(f32[16,128]{1,0:T(8,128)S(1)} %row_table.1), channel_id=1, source_target_pairs={{0,8},{8,0},{1,9},{9,1},{2,10},{10,2},{3,11},{11,3},{4,12},{12,4},... | collective-permute-start | bytes 24584 | tf_op jit(solution)/shard_map/ppermute | solution.py:28
